TPU v7x, 128 devices: a whole 4x4x4 slice. The times are simulated.
128 devices in a mesh: grp: 16 (over x, z), tp: 8 (over y, core).
Axes of the slice: x: 4, y: 4, z: 4, core: 2. Of those that a mesh axis runs over, the one named last changes fastest.
Arguments:
- thinker_rows: bfloat16 [4096, 8192], P(('grp', 'tp')), may hold values from -6 to 6
- norm_gain: bfloat16 [8192], replicated, may hold values from 0.5 to 1.5
- w_query: bfloat16 [8192, 4096], P(None, 'tp'), may hold values from -0.0625 to 0.0625
- w_key: bfloat16 [8192, 1024], P(None, 'tp'), may hold values from -0.0625 to 0.0625
- w_value: bfloat16 [8192, 1024], P(None, 'tp'), may hold values from -0.0625 to 0.0625
- w_out: bfloat16 [4096, 8192], P('tp'), may hold values from -0.75 to 0.75
- cache_keys: bfloat16 [256, 320, 1024], P('grp', None, 'tp'), may hold values from -576 to 576
- cache_values: bfloat16 [256, 320, 1024], P('grp', None, 'tp'), may hold values from -6 to 6
- session_ids: int32 [16, 256], P('grp'), may hold values from 0 to 15, never falling along the last dimension, each value on 1 to 20 neighbouring positions
- cache_lens: int32 [16, 16], P('grp'), may hold values from 1 to 320, 3200 in all within a row
- owners: int32 [256, 1], P('grp'), may hold values from 0 to 15; in each aligned block of 16 rows (0 to 15, 16 to 31, ...) at most 2 rows name the same one
- talker_gain: bfloat16 [8192], replicated, may hold values from 0.5 to 1.5
- w_talker: bfloat16 [8192, 1024], P(None, 'tp'), may hold values from -0.0625 to 0.0625
Outputs:
- talker_rows: bfloat16 [10240, 1024], P('grp', 'tp')
Inputs may be any that keep to these rules, and one draw needn't show every extreme that they name: `session_ids`: within a group the ids never fall; every one of the 16 sessions has 1 to 20 tokens and some session exactly 20. `cache_lens`: some session of every group has exactly 320 live slots. `owners`: of one group's 16 sessions at most 2 have the same owner, and some owner has exactly 2 of some group.
All inputs are finite; a program needn't handle non-finite values.
Results may differ from a plain program's by a relative error of at most 0.017.
The roundings to bfloat16 on the way count: a program that leaves them out, or rounds other values in their place, can miss the bound.
Values may be sent and summed in bfloat16 or wider, within the bound.
No kernel may reach another device: no remote copies, remote signals or barrier semaphores. Data moves between devices by JAX's collectives and lax.ppermute only.
A program may use at most 128 MiB of HBM per device.

v0:
```python
import jax
import jax.numpy as jnp
from jax import lax
from jax.sharding import PartitionSpec as P

HEAD_DIM = 128
SESS = 16
CAPS = 2
GQA = 4
MOST = 20


EPSILON = 1e-06


def rms_scaled(values, weights):
    floats = values.astype(jnp.float32)
    mean_square = jnp.mean(floats * floats, axis=-1, keepdims=True)
    return (floats * lax.rsqrt(mean_square + EPSILON) * weights.astype(jnp.float32)).astype(
        jnp.bfloat16
    )


def slot_tables(session_row, owner_row):
    session_range = jnp.arange(SESS, dtype=jnp.int32)
    member = (session_row[:, None] == session_range[None, :]).astype(jnp.int32)
    counts = jnp.sum(member, axis=0)
    starts = jnp.cumsum(counts) - counts
    first_row = jnp.sum(member * starts[None, :], axis=1)
    position = jnp.arange(session_row.shape[0], dtype=jnp.int32) - first_row
    earlier = (owner_row[:, None] == owner_row[None, :]) & (
        session_range[None, :] < session_range[:, None]
    )
    owner_rank = jnp.sum(earlier.astype(jnp.int32), axis=1)
    owner_slot = owner_row * CAPS + owner_rank
    destination = jnp.sum(member * owner_slot[None, :], axis=1) * MOST + position
    slot_index = session_row * MOST + position
    return (counts, slot_index, destination)


def attend(q_slots, k_slots, v_slots, cache_k, cache_v, live_lens, counts):
    score_scale = HEAD_DIM ** (-0.5)
    cached = (
        jnp.einsum("smkgd,sckd->skgmc", q_slots, cache_k, preferred_element_type=jnp.float32)
        * score_scale
    )
    fresh = (
        jnp.einsum("smkgd,snkd->skgmn", q_slots, k_slots, preferred_element_type=jnp.float32)
        * score_scale
    )
    live_cache = jnp.arange(cache_k.shape[1], dtype=jnp.int32)[None, :] < live_lens[:, None]
    places = jnp.arange(MOST, dtype=jnp.int32)
    causal = places[None, :] <= places[:, None]
    live_fresh = causal[None, :, :] & (places[None, None, :] < counts[:, None, None])
    cached = jnp.where(live_cache[:, None, None, None, :], cached, -1e30)
    fresh = jnp.where(live_fresh[:, None, None, :, :], fresh, -1e30)
    highest = jnp.maximum(jnp.max(cached, axis=-1), jnp.max(fresh, axis=-1))
    exp_cached = jnp.exp(cached - highest[..., None])
    exp_fresh = jnp.exp(fresh - highest[..., None])
    denominator = jnp.sum(exp_cached, axis=-1) + jnp.sum(exp_fresh, axis=-1)
    weight_cached = (exp_cached / denominator[..., None]).astype(jnp.bfloat16)
    weight_fresh = (exp_fresh / denominator[..., None]).astype(jnp.bfloat16)
    mixed = jnp.einsum(
        "skgmc,sckd->smkgd", weight_cached, cache_v, preferred_element_type=jnp.float32
    )
    mixed = mixed + jnp.einsum(
        "skgmn,snkd->smkgd", weight_fresh, v_slots, preferred_element_type=jnp.float32
    )
    return mixed.astype(jnp.bfloat16)


def on_device(
    thinker_rows,
    norm_gain,
    w_query,
    w_key,
    w_value,
    w_out,
    cache_keys,
    cache_values,
    session_ids,
    cache_lens,
    owners,
    talker_gain,
    w_talker,
):
    model_width = thinker_rows.shape[1]
    kv_local = w_key.shape[1] // HEAD_DIM
    head_width = GQA * HEAD_DIM
    slot_count = SESS * MOST
    owner_count = lax.axis_size("grp")
    gathered = lax.all_gather(thinker_rows, "tp", axis=0, tiled=True)
    normed = rms_scaled(gathered, norm_gain)
    query = jnp.dot(normed, w_query, preferred_element_type=jnp.float32).astype(jnp.bfloat16)
    key_new = jnp.dot(normed, w_key, preferred_element_type=jnp.float32).astype(jnp.bfloat16)
    value_new = jnp.dot(normed, w_value, preferred_element_type=jnp.float32).astype(jnp.bfloat16)
    counts, slot_index, destination = slot_tables(session_ids[0], owners[:, 0])
    placing = (slot_index[None, :] == jnp.arange(slot_count, dtype=jnp.int32)[:, None]).astype(
        jnp.bfloat16
    )
    q_slots = jnp.dot(placing, query, preferred_element_type=jnp.float32).astype(jnp.bfloat16)
    k_slots = jnp.dot(placing, key_new, preferred_element_type=jnp.float32).astype(jnp.bfloat16)
    v_slots = jnp.dot(placing, value_new, preferred_element_type=jnp.float32).astype(jnp.bfloat16)
    mixed = attend(
        q_slots.reshape(SESS, MOST, kv_local, GQA, HEAD_DIM),
        k_slots.reshape(SESS, MOST, kv_local, HEAD_DIM),
        v_slots.reshape(SESS, MOST, kv_local, HEAD_DIM),
        cache_keys.reshape(SESS, cache_keys.shape[1], kv_local, HEAD_DIM),
        cache_values.reshape(SESS, cache_values.shape[1], kv_local, HEAD_DIM),
        cache_lens[0],
        counts,
    )
    attention_rows = lax.dot_general(
        placing,
        mixed.reshape(slot_count, kv_local * head_width),
        (((0,), (0,)), ((), ())),
        preferred_element_type=jnp.float32,
    ).astype(jnp.bfloat16)
    routing = (
        destination[None, :] == jnp.arange(owner_count * CAPS * MOST, dtype=jnp.int32)[:, None]
    ).astype(jnp.bfloat16)
    partial_sum = jnp.dot(attention_rows, w_out, preferred_element_type=jnp.float32).astype(
        jnp.bfloat16
    )
    head_total = partial_sum.astype(jnp.float32)
    summed = lax.psum_scatter(
        head_total.astype(jnp.bfloat16), "tp", scatter_dimension=0, tiled=True
    ).astype(jnp.float32)
    hidden_local = (thinker_rows.astype(jnp.float32) + summed).astype(jnp.bfloat16)
    hidden = lax.all_gather(hidden_local, "tp", axis=0, tiled=True)
    outgoing = (
        jnp.dot(routing, hidden, preferred_element_type=jnp.float32)
        .astype(jnp.bfloat16)
        .reshape(owner_count, CAPS * MOST, model_width)
    )
    arrived = lax.all_to_all(outgoing, "grp", split_axis=0, concat_axis=0, tiled=True)
    arrived_rows = arrived.reshape(owner_count * CAPS * MOST, model_width)
    return jnp.dot(
        rms_scaled(arrived_rows, talker_gain), w_talker, preferred_element_type=jnp.float32
    ).astype(jnp.bfloat16)


def solution(mesh):
    return jax.shard_map(
        on_device,
        mesh=mesh,
        in_specs=(
            P(("grp", "tp"), None),
            P(),
            P(None, "tp"),
            P(None, "tp"),
            P(None, "tp"),
            P("tp", None),
            P("grp", None, "tp"),
            P("grp", None, "tp"),
            P("grp", None),
            P("grp", None),
            P("grp", None),
            P(),
            P(None, "tp"),
        ),
        out_specs=P("grp", "tp"),
        check_vma=False,
    )
```

profile of v0, /device:TPU:0, one launch (start us, length us, event | category | flops | bytes accessed | tf_op | source)
XLA Modules:
  0.0 370.0 jit_solution(12087315956957895929)
XLA Ops:
  6.5 0.0 copy-start
  6.5 0.0 all-gather.3.cloned.1.call-start
  6.5 0.7 all-gather.3.cloned.1.call-update
  7.3 0.0 reduce-scatter.2.cloned.1.call-start
  7.3 0.8 convert_reduce_fusion
  8.1 0.1 copy.23
  8.2 0.1 reduce.5
  8.4 0.7 convert_element_type.92
  9.1 0.9 convert_reduce_fusion.1
  10.0 0.7 multiply_add_fusion
  10.7 0.8 select_reduce_fusion.1
  11.4 0.1 iota_compare_fusion.11
  11.5 0.7 subtract_add_fusion
  12.2 0.7 iota_compare_fusion.8
  12.9 0.1 broadcast_and_fusion
  13.0 30.6 %all-gather.3.cloned.1.call-done = bf16[256,8192]{1,0:T(8,128)(2,1)} async-done(((bf16[32,8192]{1,0:T(8,128)(2,1)}), bf16[256,8192]{1,0:T(8,128)(2,1)}) %all-gather.3.cloned.1.call-update) | async-done | bytes 4194320 | tf_op jit(solution)/shard_map/all_gather | solution.py:92
  43.6 3.1 fusion.2
  46.7 7.3 %convolution_convert_fusion.2 = bf16[320,512]{1,0:T(8,128)(2,1)S(1)} fusion(bf16[8192,512]{1,0:T(8,128)(2,1)} %param.15, s32[256]{0:T(256)S(1)} %bitcast.109, bf16[256,8192]{1,0:T(8,128)(2,1)} %all-gather.3.cloned.1.call-done, f32[8192]{0:T(1024)S(1)} %convert_element_type.92, f32[256]{0:T(256)S(1)} %add_rsqrt_fusion.1), kind=kOutput, calls=%fused_computation.26 | convolution fusion | flops 2240135168 | bytes 12945408 | tf_op jit(solution)/shard_map/dot_general | solution.py:101
  54.0 0.1 reshape.227
  54.1 4.5 %convolution_convert_fusion.7 = bf16[320,128]{1,0:T(8,128)(2,1)S(1)} fusion(bf16[8192,128]{1,0:T(8,128)(2,1)} %param.16, s32[256]{0:T(256)S(1)} %bitcast.110, bf16[256,8192]{1,0:T(8,128)(2,1)} %all-gather.3.cloned.1.call-done, f32[8192]{0:T(1024)S(1)} %convert_element_type.92, f32[256]{0:T(256)S(1)} %add_rsqrt_fusion.1), kind=kOutput, calls=%fused_computation.38 | convolution fusion | flops 566386688 | bytes 6408192 | tf_op jit(solution)/shard_map/dot_general | solution.py:102
  58.6 0.8 fusion.58
  59.5 2.3 fusion.7
  61.8 0.0 copy-start.1
  61.8 0.2 fusion.31
  62.0 1.2 copy-done.1
  63.2 0.9 fusion.6
  64.1 4.5 %convolution_convert_fusion.6 = bf16[320,128]{1,0:T(8,128)(2,1)S(1)} fusion(bf16[8192,128]{1,0:T(8,128)(2,1)} %param.17, s32[256]{0:T(256)S(1)} %bitcast.111, bf16[256,8192]{1,0:T(8,128)(2,1)} %all-gather.3.cloned.1.call-done, f32[8192]{0:T(1024)S(1)} %convert_element_type.92, f32[256]{0:T(256)S(1)} %add_rsqrt_fusion.1), kind=kOutput, calls=%fused_computation.37 | convolution fusion | flops 566386688 | bytes 6408192 | tf_op jit(solution)/shard_map/dot_general | solution.py:103
  68.7 0.3 fusion.32
  69.0 2.9 fusion.23
  72.0 0.1 copy.27
  72.1 8.1 %convolution_convert_fusion.1 = bf16[256,8192]{1,0:T(8,128)(2,1)} fusion(bf16[512,8192]{1,0:T(8,128)(2,1)} %param.18, bf16[40,8,4,128]{3,2,1,0:T(4,128)(2,1)S(1)} %bitcast.107, s32[256]{0:T(256)S(1)} %bitcast.112), kind=kOutput, calls=%fused_computation.7 | convolution fusion | flops 2233679872 | bytes 12911616 | tf_op jit(solution)/shard_map/dot_general | solution.py:122
  80.2 0.0 copy-start.2
  80.2 0.0 reduce-scatter.2.cloned.1.call-update
  80.3 0.0 all-gather.5.cloned.1.call-start
  80.3 38.0 %reduce-scatter.2.cloned.1.call-done = bf16[32,8192]{1,0:T(8,128)(2,1)} async-done(((bf16[256,8192]{1,0:T(8,128)(2,1)}), bf16[32,8192]{1,0:T(8,128)(2,1)}) %reduce-scatter.2.cloned.1.call-update) | async-done | bytes 524304 | tf_op jit(solution)/shard_map/reduce_scatter | solution.py:126
  118.3 0.0 copy-done.2
  118.3 2.0 add_convert_fusion
  120.3 0.0 all-gather.5.cloned.1.call-update
  120.3 31.1 %all-gather.5.cloned.1.call-done = bf16[256,8192]{1,0:T(8,128)(2,1)} async-done(((bf16[32,8192]{1,0:T(8,128)(2,1)}), bf16[256,8192]{1,0:T(8,128)(2,1)}) %all-gather.5.cloned.1.call-update) | async-done | bytes 4194320 | tf_op jit(solution)/shard_map/all_gather | solution.py:130
  151.4 7.7 %convolution_convert_fusion = bf16[640,8192]{1,0:T(8,128)(2,1)} fusion(bf16[256,8192]{1,0:T(8,128)(2,1)} %all-gather.5.cloned.1.call-done, s32[256]{0:T(256)S(1)} %subtract_add_fusion.1), kind=kOutput, calls=%fused_computation.4 | convolution fusion | flops 2689761280 | bytes 14681088 | tf_op jit(solution)/shard_map/dot_general | solution.py:132
  159.1 7.1 %all-to-all-start = ((bf16[16,40,8192]{2,1,0:T(8,128)(2,1)}), bf16[16,40,8192]{2,1,0:T(8,128)(2,1)}, u32[]{:S(2)}, u32[]{:S(2)}) async-start(bf16[16,40,8192]{2,1,0:T(8,128)(2,1)} %bitcast.106), calls=%async_computation.1 | async-start | bytes 20971520 | tf_op jit(solution)/shard_map/all_to_all | solution.py:136
  166.3 0.0 copy-done.3
  166.3 180.9 %all-to-all-done = bf16[16,40,8192]{2,1,0:T(8,128)(2,1)} async-done(((bf16[16,40,8192]{2,1,0:T(8,128)(2,1)}), bf16[16,40,8192]{2,1,0:T(8,128)(2,1)}, u32[]{:S(2)}, u32[]{:S(2)}) %all-to-all-start) | async-done | bytes 10485792 | tf_op jit(solution)/shard_map/all_to_all | solution.py:136
  347.2 6.1 %multiply_reduce_fusion = f32[16,40]{1,0:T(8,128)S(1)} fusion(bf16[16,40,8192]{2,1,0:T(8,128)(2,1)} %all-to-all-done), kind=kLoop, calls=%fused_computation.3 | loop fusion | flops 15728000 | bytes 10488320 | tf_op jit(solution)/shard_map/reduce_sum | solution.py:18
  353.3 0.1 rsqrt.21
  353.4 6.5 %fusion.1 = bf16[640,8192]{1,0:T(8,128)(2,1)S(1)} fusion(f32[8192]{0:T(1024)S(1)} %convert_element_type.113, f32[640]{0:T(1024)S(1)} %rsqrt.21, bf16[16,40,8192]{2,1,0:T(8,128)(2,1)} %all-to-all-done), kind=kLoop, calls=%fused_computation.2 | loop fusion | flops 20971520 | bytes 21006848 | tf_op jit(solution)/shard_map/convert_element_type | solution.py:19
  359.9 0.0 copy-done
  359.9 3.5 convolution_convert_fusion.5
  (12 shorter events, 0.1 us)
Async XLA Ops:
  6.5 353.4 %copy-start = (bf16[8192,128]{1,0:T(8,128)(2,1)S(1)}, bf16[8192,128]{1,0:T(8,128)(2,1)}, u32[]{:S(2)}) copy-start(bf16[8192,128]{1,0:T(8,128)(2,1)} %param.25) | copy-start | bytes 6291460
  6.5 37.1 %all-gather.3.cloned.1.call-start = ((), (), s32[]{:S(2)}) async-start(), calls=%async_computation.2 | async-start | bytes 4718592 | tf_op jit(solution)/shard_map/all_gather | solution.py:92
  7.3 111.1 %reduce-scatter.2.cloned.1.call-start = ((), (), s32[]{:S(2)}) async-start(), calls=%async_computation.3 | async-start | bytes 4718592 | tf_op jit(solution)/shard_map/reduce_scatter | solution.py:126
  61.8 1.4 copy-start.1
  80.2 38.1 %copy-start.2 = (bf16[32,8192]{1,0:T(8,128)(2,1)S(1)}, bf16[32,8192]{1,0:T(8,128)(2,1)}, u32[]{:S(2)}) copy-start(bf16[32,8192]{1,0:T(8,128)(2,1)} %param.13) | copy-start | bytes 1572868
  80.3 71.2 %all-gather.5.cloned.1.call-start = ((), (), s32[]{:S(2)}) async-start(), calls=%async_computation.4 | async-start | bytes 4718592 | tf_op jit(solution)/shard_map/all_gather | solution.py:130
  159.1 7.1 %copy-start.3 = (bf16[8192]{0:T(1024)(128)(2,1)S(1)}, bf16[8192]{0:T(1024)(128)(2,1)}, u32[]{:S(2)}) copy-start(bf16[8192]{0:T(1024)(128)(2,1)} %param.24) | copy-start | bytes 49156
  159.1 188.0 %all-to-all-start = ((bf16[16,40,8192]{2,1,0:T(8,128)(2,1)}), bf16[16,40,8192]{2,1,0:T(8,128)(2,1)}, u32[]{:S(2)}, u32[]{:S(2)}) async-start(bf16[16,40,8192]{2,1,0:T(8,128)(2,1)} %bitcast.106), calls=%async_computation.1 | async-start | bytes 20971520 | tf_op jit(solution)/shard_map/all_to_all | solution.py:136
Sparse Core Ops, SparseCore 0:
  9.0 34.5 all-gather.2
  80.4 37.9 reduce-scatter.1
  120.4 30.9 all-gather.4
where the time goes:
time: 375 us; the launch traced here: 370 us
  waiting for transfers between devices  281 us (75%)
  matrix products  42 us (11%)
  other arithmetic  24.6 us (7%)
  between operations  13.3 us (4%)
  starting transfers between devices  7.21 us (2%)
    all_to_all x1, waiting for transfers between devices, on_device(): lax.all_to_all(outgoing, 'grp', split_axis=0, concat_axis=0, tiled=True)  181 us
    reduce_scatter x1, waiting for transfers between devices, on_device(): lax.psum_scatter(head_total.astype(jnp.bfloat16), 'tp', scatter_dimension...  38 us
    all_gather x1, waiting for transfers between devices, on_device(): hidden = lax.all_gather(hidden_local, 'tp', axis=0, tiled=True)  31.1 us
    all_gather x1, waiting for transfers between devices, on_device(): gathered = lax.all_gather(thinker_rows, 'tp', axis=0, tiled=True)  30.6 us
    reduce_sum x2, other arithmetic, rms_scaled(): mean_square = jnp.mean(floats * floats, axis=-1, keepdims=True)  9.2 us
    dot_general x1, matrix products, on_device(): jnp.dot(attention_rows, w_out, preferred_element_type=jnp.float32)  8.11 us
    dot_general x1, matrix products, on_device(): jnp.dot(routing, hidden, preferred_element_type=jnp.float32)  7.7 us
  transfers between devices with their start and end apart: 4, of which 4 were waited for; matrix products, arithmetic and copies ran while one was open for 2% of the time, Pallas kernels for 0%

commit v1 on v0

--- a/solution.py
+++ b/solution.py
@@ -84,7 +84,6 @@
     talker_gain,
     w_talker,
 ):
-    model_width = thinker_rows.shape[1]
     kv_local = w_key.shape[1] // HEAD_DIM
     head_width = GQA * HEAD_DIM
     slot_count = SESS * MOST
@@ -128,16 +127,16 @@
     ).astype(jnp.float32)
     hidden_local = (thinker_rows.astype(jnp.float32) + summed).astype(jnp.bfloat16)
     hidden = lax.all_gather(hidden_local, "tp", axis=0, tiled=True)
+    talker_here = jnp.dot(
+        rms_scaled(hidden, talker_gain), w_talker, preferred_element_type=jnp.float32
+    ).astype(jnp.bfloat16)
     outgoing = (
-        jnp.dot(routing, hidden, preferred_element_type=jnp.float32)
+        jnp.dot(routing, talker_here, preferred_element_type=jnp.float32)
         .astype(jnp.bfloat16)
-        .reshape(owner_count, CAPS * MOST, model_width)
+        .reshape(owner_count, CAPS * MOST, w_talker.shape[1])
     )
     arrived = lax.all_to_all(outgoing, "grp", split_axis=0, concat_axis=0, tiled=True)
-    arrived_rows = arrived.reshape(owner_count * CAPS * MOST, model_width)
-    return jnp.dot(
-        rms_scaled(arrived_rows, talker_gain), w_talker, preferred_element_type=jnp.float32
-    ).astype(jnp.bfloat16)
+    return arrived.reshape(owner_count * CAPS * MOST, w_talker.shape[1])
 
 
 def solution(mesh):

time: 375 us -> 178 us (0.47); the launches traced: 370 us -> 177 us
  waiting for transfers between devices: 281 us -> 100 us
  blocking collectives: 0 us -> 14.8 us
  other arithmetic: 24.6 us -> 15.1 us
  matrix products: 42 us -> 32.8 us
  starting transfers between devices: 7.21 us -> 0.08 us
    all_to_all x1 -> x0, waiting for transfers between devices: 181 us -> none  [on_device(): lax.all_to_all(outgoing, 'grp', split_axis=0, concat_axis=0, tiled=True)]
    all_to_all x0 -> x1, blocking collectives: none -> 14.8 us  [on_device(): lax.all_to_all(outgoing, 'grp', split_axis=0, concat_axis=0, tiled=True)]
    dot_general x2 -> x1, matrix products: 11.2 us -> 3.82 us  [on_device(): jnp.dot(routing, talker_here, preferred_element_type=jnp.float32)]
    all_to_all x1 -> x0, starting transfers between devices: 7.13 us -> none  [on_device(): lax.all_to_all(outgoing, 'grp', split_axis=0, concat_axis=0, tiled=True)]
    convert_element_type x1 -> x0, other arithmetic: 6.54 us -> none  [rms_scaled(): (floats * lax.rsqrt(mean_square + EPSILON) * weights.astype(jnp.float32))...]
  transfers between devices with their start and end apart: 4 -> 3, of which waited for: 4 -> 3; matrix products, arithmetic and copies ran while one was open for 2% -> 3% of each run, Pallas kernels for 0% -> 0%
where the time goes in v1:
time: 178 us; the launch traced here: 177 us
  waiting for transfers between devices  100 us (56%)
  matrix products  32.8 us (18%)
  other arithmetic  15.1 us (8%)
  blocking collectives  14.8 us (8%)
  between operations  13.3 us (7%)
    reduce_scatter x1, waiting for transfers between devices, on_device(): lax.psum_scatter(head_total.astype(jnp.bfloat16), 'tp', scatter_dimension...  37.9 us
    all_gather x1, waiting for transfers between devices, on_device(): hidden = lax.all_gather(hidden_local, 'tp', axis=0, tiled=True)  31.1 us
    all_gather x1, waiting for transfers between devices, on_device(): gathered = lax.all_gather(thinker_rows, 'tp', axis=0, tiled=True)  30.6 us
    all_to_all x1, blocking collectives, on_device(): lax.all_to_all(outgoing, 'grp', split_axis=0, concat_axis=0, tiled=True)  14.8 us
    dot_general x1, matrix products, on_device(): jnp.dot(attention_rows, w_out, preferred_element_type=jnp.float32)  7.93 us
    dot_general x1, matrix products, on_device(): jnp.dot(placing, query, preferred_element_type=jnp.float32)  7.26 us
    reduce_sum x2, other arithmetic, rms_scaled(): mean_square = jnp.mean(floats * floats, axis=-1, keepdims=True)  6.21 us
    dot_general x1, matrix products, on_device(): jnp.dot(placing, key_new, preferred_element_type=jnp.float32)  4.51 us
  transfers between devices with their start and end apart: 3, of which 3 were waited for; matrix products, arithmetic and copies ran while one was open for 3% of the time, Pallas kernels for 0%

profile of v1, /device:TPU:0, one launch (start us, length us, event | category | flops | bytes accessed | tf_op | source)
XLA Modules:
  0.0 177.3 jit_solution(13249592101484979585)
XLA Ops:
  6.5 0.0 copy-start
  6.5 0.0 all-gather.3.cloned.1.call-start
  6.5 0.7 all-gather.3.cloned.1.call-update
  7.3 0.0 reduce-scatter.2.cloned.1.call-start
  7.3 0.8 convert_reduce_fusion
  8.1 0.1 copy.23
  8.2 0.1 reduce.4
  8.4 0.7 convert_element_type.86
  9.1 0.9 convert_reduce_fusion.1
  10.0 0.7 multiply_add_fusion
  10.7 0.8 select_reduce_fusion.1
  11.4 0.1 iota_compare_fusion.11
  11.5 0.7 subtract_add_fusion
  12.2 0.7 iota_compare_fusion.8
  12.9 0.1 broadcast_and_fusion
  13.0 30.6 %all-gather.3.cloned.1.call-done = bf16[256,8192]{1,0:T(8,128)(2,1)} async-done(((bf16[32,8192]{1,0:T(8,128)(2,1)}), bf16[256,8192]{1,0:T(8,128)(2,1)}) %all-gather.3.cloned.1.call-update) | async-done | bytes 4194320 | tf_op jit(solution)/shard_map/all_gather | solution.py:91
  43.6 3.1 %fusion = f32[256]{0:T(256)S(1)} fusion(bf16[256,8192]{1,0:T(8,128)(2,1)} %all-gather.3.cloned.1.call-done), kind=kLoop, calls=%fused_computation.5 | loop fusion | flops 6291200 | bytes 4195328 | tf_op jit(solution)/shard_map/reduce_sum | solution.py:18
  46.7 4.5 %convolution_convert_fusion.6 = bf16[320,128]{1,0:T(8,128)(2,1)S(1)} fusion(bf16[8192,128]{1,0:T(8,128)(2,1)} %param.16, s32[256]{0:T(256)S(1)} %bitcast.103, bf16[256,8192]{1,0:T(8,128)(2,1)} %all-gather.3.cloned.1.call-done, f32[8192]{0:T(1024)S(1)} %convert_element_type.86, f32[256]{0:T(256)S(1)} %add_rsqrt_fusion.1), kind=kOutput, calls=%fused_computation.41 | convolution fusion | flops 566386688 | bytes 6408192 | tf_op jit(solution)/shard_map/dot_general | solution.py:101
  51.3 7.3 %convolution_convert_fusion.1 = bf16[320,512]{1,0:T(8,128)(2,1)S(1)} fusion(bf16[8192,512]{1,0:T(8,128)(2,1)} %param.15, s32[256]{0:T(256)S(1)} %bitcast.104, bf16[256,8192]{1,0:T(8,128)(2,1)} %all-gather.3.cloned.1.call-done, f32[8192]{0:T(1024)S(1)} %convert_element_type.86, f32[256]{0:T(256)S(1)} %add_rsqrt_fusion.1), kind=kOutput, calls=%fused_computation.29 | convolution fusion | flops 2240135168 | bytes 12945408 | tf_op jit(solution)/shard_map/dot_general | solution.py:100
  58.6 0.1 reshape.218
  58.6 4.5 %convolution_convert_fusion.5 = bf16[320,128]{1,0:T(8,128)(2,1)S(1)} fusion(bf16[8192,128]{1,0:T(8,128)(2,1)} %param.17, s32[256]{0:T(256)S(1)} %bitcast.105, bf16[256,8192]{1,0:T(8,128)(2,1)} %all-gather.3.cloned.1.call-done, f32[8192]{0:T(1024)S(1)} %convert_element_type.86, f32[256]{0:T(256)S(1)} %add_rsqrt_fusion.1), kind=kOutput, calls=%fused_computation.40 | convolution fusion | flops 566386688 | bytes 6408192 | tf_op jit(solution)/shard_map/dot_general | solution.py:102
  63.2 0.8 fusion.68
  64.0 2.3 %fusion.12 = (f32[16,4,20]{2,1,0:T(4,128)S(1)}, f32[16,20,4,320]{3,1,2,0:T(8,128)S(1)}) fusion(pred[16,320]{1,0:T(8,128)(4,1)S(1)} %iota_compare_fusion.8, bf16[16,320,128]{2,1,0:T(8,128)(2,1)} %param.19, bf16[16,20,4,128]{3,2,1,0:T(4,128)(2,1)S(1)} %reshape.218), kind=kOutput, calls=%fused_computation.19 | convolution fusion | flops 106085120 | bytes 3287040 | tf_op jit(solution)/shard_map/smkgd,sckd->skgmc/dot_general | solution.py:44
  66.3 0.0 copy-start.3
  66.3 0.3 fusion.41
  66.6 0.9 fusion.11
  67.6 0.3 fusion.42
  67.9 0.0 copy-done.3
  67.9 1.3 fusion.28
  69.2 0.1 copy.27
  69.4 7.9 %convolution_convert_fusion = bf16[256,8192]{1,0:T(8,128)(2,1)} fusion(bf16[512,8192]{1,0:T(8,128)(2,1)} %param.18, bf16[40,8,4,128]{3,2,1,0:T(4,128)(2,1)S(1)} %bitcast.99, s32[256]{0:T(256)S(1)} %bitcast.106), kind=kOutput, calls=%fused_computation.4 | convolution fusion | flops 2233679872 | bytes 12911616 | tf_op jit(solution)/shard_map/dot_general | solution.py:121
  77.3 0.0 copy-start.1
  77.3 0.0 copy-start.2
  77.3 0.0 reduce-scatter.2.cloned.1.call-update
  77.3 0.0 all-gather.5.cloned.1.call-start
  77.4 37.9 %reduce-scatter.2.cloned.1.call-done = bf16[32,8192]{1,0:T(8,128)(2,1)} async-done(((bf16[256,8192]{1,0:T(8,128)(2,1)}), bf16[32,8192]{1,0:T(8,128)(2,1)}) %reduce-scatter.2.cloned.1.call-update) | async-done | bytes 524304 | tf_op jit(solution)/shard_map/reduce_scatter | solution.py:125
  115.3 0.0 copy-done.1
  115.3 2.0 %add_convert_fusion = bf16[32,8192]{1,0:T(8,128)(2,1)} fusion(bf16[32,8192]{1,0:T(8,128)(2,1)} %reduce-scatter.2.cloned.1.call-done, bf16[32,8192]{1,0:T(8,128)(2,1)S(1)} %copy-done.1), kind=kLoop, calls=%fused_computation.45 | loop fusion | flops 1048576 | bytes 1572864 | tf_op jit(solution)/shard_map/convert_element_type | solution.py:128
  117.3 0.0 all-gather.5.cloned.1.call-update
  117.3 0.0 copy-done.2
  117.3 31.1 %all-gather.5.cloned.1.call-done = bf16[256,8192]{1,0:T(8,128)(2,1)} async-done(((bf16[32,8192]{1,0:T(8,128)(2,1)}), bf16[256,8192]{1,0:T(8,128)(2,1)}) %all-gather.5.cloned.1.call-update) | async-done | bytes 4194320 | tf_op jit(solution)/shard_map/all_gather | solution.py:129
  148.4 3.1 %fusion.3 = f32[256]{0:T(256)S(1)} fusion(bf16[256,8192]{1,0:T(8,128)(2,1)} %all-gather.5.cloned.1.call-done), kind=kLoop, calls=%fused_computation.8 | loop fusion | flops 6291200 | bytes 4195328 | tf_op jit(solution)/shard_map/reduce_sum | solution.py:18
  151.5 0.0 copy-done
  151.5 3.8 %convolution_convert_fusion.4 = bf16[640,128]{1,0:T(8,128)(2,1)S(1)} fusion(bf16[8192,128]{1,0:T(8,128)(2,1)S(1)} %copy-done, bf16[256,8192]{1,0:T(8,128)(2,1)} %all-gather.5.cloned.1.call-done, f32[8192]{0:T(1024)S(1)} %convert_element_type.104, f32[256]{0:T(256)S(1)} %add_rsqrt_fusion, s32[256]{0:T(256)S(1)} %subtract_add_fusion.1), kind=kOutput, calls=%fused_computation.39 | convolution fusion | flops 587481088 | bytes 6490112 | tf_op jit(solution)/shard_map/dot_general | solution.py:134
  155.4 14.8 %all_to_all.5 = bf16[16,40,128]{2,1,0:T(8,128)(2,1)S(1)} all-to-all(bf16[16,40,128]{2,1,0:T(8,128)(2,1)S(1)} %bitcast.101), channel_id=1, replica_groups=mesh['grp'=16,'tp'=8] {'grp'}, dimensions={0} | all-to-all | bytes 327680 | tf_op jit(solution)/shard_map/all_to_all | solution.py:138
  170.1 0.7 copy.48
  (11 shorter events, 0.1 us)
Async XLA Ops:
  6.5 145.0 %copy-start = (bf16[8192,128]{1,0:T(8,128)(2,1)S(1)}, bf16[8192,128]{1,0:T(8,128)(2,1)}, u32[]{:S(2)}) copy-start(bf16[8192,128]{1,0:T(8,128)(2,1)} %param.25) | copy-start | bytes 6291460
  6.5 37.1 %all-gather.3.cloned.1.call-start = ((), (), s32[]{:S(2)}) async-start(), calls=%async_computation.2 | async-start | bytes 4718592 | tf_op jit(solution)/shard_map/all_gather | solution.py:91
  7.3 108.0 %reduce-scatter.2.cloned.1.call-start = ((), (), s32[]{:S(2)}) async-start(), calls=%async_computation.3 | async-start | bytes 4718592 | tf_op jit(solution)/shard_map/reduce_scatter | solution.py:125
  66.3 1.6 copy-start.3
  77.3 38.0 %copy-start.1 = (bf16[32,8192]{1,0:T(8,128)(2,1)S(1)}, bf16[32,8192]{1,0:T(8,128)(2,1)}, u32[]{:S(2)}) copy-start(bf16[32,8192]{1,0:T(8,128)(2,1)} %param.13) | copy-start | bytes 1572868
  77.3 40.0 %copy-start.2 = (bf16[8192]{0:T(1024)(128)(2,1)S(1)}, bf16[8192]{0:T(1024)(128)(2,1)}, u32[]{:S(2)}) copy-start(bf16[8192]{0:T(1024)(128)(2,1)} %param.24) | copy-start | bytes 49156
  77.3 71.1 %all-gather.5.cloned.1.call-start = ((), (), s32[]{:S(2)}) async-start(), calls=%async_computation.4 | async-start | bytes 4718592 | tf_op jit(solution)/shard_map/all_gather | solution.py:129
Sparse Core Ops, SparseCore 0:
  9.0 34.5 all-gather.2
  77.4 37.8 reduce-scatter.1
  117.4 30.9 all-gather.4

commit v2 on v1

--- a/solution.py
+++ b/solution.py
@@ -1,7 +1,7 @@
 import jax
 import jax.numpy as jnp
 from jax import lax
-from jax.sharding import PartitionSpec as P
+from jax.sharding import Mesh, PartitionSpec as P
 
 HEAD_DIM = 128
 SESS = 16
@@ -67,6 +67,74 @@
         "skgmn,snkd->smkgd", weight_fresh, v_slots, preferred_element_type=jnp.float32
     )
     return mixed.astype(jnp.bfloat16)
+
+
+def shift(values, axis, step):
+    size = lax.axis_size(axis)
+    return lax.ppermute(values, axis, [(i, (i + step) % size) for i in range(size)])
+
+
+def pick(values, index):
+    return lax.dynamic_index_in_dim(values, index, 0, keepdims=False)
+
+
+def exchange(values, axis):
+    here = lax.axis_index(axis)
+    return [pick(values, here)] + [
+        shift(pick(values, (here + d) % 4), axis, d) for d in (1, 3, 2)
+    ]
+
+
+def in_order(parts, sources, shape):
+    held = jnp.zeros((len(parts),) + shape, parts[0].dtype)
+    for part, source in zip(parts, sources):
+        held = lax.dynamic_update_index_in_dim(held, part, source, 0)
+    return held
+
+
+def all_to_all_4(values, axis):
+    here = lax.axis_index(axis)
+    got = exchange(values, axis)
+    return in_order(got, [(here - d) % 4 for d in (0, 1, 3, 2)], values.shape[1:])
+
+
+def gather_4(values, axis):
+    here = lax.axis_index(axis)
+    half = values.shape[0] // 2
+    left, right = shift(values, axis, 1), shift(values, axis, -1)
+    far = jnp.concatenate([shift(left[:half], axis, 1), shift(right[half:], axis, -1)], 0)
+    return [values, left, right, far], [(here - d) % 4 for d in (0, 1, 3, 2)]
+
+
+def gather_rows(rows):
+    y, core = lax.axis_index("y"), lax.axis_index("core")
+    blocks, sources = gather_4(rows, "y")
+    twins = [shift(block, "core", 1) for block in blocks]
+    every = jnp.zeros((8,) + rows.shape, rows.dtype)
+    for block, twin, source in zip(blocks, twins, sources):
+        every = lax.dynamic_update_index_in_dim(every, block, source * 2 + core, 0)
+        every = lax.dynamic_update_index_in_dim(every, twin, source * 2 + 1 - core, 0)
+    return every.reshape(-1, rows.shape[1])
+
+
+def talker_rows_of(w_talker):
+    core = lax.axis_index("core")
+    group = lax.axis_index("x") * 4 + lax.axis_index("z")
+    width = w_talker.shape[1]
+    depth = w_talker.shape[0] // 8
+    piece = depth // 16
+    mine = lax.dynamic_index_in_dim(
+        w_talker.reshape(4, 2, 16, piece, width), group, 2, keepdims=False
+    )
+    kept = lax.dynamic_index_in_dim(mine, core, 1, keepdims=False)
+    twin = shift(lax.dynamic_index_in_dim(mine, 1 - core, 1, keepdims=False), "core", 1)
+    both = jnp.where(core == 0, jnp.stack([kept, twin], 1), jnp.stack([twin, kept], 1))
+    across = all_to_all_4(both, "y").reshape(8, piece, width)
+    strip = jnp.transpose(across, (1, 0, 2)).reshape(piece, 8 * width)
+    parts, sources = gather_4(strip, "z")
+    strip = in_order(parts, sources, strip.shape).reshape(4 * piece, 8 * width)
+    parts, sources = gather_4(strip, "x")
+    return in_order(parts, sources, strip.shape).reshape(depth, 8 * width)
 
 
 def on_device(
@@ -84,11 +152,16 @@
     talker_gain,
     w_talker,
 ):
+    model_width = thinker_rows.shape[1]
     kv_local = w_key.shape[1] // HEAD_DIM
     head_width = GQA * HEAD_DIM
     slot_count = SESS * MOST
-    owner_count = lax.axis_size("grp")
-    gathered = lax.all_gather(thinker_rows, "tp", axis=0, tiled=True)
+    owner_count = 16
+    y, core = lax.axis_index("y"), lax.axis_index("core")
+    member = y * 2 + core
+    share = model_width // 8
+    gathered = gather_rows(thinker_rows)
+    talker_block = talker_rows_of(w_talker)
     normed = rms_scaled(gathered, norm_gain)
     query = jnp.dot(normed, w_query, preferred_element_type=jnp.float32).astype(jnp.bfloat16)
     key_new = jnp.dot(normed, w_key, preferred_element_type=jnp.float32).astype(jnp.bfloat16)
@@ -121,43 +194,78 @@
     partial_sum = jnp.dot(attention_rows, w_out, preferred_element_type=jnp.float32).astype(
         jnp.bfloat16
     )
-    head_total = partial_sum.astype(jnp.float32)
-    summed = lax.psum_scatter(
-        head_total.astype(jnp.bfloat16), "tp", scatter_dimension=0, tiled=True
-    ).astype(jnp.float32)
-    hidden_local = (thinker_rows.astype(jnp.float32) + summed).astype(jnp.bfloat16)
-    hidden = lax.all_gather(hidden_local, "tp", axis=0, tiled=True)
-    talker_here = jnp.dot(
-        rms_scaled(hidden, talker_gain), w_talker, preferred_element_type=jnp.float32
+    def block_of(chip, which):
+        return lax.dynamic_slice(
+            partial_sum, (0, ((chip % 4) * 2 + which) * share), (partial_sum.shape[0], share)
+        )
+
+    def joined(chip):
+        other = shift(block_of(chip, 1 - core), "core", 1)
+        return block_of(chip, core).astype(jnp.float32) + other.astype(jnp.float32)
+
+    half = partial_sum.shape[0] // 2
+    far = joined(y + 2).astype(jnp.bfloat16)
+    ahead, behind = shift(far[:half], "y", 1), shift(far[half:], "y", -1)
+    none = jnp.zeros((half, share), jnp.float32)
+    to_next = joined(y + 1) + jnp.concatenate([ahead.astype(jnp.float32), none], 0)
+    to_last = joined(y + 3) + jnp.concatenate([none, behind.astype(jnp.float32)], 0)
+    from_last = shift(to_next.astype(jnp.bfloat16), "y", 1)
+    from_next = shift(to_last.astype(jnp.bfloat16), "y", -1)
+    own = lax.dynamic_slice(gathered, (0, member * share), (gathered.shape[0], share))
+    hidden = (
+        own.astype(jnp.float32)
+        + joined(y)
+        + from_last.astype(jnp.float32)
+        + from_next.astype(jnp.float32)
     ).astype(jnp.bfloat16)
+    floats = hidden.astype(jnp.float32)
+    squares = jnp.sum(floats * floats, axis=1)
+    squares = squares + shift(squares, "core", 1)
+    squares = squares + shift(squares, "y", 1) + shift(squares, "y", 2) + shift(squares, "y", 3)
+    scale = lax.rsqrt(squares / model_width + EPSILON)
+    gain = lax.dynamic_slice(talker_gain, (member * share,), (share,)).astype(jnp.float32)
+    product = jnp.dot(
+        (floats * gain[None, :]).astype(jnp.bfloat16),
+        talker_block,
+        preferred_element_type=jnp.float32,
+    ).reshape(-1, 4, 2, w_talker.shape[1])
+    kept = lax.dynamic_index_in_dim(product, core, 2, keepdims=False)
+    sent = lax.dynamic_index_in_dim(product, 1 - core, 2, keepdims=False)
+    kept = kept + shift(sent.astype(jnp.bfloat16), "core", 1).astype(jnp.float32)
+    kept = jnp.transpose(kept, (1, 0, 2))
+    got = exchange(kept.astype(jnp.bfloat16), "y")
+    total = pick(kept, y) + sum(part.astype(jnp.float32) for part in got[1:])
+    talker_here = (total * scale[:, None]).astype(jnp.bfloat16)
     outgoing = (
         jnp.dot(routing, talker_here, preferred_element_type=jnp.float32)
         .astype(jnp.bfloat16)
-        .reshape(owner_count, CAPS * MOST, w_talker.shape[1])
-    )
-    arrived = lax.all_to_all(outgoing, "grp", split_axis=0, concat_axis=0, tiled=True)
+        .reshape(4, 4, CAPS * MOST, w_talker.shape[1])
+    )
+    arrived = jnp.transpose(all_to_all_4(outgoing, "x"), (1, 0, 2, 3))
+    arrived = jnp.transpose(all_to_all_4(arrived, "z"), (1, 0, 2, 3))
     return arrived.reshape(owner_count * CAPS * MOST, w_talker.shape[1])
 
 
 def solution(mesh):
+    grp, tp = ("x", "z"), ("y", "core")
     return jax.shard_map(
         on_device,
-        mesh=mesh,
+        mesh=Mesh(mesh.devices.reshape(4, 4, 4, 2), grp + tp),
         in_specs=(
-            P(("grp", "tp"), None),
+            P(grp + tp, None),
             P(),
-            P(None, "tp"),
-            P(None, "tp"),
-            P(None, "tp"),
-            P("tp", None),
-            P("grp", None, "tp"),
-            P("grp", None, "tp"),
-            P("grp", None),
-            P("grp", None),
-            P("grp", None),
+            P(None, tp),
+            P(None, tp),
+            P(None, tp),
+            P(tp, None),
+            P(grp, None, tp),
+            P(grp, None, tp),
+            P(grp, None),
+            P(grp, None),
+            P(grp, None),
             P(),
-            P(None, "tp"),
+            P(None, tp),
         ),
-        out_specs=P("grp", "tp"),
+        out_specs=P(grp, tp),
         check_vma=False,
     )

time: 178 us -> 179 us (level)
  waiting for transfers between devices: 100 us -> 43.4 us
  starting transfers between devices: 0.08 us -> 50.3 us
  local copies, waits for them, and re-layouts: 1.02 us -> 29.5 us
  blocking collectives: 14.8 us -> 0 us
  between operations: 13.3 us -> 0.84 us
  other arithmetic: 15.1 us -> 21.6 us
    all_gather x2 -> x0, waiting for transfers between devices: 61.7 us -> none  [the longest x1 31.1 us: on_device(): hidden = lax.all_gather(hidden_local, 'tp', axis=0, tiled=True)]
    ppermute x0 -> x42, starting transfers between devices: none -> 50.3 us  [shift(): lax.ppermute(values, axis, [(i, (i + step) % size) for i in range(size)])]
    ppermute x0 -> x42, waiting for transfers between devices: none -> 43.4 us  [shift(): lax.ppermute(values, axis, [(i, (i + step) % size) for i in range(size)])]
    reduce_scatter x1 -> x0, waiting for transfers between devices: 37.9 us -> none  [on_device(): lax.psum_scatter(head_total.astype(jnp.bfloat16), 'tp', scatter_dimension...]
    all_to_all x1 -> x0, blocking collectives: 14.8 us -> none  [on_device(): lax.all_to_all(outgoing, 'grp', split_axis=0, concat_axis=0, tiled=True)]
    dynamic_update_slice x0 -> x25, local copies, waits for them, and re-layouts: none -> 12.1 us  [the longest x4 4.46 us: gather_rows(): lax.dynamic_update_index_in_dim(every, twin, source * 2 + 1 - core, 0)]
    convert_element_type x1 -> x5, other arithmetic: 1.98 us -> 11.5 us  [the longest x1 5.31 us: rms_scaled(): (floats * lax.rsqrt(mean_square + EPSILON) * weights.astype(jnp.float32))...]
    slice x0 -> x7, local copies, waits for them, and re-layouts: none -> 5.74 us  [the longest x3 2.46 us: gather_4(): right[half:]]
  transfers between devices with their start and end apart: 3 -> 42, of which waited for: 3 -> 15; matrix products, arithmetic and copies ran while one was open for 3% -> 43% of each run, Pallas kernels for 0% -> 0%
where the time goes in v2:
time: 179 us; the launch traced here: 178 us
  starting transfers between devices  50.3 us (28%)
  waiting for transfers between devices  43.4 us (24%)
  matrix products  32.3 us (18%)
  local copies, waits for them, and re-layouts  29.5 us (16%)
  other arithmetic  21.6 us (12%)
    ppermute x42, starting transfers between devices, shift(): lax.ppermute(values, axis, [(i, (i + step) % size) for i in range(size)])  50.3 us
    ppermute x42, waiting for transfers between devices, shift(): lax.ppermute(values, axis, [(i, (i + step) % size) for i in range(size)])  43.4 us
    dot_general x1, matrix products, on_device(): jnp.dot(attention_rows, w_out, preferred_element_type=jnp.float32)  8.18 us
    dot_general x1, matrix products, on_device(): jnp.dot(placing, query, preferred_element_type=jnp.float32)  7.2 us
    convert_element_type x1, other arithmetic, rms_scaled(): (floats * lax.rsqrt(mean_square + EPSILON) * weights.astype(jnp.float32))...  5.31 us
    dynamic_update_slice x4, local copies, waits for them, and re-layouts, gather_rows(): lax.dynamic_update_index_in_dim(every, twin, source * 2 + 1 - core, 0)  4.46 us
    dot_general x1, matrix products, on_device(): jnp.dot(placing, value_new, preferred_element_type=jnp.float32)  4.44 us
    dynamic_update_slice x4, local copies, waits for them, and re-layouts, gather_rows(): every = lax.dynamic_update_index_in_dim(every, block, source * 2 + core, 0)  4.44 us
  transfers between devices with their start and end apart: 42, of which 15 were waited for; matrix products, arithmetic and copies ran while one was open for 43% of the time, Pallas kernels for 0%

profile of v2, /device:TPU:0, one launch (start us, length us, event | category | flops | bytes accessed | tf_op | source)
XLA Modules:
  0.0 178.0 jit_solution(11939069314952258483)
XLA Ops:
  0.1 1.8 collective-permute-start.1
  1.9 1.5 collective-permute-start.3
  7.0 2.5 %broadcast_in_dim.145 = bf16[8,32,8192]{2,1,0:T(8,128)(2,1)} broadcast(bf16[]{:T(256)} %constant.359.clone.1), dimensions={} | broadcast | bytes 4194306 | tf_op jit(solution)/shard_map/broadcast_in_dim | solution.py:113
  11.6 2.8 %collective-permute-start.18 = (bf16[2,64,128]{2,1,0:T(8,128)(2,1)S(1)}, bf16[2,64,128]{2,1,0:T(8,128)(2,1)S(1)}, u32[]{:S(2)}, u32[]{:S(2)}) collective-permute-start(bf16[2,64,128]{2,1,0:T(8,128)(2,1)S(1)} %get-tuple-element.31), channel_id=1, source_target_pairs={{0,6},{2,0},{4,2},{6,4},{1,7},{3,1},{5,3},{7,5},{8,14},{10,8},{12,... | collective-permute-start | bytes 98312 | tf_op jit(solution)/shard_map/ppermute | solution.py:74
  14.4 2.4 %collective-permute-done.17 = bf16[2,64,128]{2,1,0:T(8,128)(2,1)S(1)} collective-permute-done((bf16[2,64,128]{2,1,0:T(8,128)(2,1)S(1)}, bf16[2,64,128]{2,1,0:T(8,128)(2,1)S(1)}, u32[]{:S(2)}, u32[]{:S(2)}) %collective-permute-start.17) | collective-permute-done | bytes 32800 | tf_op jit(solution)/shard_map/ppermute | solution.py:74
  16.7 1.9 %collective-permute-start.19 = (bf16[2,64,128]{2,1,0:T(8,128)(2,1)S(1)}, bf16[2,64,128]{2,1,0:T(8,128)(2,1)S(1)}, u32[]{:S(2)}, u32[]{:S(2)}) collective-permute-start(bf16[2,64,128]{2,1,0:T(8,128)(2,1)S(1)} %get-tuple-element.30), channel_id=1, source_target_pairs={{0,4},{2,6},{4,0},{6,2},{1,5},{3,7},{5,1},{7,3},{8,12},{10,14},{12... | collective-permute-start | bytes 98312 | tf_op jit(solution)/shard_map/ppermute | solution.py:74
  18.7 3.5 %collective-permute-done.19 = bf16[2,64,128]{2,1,0:T(8,128)(2,1)S(1)} collective-permute-done((bf16[2,64,128]{2,1,0:T(8,128)(2,1)S(1)}, bf16[2,64,128]{2,1,0:T(8,128)(2,1)S(1)}, u32[]{:S(2)}, u32[]{:S(2)}) %collective-permute-start.19) | collective-permute-done | bytes 32800 | tf_op jit(solution)/shard_map/ppermute | solution.py:74
  22.9 1.9 %collective-permute-start.20 = (bf16[64,1024]{1,0:T(8,128)(2,1)}, bf16[64,1024]{1,0:T(8,128)(2,1)}, u32[]{:S(2)}, u32[]{:S(2)}) collective-permute-start(bf16[64,1024]{1,0:T(8,128)(2,1)} %bitcast.224), channel_id=1, source_target_pairs={{0,8},{8,16},{16,24},{24,0},{1,9},{9,17},{17,25},{25,1},{2,10},{10... | collective-permute-start | bytes 393224 | tf_op jit(solution)/shard_map/ppermute | solution.py:74
  24.8 2.1 %collective-permute-start.21 = (bf16[64,1024]{1,0:T(8,128)(2,1)}, bf16[64,1024]{1,0:T(8,128)(2,1)}, u32[]{:S(2)}, u32[]{:S(2)}) collective-permute-start(bf16[64,1024]{1,0:T(8,128)(2,1)} %bitcast.224), channel_id=1, source_target_pairs={{0,24},{8,0},{16,8},{24,16},{1,25},{9,1},{17,9},{25,17},{2,26},{10... | collective-permute-start | bytes 393224 | tf_op jit(solution)/shard_map/ppermute | solution.py:74
  27.3 2.9 %collective-permute-done.20 = bf16[64,1024]{1,0:T(8,128)(2,1)} collective-permute-done((bf16[64,1024]{1,0:T(8,128)(2,1)}, bf16[64,1024]{1,0:T(8,128)(2,1)}, u32[]{:S(2)}, u32[]{:S(2)}) %collective-permute-start.20) | collective-permute-done | bytes 131104 | tf_op jit(solution)/shard_map/ppermute | solution.py:74
  30.2 1.5 slice.36
  31.6 1.5 slice.37
  33.1 3.2 %collective-permute-start.23 = (bf16[32,1024]{1,0:T(8,128)(2,1)}, bf16[32,1024]{1,0:T(8,128)(2,1)}, u32[]{:S(2)}, u32[]{:S(2)}) collective-permute-start(bf16[32,1024]{1,0:T(8,128)(2,1)} %slice.37), channel_id=1, source_target_pairs={{0,24},{8,0},{16,8},{24,16},{1,25},{9,1},{17,9},{25,17},{2,26},{10... | collective-permute-start | bytes 196616 | tf_op jit(solution)/shard_map/ppermute | solution.py:74
  37.7 3.0 %collective-permute-start.6 = (bf16[16,8192]{1,0:T(8,128)(2,1)S(1)}, bf16[16,8192]{1,0:T(8,128)(2,1)S(1)}, u32[]{:S(2)}, u32[]{:S(2)}) collective-permute-start(bf16[16,8192]{1,0:T(8,128)(2,1)S(1)} %slice.33), channel_id=1, source_target_pairs={{0,6},{2,0},{4,2},{6,4},{1,7},{3,1},{5,3},{7,5},{8,14},{10,8},{12,... | collective-permute-start | bytes 786440 | tf_op jit(solution)/shard_map/ppermute | solution.py:74
  40.7 1.9 %bitcast_dynamic-update-slice_fusion.9 = bf16[8,32,8192]{2,1,0:T(8,128)(2,1)} fusion(bf16[8,32,8192]{2,1,0:T(8,128)(2,1)} %bitcast_dynamic-update-slice_fusion.10, s32[]{:T(128)S(6)} %select_n.319, bf16[32,8192]{1,0:T(8,128)(2,1)} %collective-permute-done), kind=kLoop, calls=%fused_computation.59 | loop fusion | bytes 1048580 | tf_op jit(solution)/shard_map/jit(dynamic_update_index_in_dim)/dynamic_update_slice | solution.py:116
  42.6 1.9 %bitcast_dynamic-update-slice_fusion.8 = bf16[8,32,8192]{2,1,0:T(8,128)(2,1)} fusion(bf16[8,32,8192]{2,1,0:T(8,128)(2,1)} %bitcast_dynamic-update-slice_fusion.9, s32[]{:T(128)S(6)} %select_n.321, bf16[32,8192]{1,0:T(8,128)(2,1)} %collective-permute-done.1), kind=kLoop, calls=%fused_computation.58 | loop fusion | bytes 1048580 | tf_op jit(solution)/shard_map/jit(dynamic_update_index_in_dim)/dynamic_update_slice | solution.py:115
  50.1 3.1 %multiply_reduce_fusion = f32[8,32]{1,0:T(8,128)S(1)} fusion(bf16[8,32,8192]{2,1,0:T(8,128)(2,1)} %bitcast_dynamic-update-slice_fusion.3), kind=kLoop, calls=%fused_computation.2 | loop fusion | flops 6291200 | bytes 4195328 | tf_op jit(solution)/shard_map/reduce_sum | solution.py:18
  53.3 5.3 %multiply_convert_fusion = bf16[256,8192]{1,0:T(8,128)(2,1)} fusion(f32[8192]{0:T(1024)S(1)} %convert_element_type.148, f32[256]{0:T(256)S(1)} %rsqrt.15, bf16[8,32,8192]{2,1,0:T(8,128)(2,1)} %bitcast_dynamic-update-slice_fusion.3), kind=kLoop, calls=%fused_computation.1 | loop fusion | flops 8388608 | bytes 8422400 | tf_op jit(solution)/shard_map/convert_element_type | solution.py:19
  58.6 7.2 %convolution_convert_fusion.1 = bf16[320,512]{1,0:T(8,128)(2,1)S(1)} fusion(bf16[256,8192]{1,0:T(8,128)(2,1)} %multiply_convert_fusion, bf16[8192,512]{1,0:T(8,128)(2,1)} %param.15, s32[256]{0:T(256)S(1)} %bitcast.237), kind=kOutput, calls=%fused_computation.20 | convolution fusion | flops 2231746560 | bytes 12911616 | tf_op jit(solution)/shard_map/dot_general | solution.py:173
  65.9 3.7 %convolution_convert_fusion.6 = bf16[320,128]{1,0:T(8,128)(2,1)S(1)} fusion(bf16[256,8192]{1,0:T(8,128)(2,1)} %multiply_convert_fusion, bf16[8192,128]{1,0:T(8,128)(2,1)S(1)} %copy-done, s32[256]{0:T(256)S(1)} %bitcast.238), kind=kOutput, calls=%fused_computation.32 | convolution fusion | flops 557998080 | bytes 6374400 | tf_op jit(solution)/shard_map/dot_general | solution.py:174
  69.6 2.3 %fusion.2 = (f32[16,4,20]{2,1,0:T(4,128)S(1)}, f32[16,20,4,320]{3,1,2,0:T(8,128)S(1)}) fusion(pred[16,320]{1,0:T(8,128)(4,1)S(1)} %iota_compare_fusion.8, bf16[16,320,128]{2,1,0:T(8,128)(2,1)} %param.19, bf16[16,20,4,128]{3,2,1,0:T(4,128)(2,1)S(1)} %reshape.262), kind=kOutput, calls=%fused_computation.8 | convolution fusion | flops 106085120 | bytes 3287040 | tf_op jit(solution)/shard_map/smkgd,sckd->skgmc/dot_general | solution.py:44
  74.4 4.4 %convolution_convert_fusion.5 = bf16[320,128]{1,0:T(8,128)(2,1)S(1)} fusion(bf16[256,8192]{1,0:T(8,128)(2,1)} %multiply_convert_fusion, bf16[8192,128]{1,0:T(8,128)(2,1)} %param.17, s32[256]{0:T(256)S(1)} %bitcast.239), kind=kOutput, calls=%fused_computation.31 | convolution fusion | flops 557998080 | bytes 6374400 | tf_op jit(solution)/shard_map/dot_general | solution.py:175
  79.2 2.6 %fusion.18 = bf16[16,20,1,4,128]{4,1,3,0,2:T(8,128)(2,1)S(1)} fusion(f32[16,128,4,20]{1,3,2,0:T(8,128)S(1)} %fusion.34, bf16[16,320,128]{2,1,0:T(8,128)(2,1)S(1)} %copy-done.7, f32[16,20,4,320]{3,1,2,0:T(8,128)} %copy-done.2, f32[16,4,20]{2,1,0:T(4,128)S(1)} %add.483, f32[16,4,20]{2,1,0:T(4,128)S(1)} %max.9, pred[16,320]{1,0:T(8,128)(4,1)S(1)} %iota_compare_fusion.8), kind=kOutput, calls=%fused_computation.22 | convolution fusion | flops 107233280 | bytes 3947520 | tf_op jit(solution)/shard_map/skgmc,sckd->smkgd/dot_general | solution.py:63
  81.9 8.2 %convolution_convert_fusion = bf16[256,8192]{1,0:T(8,128)(2,1)} fusion(bf16[512,8192]{1,0:T(8,128)(2,1)} %param.18, bf16[40,8,4,128]{3,2,1,0:T(4,128)(2,1)S(1)} %bitcast.228, s32[256]{0:T(256)S(1)} %bitcast.240), kind=kOutput, calls=%fused_computation | convolution fusion | flops 2233679872 | bytes 12911616 | tf_op jit(solution)/shard_map/dot_general | solution.py:194
  90.1 2.7 %constant_dynamic-slice_fusion.3 = (bf16[256,1024]{1,0:T(8,128)(2,1)}, bf16[256,1024]{1,0:T(8,128)(2,1)}, bf16[256,1024]{1,0:T(8,128)(2,1)S(1)}, bf16[256,1024]{1,0:T(8,128)(2,1)}) fusion(bf16[256,8192]{1,0:T(8,128)(2,1)} %convolution_convert_fusion, s32[]{:T(128)S(6)} %select_n.334, s32[]{:T(128)S(6)} %select_n.343, s32[]{:T(128)S(6)} %select_n.340, ...), kind=kLoop, calls=%fused_computation.126 | loop fusion | bytes 4194320 | tf_op jit(solution)/shard_map/dynamic_slice | solution.py:198
  95.6 1.6 collective-permute-start.24
  97.2 1.7 collective-permute-start.25
  99.4 1.2 add_convert_fusion.3
  102.2 9.0 %collective-permute-done.24 = bf16[256,1024]{1,0:T(8,128)(2,1)S(1)} collective-permute-done((bf16[256,1024]{1,0:T(8,128)(2,1)S(1)}, bf16[256,1024]{1,0:T(8,128)(2,1)S(1)}, u32[]{:S(2)}, u32[]{:S(2)}) %collective-permute-start.24) | collective-permute-done | bytes 524320 | tf_op jit(solution)/shard_map/ppermute | solution.py:74
  111.2 2.7 %collective-permute-start.14 = (bf16[128,1024]{1,0:T(8,128)(2,1)}, bf16[128,1024]{1,0:T(8,128)(2,1)}, u32[]{:S(2)}, u32[]{:S(2)}) collective-permute-start(bf16[128,1024]{1,0:T(8,128)(2,1)} %get-tuple-element.20), channel_id=1, source_target_pairs={{0,6},{2,0},{4,2},{6,4},{1,7},{3,1},{5,3},{7,5},{8,14},{10,8},{12,... | collective-permute-start | bytes 786440 | tf_op jit(solution)/shard_map/ppermute | solution.py:74
  116.3 3.0 %collective-permute-start.27 = (bf16[128,1024]{1,0:T(8,128)(2,1)S(1)}, bf16[128,1024]{1,0:T(8,128)(2,1)S(1)}, u32[]{:S(2)}, u32[]{:S(2)}) collective-permute-start(bf16[128,1024]{1,0:T(8,128)(2,1)S(1)} %slice.39), channel_id=1, source_target_pairs={{0,96},{32,0},{64,32},{96,64},{1,97},{33,1},{65,33},{97,65},{2,98}... | collective-permute-start | bytes 786440 | tf_op jit(solution)/shard_map/ppermute | solution.py:74
  119.4 3.2 %add_convert_fusion.2 = (bf16[256,1024]{1,0:T(8,128)(2,1)}, bf16[256,1024]{1,0:T(8,128)(2,1)}) fusion(bf16[256,1024]{1,0:T(8,128)(2,1)} %collective-permute-done.9, bf16[128,1024]{1,0:T(8,128)(2,1)} %collective-permute-done.11, bf16[256,8192]{1,0:T(8,128)(2,1)} %convolution_convert_fusion, s32[]{:T(128)S(6)} %select_n.336, ...), kind=kLoop, calls=%fused_computation.39 | loop fusion | flops 3145728 | bytes 3670024 | tf_op jit(solution)/shard_map/convert_element_type | solution.py:212
  122.6 3.4 %collective-permute-start.15 = (bf16[256,1024]{1,0:T(8,128)(2,1)}, bf16[256,1024]{1,0:T(8,128)(2,1)}, u32[]{:S(2)}, u32[]{:S(2)}) collective-permute-start(bf16[256,1024]{1,0:T(8,128)(2,1)} %get-tuple-element.16), channel_id=1, source_target_pairs={{0,6},{2,0},{4,2},{6,4},{1,7},{3,1},{5,3},{7,5},{8,14},{10,8},{12,... | collective-permute-start | bytes 1572872 | tf_op jit(solution)/shard_map/ppermute | solution.py:74
  127.2 2.7 %copy.63 = bf16[1024,1024]{1,0:T(8,128)(2,1)} copy(bf16[1024,1024]{0,1:T(8,128)(2,1)S(1)} %bitcast.227) | data formatting | bytes 4194304 | tf_op jit(solution)/shard_map/dot_general | solution.py:227
  129.9 8.5 %collective-permute-done.12 = bf16[256,1024]{1,0:T(8,128)(2,1)} collective-permute-done((bf16[256,1024]{1,0:T(8,128)(2,1)}, bf16[256,1024]{1,0:T(8,128)(2,1)}, u32[]{:S(2)}, u32[]{:S(2)}) %collective-permute-start.12) | collective-permute-done | bytes 524320 | tf_op jit(solution)/shard_map/ppermute | solution.py:74
  138.4 2.0 %fusion.27 = (f32[256]{0:T(256)S(1)}, bf16[256,1024]{1,0:T(8,128)(2,1)S(1)}) fusion(bf16[256,1024]{1,0:T(8,128)(2,1)} %collective-permute-done.15, bf16[256,1024]{1,0:T(8,128)(2,1)} %collective-permute-done.12, bf16[256,1024]{1,0:T(8,128)(2,1)S(1)} %collective-permute-done.8, bf16[256,8192]{1,0:T(8,128)(2,1)} %convolution_convert_fusion, s32[]{:T(128)S(6)} %select_n.333, ...), kind=kLoop, calls=%fused_computation.36 | loop fusion | flops 3407616 | bytes 3146760 | tf_op jit(solution)/shard_map/reduce_sum | solution.py:222
  140.4 2.5 %fusion.30 = f32[256,4,2,128]{3,0,2,1:T(8,128)S(1)} fusion(bf16[4,2,128,1024]{3,2,1,0:T(8,128)(2,1)} %bitcast.226, bf16[256,1024]{1,0:T(8,128)(2,1)S(1)} %get-tuple-element.8, f32[1024]{0:T(1024)S(1)} %dynamic-slice_convert_fusion.1), kind=kOutput, calls=%fused_computation.46 | convolution fusion | flops 537657344 | bytes 3674112 | tf_op jit(solution)/shard_map/dot_general | solution.py:227
  144.7 4.4 %collective-permute-start.34 = (f32[256]{0:T(256)S(1)}, f32[256]{0:T(256)S(1)}, u32[]{:S(2)}, u32[]{:S(2)}) collective-permute-start(f32[256]{0:T(256)S(1)} %add.547), channel_id=1, source_target_pairs={{0,4},{2,6},{4,0},{6,2},{1,5},{3,7},{5,1},{7,3},{8,12},{10,14},{12... | collective-permute-start | bytes 3080 | tf_op jit(solution)/shard_map/ppermute | solution.py:74
  150.2 2.1 %collective-permute-start.29 = (bf16[256,128]{1,0:T(8,128)(2,1)S(1)}, bf16[256,128]{1,0:T(8,128)(2,1)S(1)}, u32[]{:S(2)}, u32[]{:S(2)}) collective-permute-start(bf16[256,128]{1,0:T(8,128)(2,1)S(1)} %get-tuple-element.21), channel_id=1, source_target_pairs={{0,2},{2,4},{4,6},{6,0},{1,3},{3,5},{5,7},{7,1},{8,10},{10,12},{12... | collective-permute-start | bytes 196616 | tf_op jit(solution)/shard_map/ppermute | solution.py:74
  152.3 1.2 collective-permute-start.30
  154.4 1.3 collective-permute-done.29
  156.5 2.7 %collective-permute-done.31 = bf16[256,128]{1,0:T(8,128)(2,1)S(1)} collective-permute-done((bf16[256,128]{1,0:T(8,128)(2,1)S(1)}, bf16[256,128]{1,0:T(8,128)(2,1)S(1)}, u32[]{:S(2)}, u32[]{:S(2)}) %collective-permute-start.31) | collective-permute-done | bytes 65568 | tf_op jit(solution)/shard_map/ppermute | solution.py:74
  159.7 3.2 %collective-permute-start.37 = (bf16[4,40,128]{2,1,0:T(8,128)(2,1)S(1)}, bf16[4,40,128]{2,1,0:T(8,128)(2,1)S(1)}, u32[]{:S(2)}, u32[]{:S(2)}) collective-permute-start(bf16[4,40,128]{2,1,0:T(8,128)(2,1)S(1)} %get-tuple-element.28), channel_id=1, source_target_pairs={{0,96},{32,0},{64,32},{96,64},{1,97},{33,1},{65,33},{97,65},{2,98}... | collective-permute-start | bytes 122888 | tf_op jit(solution)/shard_map/ppermute | solution.py:74
  163.2 2.0 %collective-permute-done.36 = bf16[4,40,128]{2,1,0:T(8,128)(2,1)S(1)} collective-permute-done((bf16[4,40,128]{2,1,0:T(8,128)(2,1)S(1)}, bf16[4,40,128]{2,1,0:T(8,128)(2,1)S(1)}, u32[]{:S(2)}, u32[]{:S(2)}) %collective-permute-start.36) | collective-permute-done | bytes 40992 | tf_op jit(solution)/shard_map/ppermute | solution.py:74
  165.3 3.2 %collective-permute-done.38 = bf16[4,40,128]{2,1,0:T(8,128)(2,1)S(1)} collective-permute-done((bf16[4,40,128]{2,1,0:T(8,128)(2,1)S(1)}, bf16[4,40,128]{2,1,0:T(8,128)(2,1)S(1)}, u32[]{:S(2)}, u32[]{:S(2)}) %collective-permute-start.38) | collective-permute-done | bytes 40992 | tf_op jit(solution)/shard_map/ppermute | solution.py:74
  168.6 3.2 %collective-permute-start.40 = (bf16[4,40,128]{2,1,0:T(8,128)(2,1)S(1)}, bf16[4,40,128]{2,1,0:T(8,128)(2,1)S(1)}, u32[]{:S(2)}, u32[]{:S(2)}) collective-permute-start(bf16[4,40,128]{2,1,0:T(8,128)(2,1)S(1)} %get-tuple-element.25), channel_id=1, source_target_pairs={{0,24},{8,0},{16,8},{24,16},{1,25},{9,1},{17,9},{25,17},{2,26},{10... | collective-permute-start | bytes 122888 | tf_op jit(solution)/shard_map/ppermute | solution.py:74
  171.8 1.9 %collective-permute-done.39 = bf16[4,40,128]{2,1,0:T(8,128)(2,1)S(1)} collective-permute-done((bf16[4,40,128]{2,1,0:T(8,128)(2,1)S(1)}, bf16[4,40,128]{2,1,0:T(8,128)(2,1)S(1)}, u32[]{:S(2)}, u32[]{:S(2)}) %collective-permute-start.39) | collective-permute-done | bytes 40992 | tf_op jit(solution)/shard_map/ppermute | solution.py:74
  173.8 3.5 %collective-permute-done.41 = bf16[4,40,128]{2,1,0:T(8,128)(2,1)S(1)} collective-permute-done((bf16[4,40,128]{2,1,0:T(8,128)(2,1)S(1)}, bf16[4,40,128]{2,1,0:T(8,128)(2,1)S(1)}, u32[]{:S(2)}, u32[]{:S(2)}) %collective-permute-start.41) | collective-permute-done | bytes 40992 | tf_op jit(solution)/shard_map/ppermute | solution.py:74
  (152 shorter events, 31.1 us)
Async XLA Ops:
  0.0 65.9 %copy-start = (bf16[8192,128]{1,0:T(8,128)(2,1)S(1)}, bf16[8192,128]{1,0:T(8,128)(2,1)}, u32[]{:S(2)}) copy-start(bf16[8192,128]{1,0:T(8,128)(2,1)} %param.16) | copy-start | bytes 6291460
  0.0 9.5 %copy-start.3 = (bf16[32,8192]{1,0:T(8,128)(2,1)S(1)}, bf16[32,8192]{1,0:T(8,128)(2,1)}, u32[]{:S(2)}) copy-start(bf16[32,8192]{1,0:T(8,128)(2,1)} %param.13) | copy-start | bytes 1572868
  0.0 11.4 %copy-start.6 = (s32[1,256]{1,0:T(1,128)S(1)}, s32[1,256]{1,0:T(1,128)}, u32[]{:S(2)}) copy-start(s32[1,256]{1,0:T(1,128)} %param.21) | copy-start | bytes 3076
  0.0 10.4 %copy-start.8 = (s32[16,1]{0,1:T(1,128)S(1)}, s32[16,1]{0,1:T(1,128)}, u32[]{:S(2)}) copy-start(s32[16,1]{0,1:T(1,128)} %param.23) | copy-start | bytes 196
  0.0 26.9 %copy-start.5 = (bf16[8192]{0:T(1024)(128)(2,1)S(1)}, bf16[8192]{0:T(1024)(128)(2,1)}, u32[]{:S(2)}) copy-start(bf16[8192]{0:T(1024)(128)(2,1)} %param.14) | copy-start | bytes 49156
  0.0 40.7 %collective-permute-start = (bf16[32,8192]{1,0:T(8,128)(2,1)}, bf16[32,8192]{1,0:T(8,128)(2,1)}, u32[]{:S(2)}, u32[]{:S(2)}) collective-permute-start(bf16[32,8192]{1,0:T(8,128)(2,1)} %param.13), channel_id=1, source_target_pairs={{0,1},{1,0},{2,3},{3,2},{4,5},{5,4},{6,7},{7,6},{8,9},{9,8},{10,11... | collective-permute-start | bytes 1572872 | tf_op jit(solution)/shard_map/ppermute | solution.py:74
  0.1 36.2 %collective-permute-start.1 = (bf16[32,8192]{1,0:T(8,128)(2,1)}, bf16[32,8192]{1,0:T(8,128)(2,1)}, u32[]{:S(2)}, u32[]{:S(2)}) collective-permute-start(bf16[32,8192]{1,0:T(8,128)(2,1)} %param.13), channel_id=1, source_target_pairs={{0,2},{2,4},{4,6},{6,0},{1,3},{3,5},{5,7},{7,1},{8,10},{10,12},{12... | collective-permute-start | bytes 1572872 | tf_op jit(solution)/shard_map/ppermute | solution.py:74
  1.9 35.8 %collective-permute-start.3 = (bf16[32,8192]{1,0:T(8,128)(2,1)}, bf16[32,8192]{1,0:T(8,128)(2,1)S(1)}, u32[]{:S(2)}, u32[]{:S(2)}) collective-permute-start(bf16[32,8192]{1,0:T(8,128)(2,1)} %param.13), channel_id=1, source_target_pairs={{0,6},{2,0},{4,2},{6,4},{1,7},{3,1},{5,3},{7,5},{8,14},{10,8},{12,... | collective-permute-start | bytes 1572872 | tf_op jit(solution)/shard_map/ppermute | solution.py:74
  4.3 6.5 %collective-permute-start.16 = (bf16[4,64,128]{2,1,0:T(8,128)(2,1)S(1)}, bf16[4,64,128]{2,1,0:T(8,128)(2,1)S(1)}, u32[]{:S(2)}, u32[]{:S(2)}) collective-permute-start(bf16[4,64,128]{2,1,0:T(8,128)(2,1)S(1)} %get-tuple-element.18), channel_id=1, source_target_pairs={{0,1},{1,0},{2,3},{3,2},{4,5},{5,4},{6,7},{7,6},{8,9},{9,8},{10,11... | collective-permute-start | bytes 196616 | tf_op jit(solution)/shard_map/ppermute | solution.py:74
  10.9 5.9 %collective-permute-start.17 = (bf16[2,64,128]{2,1,0:T(8,128)(2,1)S(1)}, bf16[2,64,128]{2,1,0:T(8,128)(2,1)S(1)}, u32[]{:S(2)}, u32[]{:S(2)}) collective-permute-start(bf16[2,64,128]{2,1,0:T(8,128)(2,1)S(1)} %get-tuple-element.32), channel_id=1, source_target_pairs={{0,2},{2,4},{4,6},{6,0},{1,3},{3,5},{5,7},{7,1},{8,10},{10,12},{12... | collective-permute-start | bytes 98312 | tf_op jit(solution)/shard_map/ppermute | solution.py:74
  11.6 7.1 %collective-permute-start.18 = (bf16[2,64,128]{2,1,0:T(8,128)(2,1)S(1)}, bf16[2,64,128]{2,1,0:T(8,128)(2,1)S(1)}, u32[]{:S(2)}, u32[]{:S(2)}) collective-permute-start(bf16[2,64,128]{2,1,0:T(8,128)(2,1)S(1)} %get-tuple-element.31), channel_id=1, source_target_pairs={{0,6},{2,0},{4,2},{6,4},{1,7},{3,1},{5,3},{7,5},{8,14},{10,8},{12,... | collective-permute-start | bytes 98312 | tf_op jit(solution)/shard_map/ppermute | solution.py:74
  16.7 5.4 %collective-permute-start.19 = (bf16[2,64,128]{2,1,0:T(8,128)(2,1)S(1)}, bf16[2,64,128]{2,1,0:T(8,128)(2,1)S(1)}, u32[]{:S(2)}, u32[]{:S(2)}) collective-permute-start(bf16[2,64,128]{2,1,0:T(8,128)(2,1)S(1)} %get-tuple-element.30), channel_id=1, source_target_pairs={{0,4},{2,6},{4,0},{6,2},{1,5},{3,7},{5,1},{7,3},{8,12},{10,14},{12... | collective-permute-start | bytes 98312 | tf_op jit(solution)/shard_map/ppermute | solution.py:74
  22.9 7.3 %collective-permute-start.20 = (bf16[64,1024]{1,0:T(8,128)(2,1)}, bf16[64,1024]{1,0:T(8,128)(2,1)}, u32[]{:S(2)}, u32[]{:S(2)}) collective-permute-start(bf16[64,1024]{1,0:T(8,128)(2,1)} %bitcast.224), channel_id=1, source_target_pairs={{0,8},{8,16},{16,24},{24,0},{1,9},{9,17},{17,25},{25,1},{2,10},{10... | collective-permute-start | bytes 393224 | tf_op jit(solution)/shard_map/ppermute | solution.py:74
  24.8 6.9 %collective-permute-start.21 = (bf16[64,1024]{1,0:T(8,128)(2,1)}, bf16[64,1024]{1,0:T(8,128)(2,1)}, u32[]{:S(2)}, u32[]{:S(2)}) collective-permute-start(bf16[64,1024]{1,0:T(8,128)(2,1)} %bitcast.224), channel_id=1, source_target_pairs={{0,24},{8,0},{16,8},{24,16},{1,25},{9,1},{17,9},{25,17},{2,26},{10... | collective-permute-start | bytes 393224 | tf_op jit(solution)/shard_map/ppermute | solution.py:74
  31.6 63.1 %collective-permute-start.22 = (bf16[32,1024]{1,0:T(8,128)(2,1)}, bf16[32,1024]{1,0:T(8,128)(2,1)}, u32[]{:S(2)}, u32[]{:S(2)}) collective-permute-start(bf16[32,1024]{1,0:T(8,128)(2,1)} %slice.36), channel_id=1, source_target_pairs={{0,8},{8,16},{16,24},{24,0},{1,9},{9,17},{17,25},{25,1},{2,10},{10... | collective-permute-start | bytes 196616 | tf_op jit(solution)/shard_map/ppermute | solution.py:74
  33.1 61.6 %collective-permute-start.23 = (bf16[32,1024]{1,0:T(8,128)(2,1)}, bf16[32,1024]{1,0:T(8,128)(2,1)}, u32[]{:S(2)}, u32[]{:S(2)}) collective-permute-start(bf16[32,1024]{1,0:T(8,128)(2,1)} %slice.37), channel_id=1, source_target_pairs={{0,24},{8,0},{16,8},{24,16},{1,25},{9,1},{17,9},{25,17},{2,26},{10... | collective-permute-start | bytes 196616 | tf_op jit(solution)/shard_map/ppermute | solution.py:74
  37.3 7.7 %collective-permute-start.5 = (bf16[16,8192]{1,0:T(8,128)(2,1)S(1)}, bf16[16,8192]{1,0:T(8,128)(2,1)S(1)}, u32[]{:S(2)}, u32[]{:S(2)}) collective-permute-start(bf16[16,8192]{1,0:T(8,128)(2,1)S(1)} %slice.32), channel_id=1, source_target_pairs={{0,2},{2,4},{4,6},{6,0},{1,3},{3,5},{5,7},{7,1},{8,10},{10,12},{12... | collective-permute-start | bytes 786440 | tf_op jit(solution)/shard_map/ppermute | solution.py:74
  37.7 7.4 %collective-permute-start.6 = (bf16[16,8192]{1,0:T(8,128)(2,1)S(1)}, bf16[16,8192]{1,0:T(8,128)(2,1)S(1)}, u32[]{:S(2)}, u32[]{:S(2)}) collective-permute-start(bf16[16,8192]{1,0:T(8,128)(2,1)S(1)} %slice.33), channel_id=1, source_target_pairs={{0,6},{2,0},{4,2},{6,4},{1,7},{3,1},{5,3},{7,5},{8,14},{10,8},{12,... | collective-permute-start | bytes 786440 | tf_op jit(solution)/shard_map/ppermute | solution.py:74
  40.7 5.1 %collective-permute-start.2 = (bf16[32,8192]{1,0:T(8,128)(2,1)}, bf16[32,8192]{1,0:T(8,128)(2,1)S(1)}, u32[]{:S(2)}, u32[]{:S(2)}) collective-permute-start(bf16[32,8192]{1,0:T(8,128)(2,1)} %collective-permute-done.1), channel_id=1, source_target_pairs={{0,1},{1,0},{2,3},{3,2},{4,5},{5,4},{6,7},{7,6},{8,9},{9,8},{10,11... | collective-permute-start | bytes 1572872 | tf_op jit(solution)/shard_map/ppermute | solution.py:74
  45.0 2.6 %collective-permute-start.4 = (bf16[32,8192]{1,0:T(8,128)(2,1)S(1)}, bf16[32,8192]{1,0:T(8,128)(2,1)S(1)}, u32[]{:S(2)}, u32[]{:S(2)}) collective-permute-start(bf16[32,8192]{1,0:T(8,128)(2,1)S(1)} %collective-permute-done.3), channel_id=1, source_target_pairs={{0,1},{1,0},{2,3},{3,2},{4,5},{5,4},{6,7},{7,6},{8,9},{9,8},{10,11... | collective-permute-start | bytes 1572872 | tf_op jit(solution)/shard_map/ppermute | solution.py:74
  45.1 4.1 %collective-permute-start.7 = (bf16[32,8192]{1,0:T(8,128)(2,1)S(1)}, bf16[32,8192]{1,0:T(8,128)(2,1)S(1)}, u32[]{:S(2)}, u32[]{:S(2)}) collective-permute-start(bf16[32,8192]{1,0:T(8,128)(2,1)S(1)} %constant_dynamic-update-slice_fusion.1), channel_id=1, source_target_pairs={{0,1},{1,0},{2,3},{3,2},{4,5},{5,4},{6,7},{7,6},{8,9},{9,8},{10,11... | collective-permute-start | bytes 1572872 | tf_op jit(solution)/shard_map/ppermute | solution.py:74
  92.8 6.6 %collective-permute-start.10 = (bf16[256,1024]{1,0:T(8,128)(2,1)S(1)}, bf16[256,1024]{1,0:T(8,128)(2,1)S(1)}, u32[]{:S(2)}, u32[]{:S(2)}) collective-permute-start(bf16[256,1024]{1,0:T(8,128)(2,1)S(1)} %get-tuple-element.13), channel_id=1, source_target_pairs={{0,1},{1,0},{2,3},{3,2},{4,5},{5,4},{6,7},{7,6},{8,9},{9,8},{10,11... | collective-permute-start | bytes 1572872 | tf_op jit(solution)/shard_map/ppermute | solution.py:74
  95.6 15.6 %collective-permute-start.24 = (bf16[256,1024]{1,0:T(8,128)(2,1)S(1)}, bf16[256,1024]{1,0:T(8,128)(2,1)S(1)}, u32[]{:S(2)}, u32[]{:S(2)}) collective-permute-start(bf16[256,1024]{1,0:T(8,128)(2,1)S(1)} %bitcast.229), channel_id=1, source_target_pairs={{0,32},{32,64},{64,96},{96,0},{1,33},{33,65},{65,97},{97,1},{2,34}... | collective-permute-start | bytes 1572872 | tf_op jit(solution)/shard_map/ppermute | solution.py:74
  97.2 17.8 %collective-permute-start.25 = (bf16[256,1024]{1,0:T(8,128)(2,1)S(1)}, bf16[256,1024]{1,0:T(8,128)(2,1)}, u32[]{:S(2)}, u32[]{:S(2)}) collective-permute-start(bf16[256,1024]{1,0:T(8,128)(2,1)S(1)} %bitcast.230), channel_id=1, source_target_pairs={{0,96},{32,0},{64,32},{96,64},{1,97},{33,1},{65,33},{97,65},{2,98}... | collective-permute-start | bytes 1572872 | tf_op jit(solution)/shard_map/ppermute | solution.py:74
  98.9 17.4 %collective-permute-start.13 = (bf16[256,1024]{1,0:T(8,128)(2,1)}, bf16[256,1024]{1,0:T(8,128)(2,1)}, u32[]{:S(2)}, u32[]{:S(2)}) collective-permute-start(bf16[256,1024]{1,0:T(8,128)(2,1)} %get-tuple-element.12), channel_id=1, source_target_pairs={{0,1},{1,0},{2,3},{3,2},{4,5},{5,4},{6,7},{7,6},{8,9},{9,8},{10,11... | collective-permute-start | bytes 1572872 | tf_op jit(solution)/shard_map/ppermute | solution.py:74
  98.9 20.4 %collective-permute-start.9 = (bf16[256,1024]{1,0:T(8,128)(2,1)}, bf16[256,1024]{1,0:T(8,128)(2,1)}, u32[]{:S(2)}, u32[]{:S(2)}) collective-permute-start(bf16[256,1024]{1,0:T(8,128)(2,1)} %get-tuple-element.14), channel_id=1, source_target_pairs={{0,1},{1,0},{2,3},{3,2},{4,5},{5,4},{6,7},{7,6},{8,9},{9,8},{10,11... | collective-permute-start | bytes 1572872 | tf_op jit(solution)/shard_map/ppermute | solution.py:74
  101.5 17.8 %collective-permute-start.11 = (bf16[128,1024]{1,0:T(8,128)(2,1)}, bf16[128,1024]{1,0:T(8,128)(2,1)}, u32[]{:S(2)}, u32[]{:S(2)}) collective-permute-start(bf16[128,1024]{1,0:T(8,128)(2,1)} %get-tuple-element.19), channel_id=1, source_target_pairs={{0,2},{2,4},{4,6},{6,0},{1,3},{3,5},{5,7},{7,1},{8,10},{10,12},{12... | collective-permute-start | bytes 786440 | tf_op jit(solution)/shard_map/ppermute | solution.py:74
  111.2 8.2 %collective-permute-start.14 = (bf16[128,1024]{1,0:T(8,128)(2,1)}, bf16[128,1024]{1,0:T(8,128)(2,1)}, u32[]{:S(2)}, u32[]{:S(2)}) collective-permute-start(bf16[128,1024]{1,0:T(8,128)(2,1)} %get-tuple-element.20), channel_id=1, source_target_pairs={{0,6},{2,0},{4,2},{6,4},{1,7},{3,1},{5,3},{7,5},{8,14},{10,8},{12,... | collective-permute-start | bytes 786440 | tf_op jit(solution)/shard_map/ppermute | solution.py:74
  114.9 12.2 %collective-permute-start.26 = (bf16[128,1024]{1,0:T(8,128)(2,1)S(1)}, bf16[128,1024]{1,0:T(8,128)(2,1)S(1)}, u32[]{:S(2)}, u32[]{:S(2)}) collective-permute-start(bf16[128,1024]{1,0:T(8,128)(2,1)S(1)} %slice.38), channel_id=1, source_target_pairs={{0,32},{32,64},{64,96},{96,0},{1,33},{33,65},{65,97},{97,1},{2,34}... | collective-permute-start | bytes 786440 | tf_op jit(solution)/shard_map/ppermute | solution.py:74
  116.3 10.9 %collective-permute-start.27 = (bf16[128,1024]{1,0:T(8,128)(2,1)S(1)}, bf16[128,1024]{1,0:T(8,128)(2,1)S(1)}, u32[]{:S(2)}, u32[]{:S(2)}) collective-permute-start(bf16[128,1024]{1,0:T(8,128)(2,1)S(1)} %slice.39), channel_id=1, source_target_pairs={{0,96},{32,0},{64,32},{96,64},{1,97},{33,1},{65,33},{97,65},{2,98}... | collective-permute-start | bytes 786440 | tf_op jit(solution)/shard_map/ppermute | solution.py:74
  119.3 10.6 %collective-permute-start.8 = (bf16[256,1024]{1,0:T(8,128)(2,1)}, bf16[256,1024]{1,0:T(8,128)(2,1)S(1)}, u32[]{:S(2)}, u32[]{:S(2)}) collective-permute-start(bf16[256,1024]{1,0:T(8,128)(2,1)} %get-tuple-element.11), channel_id=1, source_target_pairs={{0,1},{1,0},{2,3},{3,2},{4,5},{5,4},{6,7},{7,6},{8,9},{9,8},{10,11... | collective-permute-start | bytes 1572872 | tf_op jit(solution)/shard_map/ppermute | solution.py:74
  122.6 15.8 %collective-permute-start.12 = (bf16[256,1024]{1,0:T(8,128)(2,1)}, bf16[256,1024]{1,0:T(8,128)(2,1)}, u32[]{:S(2)}, u32[]{:S(2)}) collective-permute-start(bf16[256,1024]{1,0:T(8,128)(2,1)} %get-tuple-element.15), channel_id=1, source_target_pairs={{0,2},{2,4},{4,6},{6,0},{1,3},{3,5},{5,7},{7,1},{8,10},{10,12},{12... | collective-permute-start | bytes 1572872 | tf_op jit(solution)/shard_map/ppermute | solution.py:74
  122.6 15.8 %collective-permute-start.15 = (bf16[256,1024]{1,0:T(8,128)(2,1)}, bf16[256,1024]{1,0:T(8,128)(2,1)}, u32[]{:S(2)}, u32[]{:S(2)}) collective-permute-start(bf16[256,1024]{1,0:T(8,128)(2,1)} %get-tuple-element.16), channel_id=1, source_target_pairs={{0,6},{2,0},{4,2},{6,4},{1,7},{3,1},{5,3},{7,5},{8,14},{10,8},{12,... | collective-permute-start | bytes 1572872 | tf_op jit(solution)/shard_map/ppermute | solution.py:74
  140.4 37.6 %copy-start.1 = (bf16[8192,128]{1,0:T(8,128)(2,1)S(1)}, bf16[8192,128]{1,0:T(8,128)(2,1)}, u32[]{:S(2)}) copy-start(bf16[8192,128]{1,0:T(8,128)(2,1)} %param.16) | copy-start | bytes 6291460
  142.9 6.2 %collective-permute-start.28 = (bf16[256,4,128]{2,0,1:T(8,128)(2,1)S(1)}, bf16[256,4,128]{2,0,1:T(8,128)(2,1)}, u32[]{:S(2)}, u32[]{:S(2)}) collective-permute-start(bf16[256,4,128]{2,0,1:T(8,128)(2,1)S(1)} %fusion.44), channel_id=1, source_target_pairs={{0,1},{1,0},{2,3},{3,2},{4,5},{5,4},{6,7},{7,6},{8,9},{9,8},{10,11... | collective-permute-start | bytes 786440 | tf_op jit(solution)/shard_map/ppermute | solution.py:74
  143.1 1.6 collective-permute-start.32
  144.7 8.8 %collective-permute-start.33 = (f32[256]{0:T(256)S(1)}, f32[256]{0:T(256)S(1)}, u32[]{:S(2)}, u32[]{:S(2)}) collective-permute-start(f32[256]{0:T(256)S(1)} %add.547), channel_id=1, source_target_pairs={{0,2},{2,4},{4,6},{6,0},{1,3},{3,5},{5,7},{7,1},{8,10},{10,12},{12... | collective-permute-start | bytes 3080 | tf_op jit(solution)/shard_map/ppermute | solution.py:74
  144.7 9.7 %collective-permute-start.34 = (f32[256]{0:T(256)S(1)}, f32[256]{0:T(256)S(1)}, u32[]{:S(2)}, u32[]{:S(2)}) collective-permute-start(f32[256]{0:T(256)S(1)} %add.547), channel_id=1, source_target_pairs={{0,4},{2,6},{4,0},{6,2},{1,5},{3,7},{5,1},{7,3},{8,12},{10,14},{12... | collective-permute-start | bytes 3080 | tf_op jit(solution)/shard_map/ppermute | solution.py:74
  149.1 5.3 %collective-permute-start.35 = (f32[256]{0:T(256)S(1)}, f32[256]{0:T(256)S(1)}, u32[]{:S(2)}, u32[]{:S(2)}) collective-permute-start(f32[256]{0:T(256)S(1)} %add.547), channel_id=1, source_target_pairs={{0,6},{2,0},{4,2},{6,4},{1,7},{3,1},{5,3},{7,5},{8,14},{10,8},{12,... | collective-permute-start | bytes 3080 | tf_op jit(solution)/shard_map/ppermute | solution.py:74
  150.2 5.5 %collective-permute-start.29 = (bf16[256,128]{1,0:T(8,128)(2,1)S(1)}, bf16[256,128]{1,0:T(8,128)(2,1)S(1)}, u32[]{:S(2)}, u32[]{:S(2)}) collective-permute-start(bf16[256,128]{1,0:T(8,128)(2,1)S(1)} %get-tuple-element.21), channel_id=1, source_target_pairs={{0,2},{2,4},{4,6},{6,0},{1,3},{3,5},{5,7},{7,1},{8,10},{10,12},{12... | collective-permute-start | bytes 196616 | tf_op jit(solution)/shard_map/ppermute | solution.py:74
  152.3 4.3 %collective-permute-start.30 = (bf16[256,128]{1,0:T(8,128)(2,1)S(1)}, bf16[256,128]{1,0:T(8,128)(2,1)S(1)}, u32[]{:S(2)}, u32[]{:S(2)}) collective-permute-start(bf16[256,128]{1,0:T(8,128)(2,1)S(1)} %get-tuple-element.23), channel_id=1, source_target_pairs={{0,6},{2,0},{4,2},{6,4},{1,7},{3,1},{5,3},{7,5},{8,14},{10,8},{12,... | collective-permute-start | bytes 196616 | tf_op jit(solution)/shard_map/ppermute | solution.py:74
  153.5 5.8 %collective-permute-start.31 = (bf16[256,128]{1,0:T(8,128)(2,1)S(1)}, bf16[256,128]{1,0:T(8,128)(2,1)S(1)}, u32[]{:S(2)}, u32[]{:S(2)}) collective-permute-start(bf16[256,128]{1,0:T(8,128)(2,1)S(1)} %get-tuple-element.22), channel_id=1, source_target_pairs={{0,4},{2,6},{4,0},{6,2},{1,5},{3,7},{5,1},{7,3},{8,12},{10,14},{12... | collective-permute-start | bytes 196616 | tf_op jit(solution)/shard_map/ppermute | solution.py:74
  159.6 5.6 %collective-permute-start.36 = (bf16[4,40,128]{2,1,0:T(8,128)(2,1)S(1)}, bf16[4,40,128]{2,1,0:T(8,128)(2,1)S(1)}, u32[]{:S(2)}, u32[]{:S(2)}) collective-permute-start(bf16[4,40,128]{2,1,0:T(8,128)(2,1)S(1)} %get-tuple-element.29), channel_id=1, source_target_pairs={{0,32},{32,64},{64,96},{96,0},{1,33},{33,65},{65,97},{97,1},{2,34}... | collective-permute-start | bytes 122888 | tf_op jit(solution)/shard_map/ppermute | solution.py:74
  159.7 5.5 %collective-permute-start.37 = (bf16[4,40,128]{2,1,0:T(8,128)(2,1)S(1)}, bf16[4,40,128]{2,1,0:T(8,128)(2,1)S(1)}, u32[]{:S(2)}, u32[]{:S(2)}) collective-permute-start(bf16[4,40,128]{2,1,0:T(8,128)(2,1)S(1)} %get-tuple-element.28), channel_id=1, source_target_pairs={{0,96},{32,0},{64,32},{96,64},{1,97},{33,1},{65,33},{97,65},{2,98}... | collective-permute-start | bytes 122888 | tf_op jit(solution)/shard_map/ppermute | solution.py:74
  162.9 5.5 %collective-permute-start.38 = (bf16[4,40,128]{2,1,0:T(8,128)(2,1)S(1)}, bf16[4,40,128]{2,1,0:T(8,128)(2,1)S(1)}, u32[]{:S(2)}, u32[]{:S(2)}) collective-permute-start(bf16[4,40,128]{2,1,0:T(8,128)(2,1)S(1)} %get-tuple-element.27), channel_id=1, source_target_pairs={{0,64},{32,96},{64,0},{96,32},{1,65},{33,97},{65,1},{97,33},{2,66}... | collective-permute-start | bytes 122888 | tf_op jit(solution)/shard_map/ppermute | solution.py:74
  168.5 5.3 %collective-permute-start.39 = (bf16[4,40,128]{2,1,0:T(8,128)(2,1)S(1)}, bf16[4,40,128]{2,1,0:T(8,128)(2,1)S(1)}, u32[]{:S(2)}, u32[]{:S(2)}) collective-permute-start(bf16[4,40,128]{2,1,0:T(8,128)(2,1)S(1)} %get-tuple-element.26), channel_id=1, source_target_pairs={{0,8},{8,16},{16,24},{24,0},{1,9},{9,17},{17,25},{25,1},{2,10},{10... | collective-permute-start | bytes 122888 | tf_op jit(solution)/shard_map/ppermute | solution.py:74
  168.6 5.2 %collective-permute-start.40 = (bf16[4,40,128]{2,1,0:T(8,128)(2,1)S(1)}, bf16[4,40,128]{2,1,0:T(8,128)(2,1)S(1)}, u32[]{:S(2)}, u32[]{:S(2)}) collective-permute-start(bf16[4,40,128]{2,1,0:T(8,128)(2,1)S(1)} %get-tuple-element.25), channel_id=1, source_target_pairs={{0,24},{8,0},{16,8},{24,16},{1,25},{9,1},{17,9},{25,17},{2,26},{10... | collective-permute-start | bytes 122888 | tf_op jit(solution)/shard_map/ppermute | solution.py:74
  171.8 5.5 %collective-permute-start.41 = (bf16[4,40,128]{2,1,0:T(8,128)(2,1)S(1)}, bf16[4,40,128]{2,1,0:T(8,128)(2,1)S(1)}, u32[]{:S(2)}, u32[]{:S(2)}) collective-permute-start(bf16[4,40,128]{2,1,0:T(8,128)(2,1)S(1)} %get-tuple-element.24), channel_id=1, source_target_pairs={{0,16},{8,24},{16,0},{24,8},{1,17},{9,25},{17,1},{25,9},{2,18},{10... | collective-permute-start | bytes 122888 | tf_op jit(solution)/shard_map/ppermute | solution.py:74
  (3 other events, 7.0 us)

commit v3 on v1

v3 whole, which is shorter than its diff:
```python
import functools

import jax
import jax.numpy as jnp
from jax import lax
from jax.experimental import pallas as pl
from jax.experimental.pallas import tpu as pltpu
from jax.sharding import Mesh, PartitionSpec as P

HEAD_DIM = 128
SESS = 16
CACHE = 320
CAPS = 2
GQA = 4
MOST = 20
ROOM = 32
KEYS = 384

EPSILON = 1e-06

VMEM = pl.BlockSpec(memory_space=pltpu.VMEM)
SMEM = pl.BlockSpec(memory_space=pltpu.SMEM)
ANY = pl.BlockSpec(memory_space=pl.ANY)


def call(kernel, name, outs, in_specs, scratch=(), limit=8, flops=0, nbytes=0):
    shapes = [jax.ShapeDtypeStruct(shape, dtype) for shape, dtype in outs]
    return pl.pallas_call(
        kernel,
        name=name,
        out_shape=shapes,
        in_specs=in_specs,
        out_specs=[VMEM] * len(shapes),
        scratch_shapes=list(scratch),
        compiler_params=pltpu.CompilerParams(vmem_limit_bytes=limit << 20),
        cost_estimate=pl.CostEstimate(flops=flops, bytes_accessed=nbytes, transcendentals=0),
    )


def shift(values, axis, step):
    size = lax.axis_size(axis)
    return lax.ppermute(values, axis, [(i, (i + step) % size) for i in range(size)])


def after(values, *others):
    return lax.optimization_barrier((values,) + others)[0]


def tables(session_row, owner_row):
    session_range = jnp.arange(SESS, dtype=jnp.int32)
    member = (session_row[:, None] == session_range[None, :]).astype(jnp.int32)
    counts = jnp.sum(member, axis=0)
    before = (session_row[None, :] < session_range[:, None]).astype(jnp.int32)
    starts = jnp.sum(before, axis=1)
    first_row = jnp.sum(member * starts[None, :], axis=1)
    position = jnp.arange(session_row.shape[0], dtype=jnp.int32) - first_row
    earlier = (owner_row[:, None] == owner_row[None, :]) & (
        session_range[None, :] < session_range[:, None]
    )
    owner_rank = jnp.sum(earlier.astype(jnp.int32), axis=1)
    owner_slot = owner_row * CAPS + owner_rank
    destination = jnp.sum(member * owner_slot[None, :], axis=1) * MOST + position
    return counts, session_row * ROOM + position, destination


def attention_kernel(
    spots, live, x0, t0, xl, tl, xr, tr, f1, f2, e1, e2, gain, wq, wk, wv, ck, cv, place,
    place_t, out, mine, xs, acc, slots, kk, vv, mixed, row_sem, cache_sem,
):
    half = f1.shape[0]
    copies = []
    for i, (ref, spot, extra) in enumerate(
        (
            (x0, 0, 0), (t0, 1, 0), (xl, 2, 0), (tl, 3, 0), (xr, 4, 0), (tr, 5, 0),
            (f1, 6, 0), (e1, 7, 0), (f2, 6, half), (e2, 7, half),
        )
    ):
        start = pl.multiple_of(spots[spot] + extra, 16)
        copies.append(
            pltpu.make_async_copy(ref, xs.at[pl.ds(start, ref.shape[0])], row_sem.at[i])
        )
    copies.append(pltpu.make_async_copy(ck, kk.at[:, pl.ds(0, CACHE)], cache_sem.at[0]))
    copies.append(pltpu.make_async_copy(cv, vv.at[:, pl.ds(0, CACHE)], cache_sem.at[1]))
    for copy in copies:
        copy.start()
    kk[:, CACHE + ROOM :, :] = jnp.zeros((SESS, KEYS - CACHE - ROOM, HEAD_DIM), jnp.bfloat16)
    vv[:, CACHE + ROOM :, :] = jnp.zeros((SESS, KEYS - CACHE - ROOM, HEAD_DIM), jnp.bfloat16)
    for copy in copies[:-2]:
        copy.wait()

    rows, width = xs.shape
    step = 512

    def square(i, total):
        x = xs[:, pl.ds(pl.multiple_of(i * step, step), step)].astype(jnp.float32)
        x = x * x
        for j in range(0, step, 128):
            total = total + x[:, j : j + 128]
        return total

    total = lax.fori_loop(0, width // step, square, jnp.zeros((rows, 128), jnp.float32))
    scale = lax.rsqrt(jnp.sum(total, axis=1, keepdims=True) / width + EPSILON)
    acc[...] = jnp.zeros_like(acc)
    heads = wq.shape[1]
    depth = 1024

    @pl.loop(0, width // depth)
    def _(i):
        part = pl.ds(pl.multiple_of(i * depth, depth), depth)
        x = xs[:, part].astype(jnp.float32) * scale * gain[:, part].astype(jnp.float32)
        x = x.astype(jnp.bfloat16)
        acc[:, :heads] += jnp.dot(x, wq[part, :], preferred_element_type=jnp.float32)
        acc[:, heads : heads + 128] += jnp.dot(
            x, wk[part, :], preferred_element_type=jnp.float32
        )
        acc[:, heads + 128 :] += jnp.dot(x, wv[part, :], preferred_element_type=jnp.float32)

    share = mine.shape[1]
    mine[...] = xs[:, pl.ds(pl.multiple_of(spots[8], share), share)]
    slots[...] = jnp.dot(
        place[...], acc[...].astype(jnp.bfloat16), preferred_element_type=jnp.float32
    ).astype(jnp.bfloat16)
    for copy in copies[-2:]:
        copy.wait()
    column = lax.broadcasted_iota(jnp.int32, (GQA * ROOM, KEYS), 1)
    place_in = lax.rem(lax.broadcasted_iota(jnp.int32, (GQA * ROOM, KEYS), 0), ROOM)
    fresh = column - CACHE
    allowed = (fresh >= 0) & (fresh <= place_in)
    fresh = jnp.where(allowed, fresh, KEYS)

    @pl.loop(0, SESS // 4)
    def _(group):
        for inner in range(4):
            s = group * 4 + inner
            at = pl.ds(pl.multiple_of(s * ROOM, ROOM), ROOM)
            kk[s, CACHE : CACHE + ROOM, :] = slots[at, heads : heads + 128]
            vv[s, CACHE : CACHE + ROOM, :] = slots[at, heads + 128 :]
            q = jnp.concatenate(
                [slots[at, h * HEAD_DIM : (h + 1) * HEAD_DIM] for h in range(GQA)], axis=0
            )
            scores = lax.dot_general(
                q, kk[s], (((1,), (1,)), ((), ())), preferred_element_type=jnp.float32
            ) * (HEAD_DIM ** (-0.5))
            keep = (column < live[0, s]) | (fresh < live[1, s])
            scores = jnp.where(keep, scores, -1e30)
            weights = jnp.exp(scores - jnp.max(scores, axis=1, keepdims=True))
            weights = weights / jnp.sum(weights, axis=1, keepdims=True)
            got = jnp.dot(
                weights.astype(jnp.bfloat16), vv[s], preferred_element_type=jnp.float32
            ).astype(jnp.bfloat16)
            for h in range(GQA):
                mixed[at, h * HEAD_DIM : (h + 1) * HEAD_DIM] = got[h * ROOM : (h + 1) * ROOM]

    out[...] = jnp.dot(place_t[...], mixed[...], preferred_element_type=jnp.float32).astype(
        jnp.bfloat16
    )


def block(values, weights, spot, width):
    return jnp.dot(
        values, weights[:, pl.ds(pl.multiple_of(spot, width), width)],
        preferred_element_type=jnp.float32,
    ).astype(jnp.bfloat16)


def far_kernel(spots, rows, w_out, send, keep):
    send[...] = block(rows[...], w_out, spots[0], send.shape[1])
    keep[...] = block(rows[...], w_out, spots[1], keep.shape[1])


def near_kernel(spots, rows, w_out, send, keep):
    @pl.loop(0, 3)
    def _(i):
        send[i] = block(rows[...], w_out, spots[2 + i], send.shape[2])
        keep[i] = block(rows[...], w_out, spots[5 + i], keep.shape[2])


def halves_kernel(keep, other, first, second):
    total = keep[...].astype(jnp.float32) + other[...].astype(jnp.float32)
    total = total.astype(jnp.bfloat16)
    half = first.shape[0]
    first[...] = total[:half]
    second[...] = total[half:]


def relay_kernel(keep, other, ahead, behind, to_next, to_last):
    half = ahead.shape[0]
    for i, ref, got, low in ((0, to_next, ahead, 0), (1, to_last, behind, half)):
        high = half - low
        first = keep[i].astype(jnp.float32) + other[i].astype(jnp.float32)
        ref[low : low + half] = (
            first[low : low + half] + got[...].astype(jnp.float32)
        ).astype(jnp.bfloat16)
        ref[high : high + half] = first[high : high + half].astype(jnp.bfloat16)


def split3(values):
    high = values.astype(jnp.bfloat16).astype(jnp.float32)
    rest = values - high
    middle = rest.astype(jnp.bfloat16).astype(jnp.float32)
    return high, middle, rest - middle


def talker_kernel(
    spots, mine, keep, other, from_last, from_next, gain, s0, sl, sr, g1, g2, send, kept,
    squares, wt, sem,
):
    piece = wt.shape[0] // 16
    copies = []
    for ref, source, first, number in ((s0, 0, 0, 4), (sl, 1, 0, 4), (sr, 2, 0, 4), (g1, 3, 0, 2), (g2, 3, 2, 2)):
        for j in range(number):
            start = pl.multiple_of(spots[8 + source * 4 + first + j], piece)
            copies.append(
                pltpu.make_async_copy(
                    ref.at[pl.ds(j * piece, piece)], wt.at[pl.ds(start, piece)], sem.at[len(copies)]
                )
            )
    for copy in copies:
        copy.start()
    total = (
        mine[...].astype(jnp.float32)
        + keep[2].astype(jnp.float32)
        + other[2].astype(jnp.float32)
        + from_last[...].astype(jnp.float32)
        + from_next[...].astype(jnp.float32)
    )
    hidden = total.astype(jnp.bfloat16).astype(jnp.float32)
    square = jnp.zeros((hidden.shape[0], 128), jnp.float32)
    for j in range(0, hidden.shape[1], 128):
        square = square + hidden[:, j : j + 128] * hidden[:, j : j + 128]
    row = jnp.sum(jnp.transpose(square), axis=0, keepdims=True)
    squares[...] = jnp.broadcast_to(row, squares.shape)
    share = hidden.shape[1]
    scaled = (hidden * gain[...].astype(jnp.float32)).astype(jnp.bfloat16)
    for copy in copies:
        copy.wait()
    rows, width = kept.shape
    kept[...] = jnp.dot(
        scaled, wt[:, pl.ds(pl.multiple_of(spots[24], width), width)],
        preferred_element_type=jnp.float32,
    )
    send[:rows] = jnp.dot(
        scaled, wt[:, pl.ds(pl.multiple_of(spots[25], width), width)],
        preferred_element_type=jnp.float32,
    ).astype(jnp.bfloat16)
    parts = jnp.concatenate(list(split3(row)) + [jnp.zeros((13, rows), jnp.float32)], axis=0)
    parts = jnp.concatenate([parts, jnp.zeros((16, width - rows), jnp.float32)], axis=1)
    send[rows:] = parts.astype(jnp.bfloat16)


def across_kernel(spots, kept, squares, got, own, squares_out, s1, s3, s2):
    rows = kept.shape[0]
    width = own.shape[1]
    tail = got[rows:, :rows].astype(jnp.float32)
    row = squares[0:1] + (tail[0:1] + tail[1:2] + tail[2:3])
    squares_out[...] = jnp.broadcast_to(row, squares_out.shape)
    pieces = []
    for part in split3(row):
        pieces += [part[:, j : j + 128] for j in range(0, rows, 128)]
    tail = jnp.concatenate(
        pieces + [jnp.zeros((16 - len(pieces), 128), jnp.float32)], axis=0
    ).astype(jnp.bfloat16)
    for i, ref in enumerate((own, s1, s3, s2)):
        at = pl.ds(pl.multiple_of(spots[26 + i], width), width)
        total = kept[:, at] + got[:rows, at].astype(jnp.float32)
        ref[:rows] = total.astype(ref.dtype)
        if i > 0:
            ref[rows:] = tail


def route_kernel(own, squares, g1, g3, g2, routing, out, *, features):
    rows = own.shape[0]
    total = own[...]
    row = squares[0:1]
    for ref in (g1, g3, g2):
        total = total + ref[:rows].astype(jnp.float32)
        tail = ref[rows:].astype(jnp.float32)
        row = row + jnp.concatenate(
            [tail[j : j + 1] + tail[2 + j : 3 + j] + tail[4 + j : 5 + j] for j in range(2)], axis=1
        )
    scale = lax.rsqrt(row / features + EPSILON)
    scale = jnp.transpose(jnp.broadcast_to(scale, (128, rows)))
    values = (total * scale).astype(jnp.bfloat16)
    out[...] = jnp.dot(routing[...], values, preferred_element_type=jnp.float32).astype(
        jnp.bfloat16
    )


def talker_strip(w_talker):
    y, core = lax.axis_index("y"), lax.axis_index("core")
    group = lax.axis_index("x") * 4 + lax.axis_index("z")
    width = w_talker.shape[1]
    piece = w_talker.shape[0] // 128
    mine = lax.dynamic_index_in_dim(
        w_talker.reshape(4, 2, 16, piece, width), group, 2, keepdims=False
    )
    kept = lax.dynamic_index_in_dim(mine, core, 1, keepdims=False)
    twin = shift(lax.dynamic_index_in_dim(mine, 1 - core, 1, keepdims=False), "core", 1)
    both = jnp.where(core == 0, jnp.stack([kept, twin], 1), jnp.stack([twin, kept], 1))
    across = jnp.zeros((4, 2, piece, width), w_talker.dtype)
    for d in (0, 1, 3, 2):
        part = lax.dynamic_index_in_dim(both, (y + d) % 4, 0, keepdims=False)
        part = part if d == 0 else shift(part, "y", d)
        across = lax.dynamic_update_index_in_dim(across, part, (y - d) % 4, 0)
    return jnp.transpose(across, (2, 1, 0, 3)).reshape(piece, 8 * width)


def on_device(
    thinker_rows,
    norm_gain,
    w_query,
    w_key,
    w_value,
    w_out,
    cache_keys,
    cache_values,
    session_ids,
    cache_lens,
    owners,
    talker_gain,
    w_talker,
):
    local, features = thinker_rows.shape
    bf16, f32 = jnp.bfloat16, jnp.float32
    tokens = local * 8
    share = features // 8
    width = w_talker.shape[1]
    heads = w_query.shape[1]
    x, z = lax.axis_index("x"), lax.axis_index("z")
    y, core = lax.axis_index("y"), lax.axis_index("core")
    member = y * 2 + core
    near = [y, (y + 3) % 4, (y + 1) % 4, (y + 2) % 4]
    counts, slot, destination = tables(session_ids[0], owners[:, 0])
    place_t = (slot[:, None] == jnp.arange(SESS * ROOM, dtype=jnp.int32)[None, :]).astype(bf16)
    place = (slot[None, :] == jnp.arange(SESS * ROOM, dtype=jnp.int32)[:, None]).astype(bf16)
    routing = (
        destination[None, :] == jnp.arange(16 * CAPS * MOST, dtype=jnp.int32)[:, None]
    ).astype(bf16)
    live = jnp.stack([cache_lens[0], counts])
    row_spots = []
    for chip in near:
        row_spots += [(chip * 2 + core) * local, (chip * 2 + 1 - core) * local]
    row_spots = jnp.stack(row_spots + [member * share]).astype(jnp.int32)
    order = [(y + 2) % 4, (y + 1) % 4, (y + 3) % 4, y]
    sends = [(chip * 2 + 1 - core) * share for chip in order]
    keeps = [(chip * 2 + core) * share for chip in order]
    column_spots = jnp.stack([sends[0], keeps[0]] + sends[1:] + keeps[1:])
    nearx = [x, (x + 3) % 4, (x + 1) % 4, (x + 2) % 4]
    nearz = [z, (z + 3) % 4, (z + 1) % 4, (z + 2) % 4]
    piece = share // 16
    row_of = [(cx * 4 + cz) * piece for cx in nearx for cz in nearz]
    rest = [core * 4 * width, (1 - core) * 4 * width]
    rest += [((y + d) % 4) * width for d in (0, 1, 3, 2)]
    spots = jnp.concatenate([column_spots, jnp.stack(row_of + rest)]).astype(jnp.int32)
    gain = lax.dynamic_slice(talker_gain, (member * share,), (share,))[None, :]

    half = local // 2
    left, right = shift(thinker_rows, "y", 1), shift(thinker_rows, "y", -1)
    twin = shift(thinker_rows, "core", 1)
    strip = talker_strip(w_talker)
    low, high = left[:half], right[half:]
    far_low, far_high = shift(low, "y", 1), shift(high, "y", -1)
    twin_left, twin_right = shift(left, "core", 1), shift(right, "core", 1)
    twin_low, twin_high = shift(far_low, "core", 1), shift(far_high, "core", 1)
    strip = after(strip, left, right)
    strips = [strip] + [shift(strip, "z", d) for d in (1, 3, 2)]

    rows, mine = call(
        attention_kernel,
        "attention",
        [((tokens, heads), bf16), ((tokens, share), bf16)],
        [SMEM, SMEM] + [ANY] * 10 + [VMEM] * 4 + [ANY] * 2 + [VMEM] * 2,
        [
            pltpu.VMEM((tokens, features), bf16),
            pltpu.VMEM((tokens, heads + 256), f32),
            pltpu.VMEM((SESS * ROOM, heads + 256), bf16),
            pltpu.VMEM((SESS, KEYS, HEAD_DIM), bf16),
            pltpu.VMEM((SESS, KEYS, HEAD_DIM), bf16),
            pltpu.VMEM((SESS * ROOM, heads), bf16),
            pltpu.SemaphoreType.DMA((10,)),
            pltpu.SemaphoreType.DMA((2,)),
        ],
        limit=20,
        flops=4 * 10**9,
        nbytes=20 * 10**6,
    )(
        row_spots, live, thinker_rows, twin, left, twin_left, right, twin_right, far_low,
        far_high, twin_low, twin_high, norm_gain[None, :], w_query, w_key, w_value, cache_keys,
        cache_values, place, place_t,
    )
    block_type = ((tokens, share), bf16)
    send_far, keep_far = call(
        far_kernel, "out_far", [block_type] * 2, [SMEM, VMEM, VMEM], flops=5 * 10**8, nbytes=4 * 10**6
    )(spots, rows, w_out)
    other_far = shift(send_far, "core", 1)
    send, keep = call(
        near_kernel, "out_near", [((3, tokens, share), bf16)] * 2, [SMEM, VMEM, VMEM],
        flops=15 * 10**8, nbytes=8 * 10**6,
    )(spots, rows, w_out)
    first, second = call(
        halves_kernel, "halves", [((tokens // 2, share), bf16)] * 2, [VMEM] * 2,
        flops=10**6, nbytes=2 * 10**6,
    )(keep_far, other_far)
    ahead, behind = shift(first, "y", 1), shift(second, "y", -1)
    other = shift(send, "core", 1)
    strip = after(jnp.concatenate(strips, 0), first)
    strip_left, strip_right = shift(strip, "x", 1), shift(strip, "x", -1)
    to_next, to_last = call(
        relay_kernel, "relay", [block_type] * 2, [VMEM] * 4, flops=10**6, nbytes=4 * 10**6
    )(keep, other, ahead, behind)
    from_last, from_next = shift(to_next, "y", 1), shift(to_last, "y", -1)
    strip_half = strip.shape[0] // 2
    strip_low = shift(after(strip_left[:strip_half], to_next), "x", 1)
    strip_high = shift(after(strip_right[strip_half:], to_next), "x", -1)
    sent, kept, squares = call(
        talker_kernel,
        "talker",
        [((tokens + 16, 4 * width), bf16), ((tokens, 4 * width), f32), ((8, tokens), f32)],
        [SMEM] + [VMEM] * 6 + [ANY] * 5,
        [pltpu.VMEM((share, 8 * width), bf16), pltpu.SemaphoreType.DMA((16,))],
        flops=6 * 10**8,
        nbytes=4 * 10**6,
    )(
        spots, mine, keep, other, from_last, from_next, gain, strip, strip_left, strip_right,
        strip_low, strip_high,
    )
    got = shift(sent, "core", 1)
    tall = ((tokens + 16, width), bf16)
    own, squares, s1, s3, s2 = call(
        across_kernel, "across", [((tokens, width), f32), ((8, tokens), f32), tall, tall, tall],
        [SMEM] + [VMEM] * 3, flops=10**6, nbytes=10**6,
    )(spots, kept, squares, got)
    g2 = shift(s2, "y", 2)
    g1, g3 = shift(s1, "y", 1), shift(s3, "y", 3)
    (outgoing,) = call(
        functools.partial(route_kernel, features=features), "route",
        [((16 * CAPS * MOST, width), bf16)], [VMEM] * 6, flops=4 * 10**7, nbytes=10**6,
    )(own, squares, g1, g3, g2, routing)
    arrived = lax.all_to_all(
        outgoing.reshape(16, CAPS * MOST, width), ("x", "z"), split_axis=0, concat_axis=0, tiled=True
    )
    return arrived.reshape(16 * CAPS * MOST, width)


def solution(mesh):
    grp, tp = ("x", "z"), ("y", "core")
    return jax.shard_map(
        on_device,
        mesh=Mesh(mesh.devices.reshape(4, 4, 4, 2), grp + tp),
        in_specs=(
            P(grp + tp, None),
            P(),
            P(None, tp),
            P(None, tp),
            P(None, tp),
            P(tp, None),
            P(grp, None, tp),
            P(grp, None, tp),
            P(grp, None),
            P(grp, None),
            P(grp, None),
            P(),
            P(None, tp),
        ),
        out_specs=P(grp, tp),
        check_vma=False,
    )
```

time: 178 us -> 154 us (0.87)
  waiting for transfers between devices: 100 us -> 38.5 us
  starting transfers between devices: 0.08 us -> 34.8 us
  matrix products: 32.8 us -> 0 us
  local copies, waits for them, and re-layouts: 1.02 us -> 31.3 us
  Pallas kernels: 0 us -> 30.2 us
  between operations: 13.3 us -> 0.43 us
  other arithmetic: 15.1 us -> 6.53 us
  blocking collectives: 14.8 us -> 11 us
    all_gather x2 -> x0, waiting for transfers between devices: 61.7 us -> none  [the longest x1 31.1 us: on_device(): hidden = lax.all_gather(hidden_local, 'tp', axis=0, tiled=True)]
    ppermute x0 -> x30, waiting for transfers between devices: none -> 38.5 us  [shift(): lax.ppermute(values, axis, [(i, (i + step) % size) for i in range(size)])]
    reduce_scatter x1 -> x0, waiting for transfers between devices: 37.9 us -> none  [on_device(): lax.psum_scatter(head_total.astype(jnp.bfloat16), 'tp', scatter_dimension...]
    ppermute x0 -> x30, starting transfers between devices: none -> 34.8 us  [shift(): lax.ppermute(values, axis, [(i, (i + step) % size) for i in range(size)])]
    dot_general x9 -> x0, matrix products: 32.8 us -> none  [the longest x1 7.93 us: on_device(): jnp.dot(attention_rows, w_out, preferred_element_type=jnp.float32)]
    pallas_call x0 -> x8, Pallas kernels: none -> 30.2 us  [the longest x1 16.4 us: on_device(): call(attention_kernel, 'attention', [((tokens, heads), bf16), ((tokens, s...]
    unnamed x9 -> x43, local copies, waits for them, and re-layouts: 0.68 us -> 20.1 us
    reduce_sum x7 -> x3, other arithmetic: 9.88 us -> 2.58 us  [the longest x1 0.91 us: tables(): owner_rank = jnp.sum(earlier.astype(jnp.int32), axis=1)]
  transfers between devices with their start and end apart: 3 -> 30, of which waited for: 3 -> 13; matrix products, arithmetic and copies ran while one was open for 3% -> 12% of each run, Pallas kernels for 0% -> 3%
where the time goes in v3:
time: 154 us; the launch traced here: 153 us
  waiting for transfers between devices  38.5 us (25%)
  starting transfers between devices  34.8 us (23%)
  local copies, waits for them, and re-layouts  31.3 us (20%)
  Pallas kernels  30.2 us (20%)
  blocking collectives  11 us (7%)
  other arithmetic  6.53 us (4%)
    ppermute x30, waiting for transfers between devices, shift(): lax.ppermute(values, axis, [(i, (i + step) % size) for i in range(size)])  38.5 us
    ppermute x30, starting transfers between devices, shift(): lax.ppermute(values, axis, [(i, (i + step) % size) for i in range(size)])  34.8 us
    unnamed x43, local copies, waits for them, and re-layouts  20.1 us
    pallas_call x1, Pallas kernels, on_device(): call(attention_kernel, 'attention', [((tokens, heads), bf16), ((tokens, s...  16.4 us
    all_to_all x1, blocking collectives, on_device(): lax.all_to_all(outgoing.reshape(16, CAPS * MOST, width), ('x', 'z'), spli...  11 us
    dynamic_update_slice x4, local copies, waits for them, and re-layouts, talker_strip(): across = lax.dynamic_update_index_in_dim(across, part, (y - d) % 4, 0)  5.44 us
    pallas_call x1, Pallas kernels, on_device(): call(talker_kernel, 'talker', [((tokens + 16, 4 * width), bf16), ((tokens...  5.1 us
    pallas_call x1, Pallas kernels, on_device(): call(near_kernel, 'out_near', [((3, tokens, share), bf16)] * 2, [SMEM, VM...  3.61 us
  transfers between devices with their start and end apart: 30, of which 13 were waited for; matrix products, arithmetic and copies ran while one was open for 12% of the time, Pallas kernels for 3%

profile of v3, /device:TPU:0, one launch (start us, length us, event | category | flops | bytes accessed | tf_op | source)
XLA Modules:
  0.0 152.7 jit_solution(9414351495196654489)
XLA Ops:
  0.0 1.7 %collective-permute-start.1 = (bf16[32,8192]{1,0:T(8,128)(2,1)}, bf16[32,8192]{1,0:T(8,128)(2,1)S(1)}, u32[]{:S(2)}, u32[]{:S(2)}) collective-permute-start(bf16[32,8192]{1,0:T(8,128)(2,1)} %x0.1), channel_id=1, source_target_pairs={{0,2},{2,4},{4,6},{6,0},{1,3},{3,5},{5,7},{7,1},{8,10},{10,12},{12... | collective-permute-start | bytes 1572872 | tf_op jit(solution)/shard_map/ppermute | solution.py:42
  1.7 1.5 %collective-permute-start.3 = (bf16[32,8192]{1,0:T(8,128)(2,1)}, bf16[32,8192]{1,0:T(8,128)(2,1)S(1)}, u32[]{:S(2)}, u32[]{:S(2)}) collective-permute-start(bf16[32,8192]{1,0:T(8,128)(2,1)} %x0.1), channel_id=1, source_target_pairs={{0,6},{2,0},{4,2},{6,4},{1,7},{3,1},{5,3},{7,5},{8,14},{10,8},{12,... | collective-permute-start | bytes 1572872 | tf_op jit(solution)/shard_map/ppermute | solution.py:42
  7.2 8.2 %collective-permute-done.1.xl = bf16[32,8192]{1,0:T(8,128)(2,1)S(1)} collective-permute-done((bf16[32,8192]{1,0:T(8,128)(2,1)}, bf16[32,8192]{1,0:T(8,128)(2,1)S(1)}, u32[]{:S(2)}, u32[]{:S(2)}) %collective-permute-start.1) | collective-permute-done | bytes 524320 | tf_op jit(solution)/shard_map/ppermute | solution.py:42
  15.7 3.1 %collective-permute-start.6 = (bf16[16,8192]{1,0:T(8,128)(2,1)S(1)}, bf16[16,8192]{1,0:T(8,128)(2,1)}, u32[]{:S(2)}, u32[]{:S(2)}) collective-permute-start(bf16[16,8192]{1,0:T(8,128)(2,1)S(1)} %slice.17), channel_id=1, source_target_pairs={{0,6},{2,0},{4,2},{6,4},{1,7},{3,1},{5,3},{7,5},{8,14},{10,8},{12,... | collective-permute-start | bytes 786440 | tf_op jit(solution)/shard_map/ppermute | solution.py:42
  20.1 3.9 %collective-permute-done.5.f1 = bf16[16,8192]{1,0:T(8,128)(2,1)S(1)} collective-permute-done((bf16[16,8192]{1,0:T(8,128)(2,1)S(1)}, bf16[16,8192]{1,0:T(8,128)(2,1)S(1)}, u32[]{:S(2)}, u32[]{:S(2)}) %collective-permute-start.5) | collective-permute-done | bytes 262176 | tf_op jit(solution)/shard_map/ppermute | solution.py:42
  26.4 3.5 %copy-done.1 = bf16[8192,512]{1,0:T(8,128)(2,1)S(1)} copy-done((bf16[8192,512]{1,0:T(8,128)(2,1)S(1)}, bf16[8192,512]{1,0:T(8,128)(2,1)}, u32[]{:S(2)}) %copy-start.1) | copy-done | bytes 8388632
  30.0 2.3 %copy-done.2 = bf16[8192,128]{1,0:T(8,128)(2,1)S(1)} copy-done((bf16[8192,128]{1,0:T(8,128)(2,1)S(1)}, bf16[8192,128]{1,0:T(8,128)(2,1)}, u32[]{:S(2)}) %copy-start.2) | copy-done | bytes 2097176
  32.3 1.6 %copy-done.3 = bf16[8192,128]{1,0:T(8,128)(2,1)S(1)} copy-done((bf16[8192,128]{1,0:T(8,128)(2,1)S(1)}, bf16[8192,128]{1,0:T(8,128)(2,1)}, u32[]{:S(2)}) %copy-start.3) | copy-done | bytes 2097176
  33.9 1.3 copy-done.7
  35.2 0.9 copy-done.18
  36.2 16.4 %attention.1 = (bf16[256,512]{1,0:T(8,128)(2,1)S(1)}, bf16[256,1024]{1,0:T(8,128)(2,1)S(1)}) custom-call(s32[9]{0:T(128)S(1)} %stack.174.spots, s32[2,16]{1,0:T(2,128)S(1)} %pad_add_fusion.live, bf16[32,8192]{1,0:T(8,128)(2,1)S(1)} %copy-done.12, bf16[32,8192]{1,0:T(8,128)(2,1)} %collective-permute-done.t0, bf16[32,8192]{1,0:T(8,128)(2,1)S(1)} %collective-permute-done.1.xl, ...), custom_call_target="tpu_custom_call" | custom-call | flops 4000000000 | bytes 20000000 | tf_op jit(solution)/shard_map/attention/pallas_call | solution.py:368
  52.6 3.6 %out_near.1 = (bf16[3,256,1024]{2,1,0:T(8,128)(2,1)}, bf16[3,256,1024]{2,1,0:T(8,128)(2,1)S(1)}) custom-call(s32[30]{0:T(128)S(1)} %concatenate.6.spots, bf16[256,512]{1,0:T(8,128)(2,1)S(1)} %get-tuple-element.28.rows, bf16[512,8192]{1,0:T(8,128)(2,1)S(1)} %bitcast.67), custom_call_target="tpu_custom_call" | custom-call | flops 1500000000 | bytes 8000000 | tf_op jit(solution)/shard_map/out_near/pallas_call | solution.py:396
  56.3 1.5 dynamic-slice_bitcast_fusion.1
  58.2 3.4 %copy-done = bf16[512,8192]{1,0:T(8,128)(2,1)S(1)} copy-done((bf16[512,8192]{1,0:T(8,128)(2,1)S(1)}, bf16[512,8192]{1,0:T(8,128)(2,1)}, u32[]{:S(2)}) %copy-start) | copy-done | bytes 8388632
  61.6 1.8 %out_far.1 = (bf16[256,1024]{1,0:T(8,128)(2,1)}, bf16[256,1024]{1,0:T(8,128)(2,1)S(1)}) custom-call(s32[30]{0:T(128)S(1)} %concatenate.6.spots, bf16[256,512]{1,0:T(8,128)(2,1)S(1)} %get-tuple-element.28.rows, bf16[512,8192]{1,0:T(8,128)(2,1)S(1)} %copy-done), custom_call_target="tpu_custom_call" | custom-call | flops 500000000 | bytes 4000000 | tf_op jit(solution)/shard_map/out_far/pallas_call | solution.py:392
  66.1 3.0 %collective-permute-start.17 = (bf16[2,64,128]{2,1,0:T(8,128)(2,1)S(1)}, bf16[2,64,128]{2,1,0:T(8,128)(2,1)S(1)}, u32[]{:S(2)}, u32[]{:S(2)}) collective-permute-start(bf16[2,64,128]{2,1,0:T(8,128)(2,1)S(1)} %get-tuple-element.55), channel_id=1, source_target_pairs={{0,6},{2,0},{4,2},{6,4},{1,7},{3,1},{5,3},{7,5},{8,14},{10,8},{12,... | collective-permute-start | bytes 98312 | tf_op jit(solution)/shard_map/ppermute | solution.py:42
  69.1 1.3 collective-permute-start.18
  70.5 1.4 dynamic_update_slice.13
  72.0 2.5 %collective-permute-done.18 = bf16[2,64,128]{2,1,0:T(8,128)(2,1)S(1)} collective-permute-done((bf16[2,64,128]{2,1,0:T(8,128)(2,1)S(1)}, bf16[2,64,128]{2,1,0:T(8,128)(2,1)S(1)}, u32[]{:S(2)}, u32[]{:S(2)}) %collective-permute-start.18) | collective-permute-done | bytes 32800 | tf_op jit(solution)/shard_map/ppermute | solution.py:42
  74.6 1.4 dynamic_update_slice.14
  76.0 1.4 dynamic_update_slice.15
  77.3 1.4 dynamic_update_slice.16
  78.8 1.9 %collective-permute-start.19 = (bf16[64,1024]{1,0:T(8,128)(2,1)S(1)}, bf16[64,1024]{1,0:T(8,128)(2,1)S(1)}, u32[]{:S(2)}, u32[]{:S(2)}) collective-permute-start(bf16[64,1024]{1,0:T(8,128)(2,1)S(1)} %reshape.58), channel_id=1, source_target_pairs={{0,8},{8,16},{16,24},{24,0},{1,9},{9,17},{17,25},{25,1},{2,10},{10... | collective-permute-start | bytes 393224 | tf_op jit(solution)/shard_map/ppermute | solution.py:42
  80.7 2.4 %collective-permute-start.20 = (bf16[64,1024]{1,0:T(8,128)(2,1)S(1)}, bf16[64,1024]{1,0:T(8,128)(2,1)S(1)}, u32[]{:S(2)}, u32[]{:S(2)}) collective-permute-start(bf16[64,1024]{1,0:T(8,128)(2,1)S(1)} %reshape.58), channel_id=1, source_target_pairs={{0,24},{8,0},{16,8},{24,16},{1,25},{9,1},{17,9},{25,17},{2,26},{10... | collective-permute-start | bytes 393224 | tf_op jit(solution)/shard_map/ppermute | solution.py:42
  83.1 1.6 %collective-permute-start.21 = (bf16[64,1024]{1,0:T(8,128)(2,1)S(1)}, bf16[64,1024]{1,0:T(8,128)(2,1)S(1)}, u32[]{:S(2)}, u32[]{:S(2)}) collective-permute-start(bf16[64,1024]{1,0:T(8,128)(2,1)S(1)} %reshape.58), channel_id=1, source_target_pairs={{0,16},{8,24},{16,0},{24,8},{1,17},{9,25},{17,1},{25,9},{2,18},{10... | collective-permute-start | bytes 393224 | tf_op jit(solution)/shard_map/ppermute | solution.py:42
  84.7 1.4 collective-permute-done.19
  86.1 1.9 %collective-permute-done.20 = bf16[64,1024]{1,0:T(8,128)(2,1)S(1)} collective-permute-done((bf16[64,1024]{1,0:T(8,128)(2,1)S(1)}, bf16[64,1024]{1,0:T(8,128)(2,1)S(1)}, u32[]{:S(2)}, u32[]{:S(2)}) %collective-permute-start.20) | collective-permute-done | bytes 131104 | tf_op jit(solution)/shard_map/ppermute | solution.py:42
  88.0 1.8 %collective-permute-done.21 = bf16[64,1024]{1,0:T(8,128)(2,1)S(1)} collective-permute-done((bf16[64,1024]{1,0:T(8,128)(2,1)S(1)}, bf16[64,1024]{1,0:T(8,128)(2,1)S(1)}, u32[]{:S(2)}, u32[]{:S(2)}) %collective-permute-start.21) | collective-permute-done | bytes 131104 | tf_op jit(solution)/shard_map/ppermute | solution.py:42
  89.9 1.2 copy-done.16
  91.1 1.2 halves.1
  92.3 2.8 %collective-permute-start.23 = (bf16[256,1024]{1,0:T(8,128)(2,1)S(1)}, bf16[256,1024]{1,0:T(8,128)(2,1)S(1)}, u32[]{:S(2)}, u32[]{:S(2)}) collective-permute-start(bf16[256,1024]{1,0:T(8,128)(2,1)S(1)} %pad_maximum_fusion.s0), channel_id=1, source_target_pairs={{0,96},{32,0},{64,32},{96,64},{1,97},{33,1},{65,33},{97,65},{2,98}... | collective-permute-start | bytes 1572872 | tf_op jit(solution)/shard_map/ppermute | solution.py:42
  95.1 3.2 %collective-permute-start.12 = (bf16[128,1024]{1,0:T(8,128)(2,1)S(1)}, bf16[128,1024]{1,0:T(8,128)(2,1)S(1)}, u32[]{:S(2)}, u32[]{:S(2)}) collective-permute-start(bf16[128,1024]{1,0:T(8,128)(2,1)S(1)} %get-tuple-element.34), channel_id=1, source_target_pairs={{0,6},{2,0},{4,2},{6,4},{1,7},{3,1},{5,3},{7,5},{8,14},{10,8},{12,... | collective-permute-start | bytes 786440 | tf_op jit(solution)/shard_map/ppermute | solution.py:42
  98.3 4.3 %collective-permute-done.11.ahead = bf16[128,1024]{1,0:T(8,128)(2,1)S(1)} collective-permute-done((bf16[128,1024]{1,0:T(8,128)(2,1)S(1)}, bf16[128,1024]{1,0:T(8,128)(2,1)S(1)}, u32[]{:S(2)}, u32[]{:S(2)}) %collective-permute-start.11) | collective-permute-done | bytes 262176 | tf_op jit(solution)/shard_map/ppermute | solution.py:42
  102.7 1.1 relay.1
  103.8 3.2 %collective-permute-start.14 = (bf16[256,1024]{1,0:T(8,128)(2,1)}, bf16[256,1024]{1,0:T(8,128)(2,1)}, u32[]{:S(2)}, u32[]{:S(2)}) collective-permute-start(bf16[256,1024]{1,0:T(8,128)(2,1)} %get-tuple-element.36), channel_id=1, source_target_pairs={{0,6},{2,0},{4,2},{6,4},{1,7},{3,1},{5,3},{7,5},{8,14},{10,8},{12,... | collective-permute-start | bytes 1572872 | tf_op jit(solution)/shard_map/ppermute | solution.py:42
  109.0 3.1 %collective-permute-start.25 = (bf16[128,1024]{1,0:T(8,128)(2,1)}, bf16[128,1024]{1,0:T(8,128)(2,1)S(1)}, u32[]{:S(2)}, u32[]{:S(2)}) collective-permute-start(bf16[128,1024]{1,0:T(8,128)(2,1)} %slice.19), channel_id=1, source_target_pairs={{0,96},{32,0},{64,32},{96,64},{1,97},{33,1},{65,33},{97,65},{2,98}... | collective-permute-start | bytes 786440 | tf_op jit(solution)/shard_map/ppermute | solution.py:42
  112.8 3.5 %collective-permute-done.25.g2 = bf16[128,1024]{1,0:T(8,128)(2,1)S(1)} collective-permute-done((bf16[128,1024]{1,0:T(8,128)(2,1)}, bf16[128,1024]{1,0:T(8,128)(2,1)S(1)}, u32[]{:S(2)}, u32[]{:S(2)}) %collective-permute-start.25) | collective-permute-done | bytes 262176 | tf_op jit(solution)/shard_map/ppermute | solution.py:42
  116.3 3.7 %collective-permute-done.24.g1 = bf16[128,1024]{1,0:T(8,128)(2,1)} collective-permute-done((bf16[128,1024]{1,0:T(8,128)(2,1)}, bf16[128,1024]{1,0:T(8,128)(2,1)}, u32[]{:S(2)}, u32[]{:S(2)}) %collective-permute-start.24) | collective-permute-done | bytes 262176 | tf_op jit(solution)/shard_map/ppermute | solution.py:42
  120.0 1.0 copy-done.5
  121.0 1.0 copy-done.9
  122.1 1.0 copy-done.11
  123.1 1.0 copy-done.14
  124.2 5.1 %talker.1 = (bf16[272,512]{1,0:T(8,128)(2,1)S(1)}, f32[256,512]{1,0:T(8,128)S(1)}, f32[8,256]{1,0:T(8,128)S(1)}) custom-call(s32[30]{0:T(128)S(1)} %concatenate.6.spots, bf16[256,1024]{1,0:T(8,128)(2,1)S(1)} %copy-done.14, bf16[3,256,1024]{2,1,0:T(8,128)(2,1)S(1)} %get-tuple-element.29.keep, bf16[3,256,1024]{2,1,0:T(8,128)(2,1)S(1)} %collective-permute-done.9.other, ...), custom_call_target="tpu_custom_call" | custom-call | flops 600000000 | bytes 4000000 | tf_op jit(solution)/shard_map/talker/pallas_call | solution.py:415
  129.4 1.5 %collective-permute-done.26.got = bf16[272,512]{1,0:T(8,128)(2,1)S(1)} collective-permute-done((bf16[272,512]{1,0:T(8,128)(2,1)S(1)}, bf16[272,512]{1,0:T(8,128)(2,1)S(1)}, u32[]{:S(2)}, u32[]{:S(2)}) %collective-permute-start.26) | collective-permute-done | bytes 278560 | tf_op jit(solution)/shard_map/ppermute | solution.py:42
  131.7 3.2 %collective-permute-start.28 = (bf16[272,128]{1,0:T(8,128)(2,1)S(1)}, bf16[272,128]{1,0:T(8,128)(2,1)S(1)}, u32[]{:S(2)}, u32[]{:S(2)}) collective-permute-start(bf16[272,128]{1,0:T(8,128)(2,1)S(1)} %get-tuple-element.47), channel_id=1, source_target_pairs={{0,6},{2,0},{4,2},{6,4},{1,7},{3,1},{5,3},{7,5},{8,14},{10,8},{12,... | collective-permute-start | bytes 208904 | tf_op jit(solution)/shard_map/ppermute | solution.py:42
  135.2 1.9 %collective-permute-done.27.g1 = bf16[272,128]{1,0:T(8,128)(2,1)S(1)} collective-permute-done((bf16[272,128]{1,0:T(8,128)(2,1)S(1)}, bf16[272,128]{1,0:T(8,128)(2,1)S(1)}, u32[]{:S(2)}, u32[]{:S(2)}) %collective-permute-start.27) | collective-permute-done | bytes 69664 | tf_op jit(solution)/shard_map/ppermute | solution.py:42
  137.2 3.5 %collective-permute-done.29.g2 = bf16[272,128]{1,0:T(8,128)(2,1)S(1)} collective-permute-done((bf16[272,128]{1,0:T(8,128)(2,1)S(1)}, bf16[272,128]{1,0:T(8,128)(2,1)S(1)}, u32[]{:S(2)}, u32[]{:S(2)}) %collective-permute-start.29) | collective-permute-done | bytes 69664 | tf_op jit(solution)/shard_map/ppermute | solution.py:42
  141.0 11.0 %all_to_all.5 = bf16[16,40,128]{2,1,0:T(8,128)(2,1)S(1)} all-to-all(bf16[16,40,128]{2,1,0:T(8,128)(2,1)S(1)} %bitcast.68), channel_id=1, replica_groups=mesh['x'=4,'z'=4,'y'=4,'core'=2] {'x','z'}, dimensions={0} | all-to-all | bytes 327680 | tf_op jit(solution)/shard_map/all_to_all | solution.py:439
  (98 shorter events, 16.2 us)
Async XLA Ops:
  0.0 26.4 %copy-start.12 = (bf16[32,8192]{1,0:T(8,128)(2,1)S(1)}, bf16[32,8192]{1,0:T(8,128)(2,1)}, u32[]{:S(2)}) copy-start(bf16[32,8192]{1,0:T(8,128)(2,1)} %x0.1) | copy-start | bytes 1572868
  0.0 26.4 %copy-start.6 = (bf16[16,320,128]{2,1,0:T(8,128)(2,1)S(1)}, bf16[16,320,128]{2,1,0:T(8,128)(2,1)}, u32[]{:S(2)}) copy-start(bf16[16,320,128]{2,1,0:T(8,128)(2,1)} %ck.1) | copy-start | bytes 3932164
  0.0 15.3 %collective-permute-start.1 = (bf16[32,8192]{1,0:T(8,128)(2,1)}, bf16[32,8192]{1,0:T(8,128)(2,1)S(1)}, u32[]{:S(2)}, u32[]{:S(2)}) collective-permute-start(bf16[32,8192]{1,0:T(8,128)(2,1)} %x0.1), channel_id=1, source_target_pairs={{0,2},{2,4},{4,6},{6,0},{1,3},{3,5},{5,7},{7,1},{8,10},{10,12},{12... | collective-permute-start | bytes 1572872 | tf_op jit(solution)/shard_map/ppermute | solution.py:42
  1.7 14.0 %collective-permute-start.3 = (bf16[32,8192]{1,0:T(8,128)(2,1)}, bf16[32,8192]{1,0:T(8,128)(2,1)S(1)}, u32[]{:S(2)}, u32[]{:S(2)}) collective-permute-start(bf16[32,8192]{1,0:T(8,128)(2,1)} %x0.1), channel_id=1, source_target_pairs={{0,6},{2,0},{4,2},{6,4},{1,7},{3,1},{5,3},{7,5},{8,14},{10,8},{12,... | collective-permute-start | bytes 1572872 | tf_op jit(solution)/shard_map/ppermute | solution.py:42
  3.2 23.1 %collective-permute-start = (bf16[32,8192]{1,0:T(8,128)(2,1)}, bf16[32,8192]{1,0:T(8,128)(2,1)}, u32[]{:S(2)}, u32[]{:S(2)}) collective-permute-start(bf16[32,8192]{1,0:T(8,128)(2,1)} %x0.1), channel_id=1, source_target_pairs={{0,1},{1,0},{2,3},{3,2},{4,5},{5,4},{6,7},{7,6},{8,9},{9,8},{10,11... | collective-permute-start | bytes 1572872 | tf_op jit(solution)/shard_map/ppermute | solution.py:42
  15.4 8.7 %collective-permute-start.5 = (bf16[16,8192]{1,0:T(8,128)(2,1)S(1)}, bf16[16,8192]{1,0:T(8,128)(2,1)S(1)}, u32[]{:S(2)}, u32[]{:S(2)}) collective-permute-start(bf16[16,8192]{1,0:T(8,128)(2,1)S(1)} %slice.16), channel_id=1, source_target_pairs={{0,2},{2,4},{4,6},{6,0},{1,3},{3,5},{5,7},{7,1},{8,10},{10,12},{12... | collective-permute-start | bytes 786440 | tf_op jit(solution)/shard_map/ppermute | solution.py:42
  15.7 8.4 %collective-permute-start.6 = (bf16[16,8192]{1,0:T(8,128)(2,1)S(1)}, bf16[16,8192]{1,0:T(8,128)(2,1)}, u32[]{:S(2)}, u32[]{:S(2)}) collective-permute-start(bf16[16,8192]{1,0:T(8,128)(2,1)S(1)} %slice.17), channel_id=1, source_target_pairs={{0,6},{2,0},{4,2},{6,4},{1,7},{3,1},{5,3},{7,5},{8,14},{10,8},{12,... | collective-permute-start | bytes 786440 | tf_op jit(solution)/shard_map/ppermute | solution.py:42
  18.9 7.5 %collective-permute-start.2 = (bf16[32,8192]{1,0:T(8,128)(2,1)S(1)}, bf16[32,8192]{1,0:T(8,128)(2,1)}, u32[]{:S(2)}, u32[]{:S(2)}) collective-permute-start(bf16[32,8192]{1,0:T(8,128)(2,1)S(1)} %collective-permute-done.1.xl), channel_id=1, source_target_pairs={{0,1},{1,0},{2,3},{3,2},{4,5},{5,4},{6,7},{7,6},{8,9},{9,8},{10,11... | collective-permute-start | bytes 1572872 | tf_op jit(solution)/shard_map/ppermute | solution.py:42
  19.0 7.4 %collective-permute-start.4 = (bf16[32,8192]{1,0:T(8,128)(2,1)S(1)}, bf16[32,8192]{1,0:T(8,128)(2,1)}, u32[]{:S(2)}, u32[]{:S(2)}) collective-permute-start(bf16[32,8192]{1,0:T(8,128)(2,1)S(1)} %collective-permute-done.3.xr), channel_id=1, source_target_pairs={{0,1},{1,0},{2,3},{3,2},{4,5},{5,4},{6,7},{7,6},{8,9},{9,8},{10,11... | collective-permute-start | bytes 1572872 | tf_op jit(solution)/shard_map/ppermute | solution.py:42
  24.1 2.3 %copy-start.17 = (bf16[16,8192]{1,0:T(8,128)(2,1)}, bf16[16,8192]{1,0:T(8,128)(2,1)S(1)}, u32[]{:S(2)}) copy-start(bf16[16,8192]{1,0:T(8,128)(2,1)S(1)} %collective-permute-done.5.f1) | copy-start | bytes 786436
  24.1 2.3 %collective-permute-start.7 = (bf16[16,8192]{1,0:T(8,128)(2,1)S(1)}, bf16[16,8192]{1,0:T(8,128)(2,1)}, u32[]{:S(2)}, u32[]{:S(2)}) collective-permute-start(bf16[16,8192]{1,0:T(8,128)(2,1)S(1)} %collective-permute-done.5.f1), channel_id=1, source_target_pairs={{0,1},{1,0},{2,3},{3,2},{4,5},{5,4},{6,7},{7,6},{8,9},{9,8},{10,11... | collective-permute-start | bytes 786440 | tf_op jit(solution)/shard_map/ppermute | solution.py:42
  24.1 2.3 %collective-permute-start.8 = (bf16[16,8192]{1,0:T(8,128)(2,1)}, bf16[16,8192]{1,0:T(8,128)(2,1)}, u32[]{:S(2)}, u32[]{:S(2)}) collective-permute-start(bf16[16,8192]{1,0:T(8,128)(2,1)} %collective-permute-done.6.f2), channel_id=1, source_target_pairs={{0,1},{1,0},{2,3},{3,2},{4,5},{5,4},{6,7},{7,6},{8,9},{9,8},{10,11... | collective-permute-start | bytes 786440 | tf_op jit(solution)/shard_map/ppermute | solution.py:42
  26.2 26.3 %slice-start = ((s8[8388608]{0:T(1024)(128)(4,1)}), s8[4194304]{0:T(1024)(128)(4,1)S(1)}, s32[]{:S(2)}) async-start(s8[8388608]{0:T(1024)(128)(4,1)} %bitcast.66), calls=%async_computation.1 | async-start | bytes 8388608
  26.3 26.2 %slice-start.1 = ((s8[8388608]{0:T(1024)(128)(4,1)}), s8[4194304]{0:T(1024)(128)(4,1)S(1)}, s32[]{:S(2)}) async-start(s8[8388608]{0:T(1024)(128)(4,1)} %bitcast.66), calls=%async_computation.2 | async-start | bytes 8388608
  26.4 3.5 %copy-start.1 = (bf16[8192,512]{1,0:T(8,128)(2,1)S(1)}, bf16[8192,512]{1,0:T(8,128)(2,1)}, u32[]{:S(2)}) copy-start(bf16[8192,512]{1,0:T(8,128)(2,1)} %wq.1) | copy-start | bytes 25165828
  30.0 2.3 %copy-start.2 = (bf16[8192,128]{1,0:T(8,128)(2,1)S(1)}, bf16[8192,128]{1,0:T(8,128)(2,1)}, u32[]{:S(2)}) copy-start(bf16[8192,128]{1,0:T(8,128)(2,1)} %wk.1) | copy-start | bytes 6291460
  32.3 1.6 %copy-start.3 = (bf16[8192,128]{1,0:T(8,128)(2,1)S(1)}, bf16[8192,128]{1,0:T(8,128)(2,1)}, u32[]{:S(2)}) copy-start(bf16[8192,128]{1,0:T(8,128)(2,1)} %wv.1) | copy-start | bytes 6291460
  33.9 1.3 copy-start.7
  52.6 3.6 %copy-start.13 = (bf16[256,1024]{1,0:T(8,128)(2,1)}, bf16[256,1024]{1,0:T(8,128)(2,1)S(1)}, u32[]{:S(2)}) copy-start(bf16[256,1024]{1,0:T(8,128)(2,1)S(1)} %get-tuple-element.27.mine) | copy-start | bytes 1572868
  56.2 46.5 %collective-permute-start.9 = (bf16[3,256,1024]{2,1,0:T(8,128)(2,1)}, bf16[3,256,1024]{2,1,0:T(8,128)(2,1)S(1)}, u32[]{:S(2)}, u32[]{:S(2)}) collective-permute-start(bf16[3,256,1024]{2,1,0:T(8,128)(2,1)} %get-tuple-element.30), channel_id=1, source_target_pairs={{0,1},{1,0},{2,3},{3,2},{4,5},{5,4},{6,7},{7,6},{8,9},{9,8},{10,11... | collective-permute-start | bytes 4718600 | tf_op jit(solution)/shard_map/ppermute | solution.py:42
  57.8 6.5 %collective-permute-start.15 = (bf16[4,64,128]{2,1,0:T(8,128)(2,1)}, bf16[4,64,128]{2,1,0:T(8,128)(2,1)}, u32[]{:S(2)}, u32[]{:S(2)}) collective-permute-start(bf16[4,64,128]{2,1,0:T(8,128)(2,1)} %get-tuple-element.53), channel_id=1, source_target_pairs={{0,1},{1,0},{2,3},{3,2},{4,5},{5,4},{6,7},{7,6},{8,9},{9,8},{10,11... | collective-permute-start | bytes 196616 | tf_op jit(solution)/shard_map/ppermute | solution.py:42
  58.2 3.4 %copy-start = (bf16[512,8192]{1,0:T(8,128)(2,1)S(1)}, bf16[512,8192]{1,0:T(8,128)(2,1)}, u32[]{:S(2)}) copy-start(bf16[512,8192]{1,0:T(8,128)(2,1)} %w_out.3) | copy-start | bytes 25165828
  64.2 25.6 %collective-permute-start.10 = (bf16[256,1024]{1,0:T(8,128)(2,1)}, bf16[256,1024]{1,0:T(8,128)(2,1)}, u32[]{:S(2)}, u32[]{:S(2)}) collective-permute-start(bf16[256,1024]{1,0:T(8,128)(2,1)} %get-tuple-element.32), channel_id=1, source_target_pairs={{0,1},{1,0},{2,3},{3,2},{4,5},{5,4},{6,7},{7,6},{8,9},{9,8},{10,11... | collective-permute-start | bytes 1572872 | tf_op jit(solution)/shard_map/ppermute | solution.py:42
  65.9 6.0 %collective-permute-start.16 = (bf16[2,64,128]{2,1,0:T(8,128)(2,1)}, bf16[2,64,128]{2,1,0:T(8,128)(2,1)S(1)}, u32[]{:S(2)}, u32[]{:S(2)}) collective-permute-start(bf16[2,64,128]{2,1,0:T(8,128)(2,1)} %get-tuple-element.56), channel_id=1, source_target_pairs={{0,2},{2,4},{4,6},{6,0},{1,3},{3,5},{5,7},{7,1},{8,10},{10,12},{12... | collective-permute-start | bytes 98312 | tf_op jit(solution)/shard_map/ppermute | solution.py:42
  66.1 5.9 %collective-permute-start.17 = (bf16[2,64,128]{2,1,0:T(8,128)(2,1)S(1)}, bf16[2,64,128]{2,1,0:T(8,128)(2,1)S(1)}, u32[]{:S(2)}, u32[]{:S(2)}) collective-permute-start(bf16[2,64,128]{2,1,0:T(8,128)(2,1)S(1)} %get-tuple-element.55), channel_id=1, source_target_pairs={{0,6},{2,0},{4,2},{6,4},{1,7},{3,1},{5,3},{7,5},{8,14},{10,8},{12,... | collective-permute-start | bytes 98312 | tf_op jit(solution)/shard_map/ppermute | solution.py:42
  69.1 5.4 %collective-permute-start.18 = (bf16[2,64,128]{2,1,0:T(8,128)(2,1)S(1)}, bf16[2,64,128]{2,1,0:T(8,128)(2,1)S(1)}, u32[]{:S(2)}, u32[]{:S(2)}) collective-permute-start(bf16[2,64,128]{2,1,0:T(8,128)(2,1)S(1)} %get-tuple-element.54), channel_id=1, source_target_pairs={{0,4},{2,6},{4,0},{6,2},{1,5},{3,7},{5,1},{7,3},{8,12},{10,14},{12... | collective-permute-start | bytes 98312 | tf_op jit(solution)/shard_map/ppermute | solution.py:42
  78.8 7.3 %collective-permute-start.19 = (bf16[64,1024]{1,0:T(8,128)(2,1)S(1)}, bf16[64,1024]{1,0:T(8,128)(2,1)S(1)}, u32[]{:S(2)}, u32[]{:S(2)}) collective-permute-start(bf16[64,1024]{1,0:T(8,128)(2,1)S(1)} %reshape.58), channel_id=1, source_target_pairs={{0,8},{8,16},{16,24},{24,0},{1,9},{9,17},{17,25},{25,1},{2,10},{10... | collective-permute-start | bytes 393224 | tf_op jit(solution)/shard_map/ppermute | solution.py:42
  80.7 7.3 %collective-permute-start.20 = (bf16[64,1024]{1,0:T(8,128)(2,1)S(1)}, bf16[64,1024]{1,0:T(8,128)(2,1)S(1)}, u32[]{:S(2)}, u32[]{:S(2)}) collective-permute-start(bf16[64,1024]{1,0:T(8,128)(2,1)S(1)} %reshape.58), channel_id=1, source_target_pairs={{0,24},{8,0},{16,8},{24,16},{1,25},{9,1},{17,9},{25,17},{2,26},{10... | collective-permute-start | bytes 393224 | tf_op jit(solution)/shard_map/ppermute | solution.py:42
  83.1 6.7 %collective-permute-start.21 = (bf16[64,1024]{1,0:T(8,128)(2,1)S(1)}, bf16[64,1024]{1,0:T(8,128)(2,1)S(1)}, u32[]{:S(2)}, u32[]{:S(2)}) collective-permute-start(bf16[64,1024]{1,0:T(8,128)(2,1)S(1)} %reshape.58), channel_id=1, source_target_pairs={{0,16},{8,24},{16,0},{24,8},{1,17},{9,25},{17,1},{25,9},{2,18},{10... | collective-permute-start | bytes 393224 | tf_op jit(solution)/shard_map/ppermute | solution.py:42
  89.8 14.0 %copy-start.4 = (bf16[256,1024]{1,0:T(8,128)(2,1)}, bf16[256,1024]{1,0:T(8,128)(2,1)S(1)}, u32[]{:S(2)}) copy-start(bf16[256,1024]{1,0:T(8,128)(2,1)S(1)} %pad_maximum_fusion.s0) | copy-start | bytes 1572868
  89.9 1.2 copy-start.16
  92.3 14.8 %collective-permute-start.23 = (bf16[256,1024]{1,0:T(8,128)(2,1)S(1)}, bf16[256,1024]{1,0:T(8,128)(2,1)S(1)}, u32[]{:S(2)}, u32[]{:S(2)}) collective-permute-start(bf16[256,1024]{1,0:T(8,128)(2,1)S(1)} %pad_maximum_fusion.s0), channel_id=1, source_target_pairs={{0,96},{32,0},{64,32},{96,64},{1,97},{33,1},{65,33},{97,65},{2,98}... | collective-permute-start | bytes 1572872 | tf_op jit(solution)/shard_map/ppermute | solution.py:42
  95.1 13.0 %collective-permute-start.22 = (bf16[256,1024]{1,0:T(8,128)(2,1)S(1)}, bf16[256,1024]{1,0:T(8,128)(2,1)S(1)}, u32[]{:S(2)}, u32[]{:S(2)}) collective-permute-start(bf16[256,1024]{1,0:T(8,128)(2,1)S(1)} %pad_maximum_fusion.s0), channel_id=1, source_target_pairs={{0,32},{32,64},{64,96},{96,0},{1,33},{33,65},{65,97},{97,1},{2,34}... | collective-permute-start | bytes 1572872 | tf_op jit(solution)/shard_map/ppermute | solution.py:42
  95.1 7.6 %collective-permute-start.11 = (bf16[128,1024]{1,0:T(8,128)(2,1)S(1)}, bf16[128,1024]{1,0:T(8,128)(2,1)S(1)}, u32[]{:S(2)}, u32[]{:S(2)}) collective-permute-start(bf16[128,1024]{1,0:T(8,128)(2,1)S(1)} %get-tuple-element.33), channel_id=1, source_target_pairs={{0,2},{2,4},{4,6},{6,0},{1,3},{3,5},{5,7},{7,1},{8,10},{10,12},{12... | collective-permute-start | bytes 786440 | tf_op jit(solution)/shard_map/ppermute | solution.py:42
  95.1 7.6 %collective-permute-start.12 = (bf16[128,1024]{1,0:T(8,128)(2,1)S(1)}, bf16[128,1024]{1,0:T(8,128)(2,1)S(1)}, u32[]{:S(2)}, u32[]{:S(2)}) collective-permute-start(bf16[128,1024]{1,0:T(8,128)(2,1)S(1)} %get-tuple-element.34), channel_id=1, source_target_pairs={{0,6},{2,0},{4,2},{6,4},{1,7},{3,1},{5,3},{7,5},{8,14},{10,8},{12,... | collective-permute-start | bytes 786440 | tf_op jit(solution)/shard_map/ppermute | solution.py:42
  103.8 16.2 %collective-permute-start.13 = (bf16[256,1024]{1,0:T(8,128)(2,1)}, bf16[256,1024]{1,0:T(8,128)(2,1)}, u32[]{:S(2)}, u32[]{:S(2)}) collective-permute-start(bf16[256,1024]{1,0:T(8,128)(2,1)} %get-tuple-element.35), channel_id=1, source_target_pairs={{0,2},{2,4},{4,6},{6,0},{1,3},{3,5},{5,7},{7,1},{8,10},{10,12},{12... | collective-permute-start | bytes 1572872 | tf_op jit(solution)/shard_map/ppermute | solution.py:42
  103.8 16.2 %collective-permute-start.14 = (bf16[256,1024]{1,0:T(8,128)(2,1)}, bf16[256,1024]{1,0:T(8,128)(2,1)}, u32[]{:S(2)}, u32[]{:S(2)}) collective-permute-start(bf16[256,1024]{1,0:T(8,128)(2,1)} %get-tuple-element.36), channel_id=1, source_target_pairs={{0,6},{2,0},{4,2},{6,4},{1,7},{3,1},{5,3},{7,5},{8,14},{10,8},{12,... | collective-permute-start | bytes 1572872 | tf_op jit(solution)/shard_map/ppermute | solution.py:42
  107.1 1.0 copy-start.8
  109.0 7.3 %collective-permute-start.25 = (bf16[128,1024]{1,0:T(8,128)(2,1)}, bf16[128,1024]{1,0:T(8,128)(2,1)S(1)}, u32[]{:S(2)}, u32[]{:S(2)}) collective-permute-start(bf16[128,1024]{1,0:T(8,128)(2,1)} %slice.19), channel_id=1, source_target_pairs={{0,96},{32,0},{64,32},{96,64},{1,97},{33,1},{65,33},{97,65},{2,98}... | collective-permute-start | bytes 786440 | tf_op jit(solution)/shard_map/ppermute | solution.py:42
  112.1 7.9 %collective-permute-start.24 = (bf16[128,1024]{1,0:T(8,128)(2,1)}, bf16[128,1024]{1,0:T(8,128)(2,1)}, u32[]{:S(2)}, u32[]{:S(2)}) collective-permute-start(bf16[128,1024]{1,0:T(8,128)(2,1)} %slice.18), channel_id=1, source_target_pairs={{0,32},{32,64},{64,96},{96,0},{1,33},{33,65},{65,97},{97,1},{2,34}... | collective-permute-start | bytes 786440 | tf_op jit(solution)/shard_map/ppermute | solution.py:42
  120.0 1.0 copy-start.5
  121.0 1.0 copy-start.9
  122.1 1.0 copy-start.11
  123.1 1.0 copy-start.14
  129.3 1.6 %collective-permute-start.26 = (bf16[272,512]{1,0:T(8,128)(2,1)S(1)}, bf16[272,512]{1,0:T(8,128)(2,1)S(1)}, u32[]{:S(2)}, u32[]{:S(2)}) collective-permute-start(bf16[272,512]{1,0:T(8,128)(2,1)S(1)} %get-tuple-element.43), channel_id=1, source_target_pairs={{0,1},{1,0},{2,3},{3,2},{4,5},{5,4},{6,7},{7,6},{8,9},{9,8},{10,11... | collective-permute-start | bytes 835592 | tf_op jit(solution)/shard_map/ppermute | solution.py:42
  131.6 5.6 %collective-permute-start.27 = (bf16[272,128]{1,0:T(8,128)(2,1)S(1)}, bf16[272,128]{1,0:T(8,128)(2,1)S(1)}, u32[]{:S(2)}, u32[]{:S(2)}) collective-permute-start(bf16[272,128]{1,0:T(8,128)(2,1)S(1)} %get-tuple-element.46), channel_id=1, source_target_pairs={{0,2},{2,4},{4,6},{6,0},{1,3},{3,5},{5,7},{7,1},{8,10},{10,12},{12... | collective-permute-start | bytes 208904 | tf_op jit(solution)/shard_map/ppermute | solution.py:42
  131.7 5.5 %collective-permute-start.28 = (bf16[272,128]{1,0:T(8,128)(2,1)S(1)}, bf16[272,128]{1,0:T(8,128)(2,1)S(1)}, u32[]{:S(2)}, u32[]{:S(2)}) collective-permute-start(bf16[272,128]{1,0:T(8,128)(2,1)S(1)} %get-tuple-element.47), channel_id=1, source_target_pairs={{0,6},{2,0},{4,2},{6,4},{1,7},{3,1},{5,3},{7,5},{8,14},{10,8},{12,... | collective-permute-start | bytes 208904 | tf_op jit(solution)/shard_map/ppermute | solution.py:42
  134.9 5.8 %collective-permute-start.29 = (bf16[272,128]{1,0:T(8,128)(2,1)S(1)}, bf16[272,128]{1,0:T(8,128)(2,1)S(1)}, u32[]{:S(2)}, u32[]{:S(2)}) collective-permute-start(bf16[272,128]{1,0:T(8,128)(2,1)S(1)} %get-tuple-element.48), channel_id=1, source_target_pairs={{0,4},{2,6},{4,0},{6,2},{1,5},{3,7},{5,1},{7,3},{8,12},{10,14},{12... | collective-permute-start | bytes 208904 | tf_op jit(solution)/shard_map/ppermute | solution.py:42
  (3 other events, 2.7 us)

commit v4 on v3

v4 whole, which is shorter than its diff:
```python
import functools

import jax
import jax.numpy as jnp
from jax import lax
from jax.experimental import pallas as pl
from jax.experimental.pallas import tpu as pltpu
from jax.sharding import Mesh, PartitionSpec as P

HEAD_DIM = 128
SESS = 16
CACHE = 320
CAPS = 2
GQA = 4
MOST = 20
ROOM = 24
KEYS = 384

EPSILON = 1e-06

VMEM = pl.BlockSpec(memory_space=pltpu.VMEM)
SMEM = pl.BlockSpec(memory_space=pltpu.SMEM)
ANY = pl.BlockSpec(memory_space=pl.ANY)
DMA = pltpu.SemaphoreType.DMA


def call(kernel, outs, in_specs, scratch=(), limit=10, flops=0, nbytes=0):
    shapes = [jax.ShapeDtypeStruct(out[0], out[1]) for out in outs]
    return pl.pallas_call(
        kernel,
        out_shape=shapes,
        in_specs=in_specs,
        out_specs=[out[2] if len(out) > 2 else VMEM for out in outs],
        scratch_shapes=list(scratch),
        compiler_params=pltpu.CompilerParams(vmem_limit_bytes=limit << 20),
        cost_estimate=pl.CostEstimate(flops=flops, bytes_accessed=nbytes, transcendentals=0),
    )


def shift(values, axis, step):
    size = lax.axis_size(axis)
    return lax.ppermute(values, axis, [(i, (i + step) % size) for i in range(size)])


def tables(session_row, owner_row):
    session_range = jnp.arange(SESS, dtype=jnp.int32)
    member = (session_row[:, None] == session_range[None, :]).astype(jnp.int32)
    before = (session_row[None, :] < session_range[:, None]).astype(jnp.int32)
    starts = jnp.sum(before, axis=1)
    first_row = jnp.sum(member * starts[None, :], axis=1)
    position = jnp.arange(session_row.shape[0], dtype=jnp.int32) - first_row
    earlier = (owner_row[:, None] == owner_row[None, :]) & (
        session_range[None, :] < session_range[:, None]
    )
    owner_rank = jnp.sum(earlier.astype(jnp.int32), axis=1)
    owner_slot = owner_row * CAPS + owner_rank
    destination = jnp.sum(member * owner_slot[None, :], axis=1) * MOST + position
    return session_row * ROOM + position, destination


def block(values, weights):
    return jnp.dot(values, weights[...], preferred_element_type=jnp.float32).astype(jnp.bfloat16)


def columns(ref, spot, width):
    return ref.at[:, pl.ds(pl.multiple_of(spot, width), width)]


def attention_kernel(
    spots, live, x0, t0, xl, tl, xr, tr, f1, f2, e1, e2, gain, wq, wk, wv, ck, cv, w_out, place,
    place_t, out, mine, send, keep, xs, ws, wo, acc, slots, kk, vv, mixed, row_sem, w_sem, sem,
):
    half = f1.shape[0]
    rows, width = xs.shape
    heads = wq.shape[1]
    share = mine.shape[1]
    depth = 1024
    row_copies = []
    for i, (ref, spot, extra) in enumerate(
        (
            (x0, 0, 0), (t0, 1, 0), (xl, 2, 0), (tl, 3, 0), (xr, 4, 0), (tr, 5, 0),
            (f1, 6, 0), (e1, 7, 0), (f2, 6, half), (e2, 7, half),
        )
    ):
        start = pl.multiple_of(spots[spot] + extra, 16)
        row_copies.append(
            pltpu.make_async_copy(ref, xs.at[pl.ds(start, ref.shape[0])], row_sem.at[i])
        )

    def weight_copies(i):
        part = pl.ds(pl.multiple_of(i * depth, depth), depth)
        return [
            pltpu.make_async_copy(
                ref.at[part], ws.at[part, pl.ds(low, ref.shape[1])], w_sem.at[j, i]
            )
            for j, (ref, low) in enumerate(((wq, 0), (wk, heads), (wv, heads + 128)))
        ]

    cache_copies = [
        pltpu.make_async_copy(ck, kk.at[:, pl.ds(0, CACHE)], sem.at[0]),
        pltpu.make_async_copy(cv, vv.at[:, pl.ds(0, CACHE)], sem.at[1]),
    ]
    out_copies = [
        pltpu.make_async_copy(columns(w_out, spots[9 + i], share), wo.at[i], sem.at[2 + i])
        for i in range(2)
    ]
    for copy in row_copies:
        copy.start()
    for i in range(width // depth):
        for copy in weight_copies(i):
            copy.start()
    for copy in cache_copies + out_copies:
        copy.start()
    unused = jnp.zeros((SESS, KEYS - CACHE - ROOM, HEAD_DIM), jnp.bfloat16)
    kk[:, CACHE + ROOM :, :] = unused
    vv[:, CACHE + ROOM :, :] = unused
    for copy in row_copies:
        copy.wait()
    mine_copy = pltpu.make_async_copy(columns(xs, spots[8], share), mine, sem.at[4])
    mine_copy.start()
    step = 512

    def square(i, total):
        x = xs[:, pl.ds(pl.multiple_of(i * step, step), step)].astype(jnp.float32)
        x = x * x
        for j in range(0, step, 128):
            total = total + x[:, j : j + 128]
        return total

    total = lax.fori_loop(0, width // step, square, jnp.zeros((rows, 128), jnp.float32))
    scale = lax.rsqrt(jnp.sum(total, axis=1, keepdims=True) / width + EPSILON)
    acc[...] = jnp.zeros_like(acc)

    @pl.loop(0, width // depth)
    def _(i):
        part = pl.ds(pl.multiple_of(i * depth, depth), depth)
        x = xs[:, part].astype(jnp.float32) * scale * gain[:, part].astype(jnp.float32)
        for copy in weight_copies(i):
            copy.wait()
        acc[...] += jnp.dot(
            x.astype(jnp.bfloat16), ws[part, :], preferred_element_type=jnp.float32
        )

    slots[...] = jnp.dot(
        place[...], acc[...].astype(jnp.bfloat16), preferred_element_type=jnp.float32
    )
    for copy in cache_copies:
        copy.wait()
    new_keys = slots[:, heads : heads + 128].reshape(SESS, ROOM, HEAD_DIM)
    new_values = slots[:, heads + 128 :].reshape(SESS, ROOM, HEAD_DIM)
    kk[:, CACHE : CACHE + ROOM, :] = new_keys.astype(jnp.bfloat16)
    vv[:, CACHE : CACHE + ROOM, :] = new_values.astype(jnp.bfloat16)
    column = lax.broadcasted_iota(jnp.int32, (GQA * ROOM, KEYS), 1)
    place_in = lax.rem(lax.broadcasted_iota(jnp.int32, (GQA * ROOM, KEYS), 0), ROOM)
    fresh = column - CACHE
    causal = (fresh <= place_in) & (fresh < ROOM)
    column = jnp.where(fresh < 0, column, jnp.where(causal, -1, CACHE))
    together = 4

    @pl.loop(0, SESS // together)
    def _(group):
        first = group * together
        spans = [pl.ds(pl.multiple_of((first + i) * ROOM, 8), ROOM) for i in range(together)]
        queries = [
            jnp.concatenate(
                [slots[at, h * HEAD_DIM : (h + 1) * HEAD_DIM] for h in range(GQA)], axis=0
            ).astype(jnp.bfloat16)
            for at in spans
        ]
        scores = [
            lax.dot_general(
                queries[i], kk[first + i], (((1,), (1,)), ((), ())),
                preferred_element_type=jnp.float32,
            )
            for i in range(together)
        ]
        results = []
        for i in range(together):
            score = jnp.where(
                column < live[0, first + i], scores[i] * (HEAD_DIM ** (-0.5)), -1e30
            )
            weights = jnp.exp(score - jnp.max(score, axis=1, keepdims=True))
            weights = weights * (1.0 / jnp.sum(weights, axis=1, keepdims=True))
            results.append(
                jnp.dot(
                    weights.astype(jnp.bfloat16), vv[first + i],
                    preferred_element_type=jnp.float32,
                )
            )
        for at, got in zip(spans, results):
            for h in range(GQA):
                mixed[at, h * HEAD_DIM : (h + 1) * HEAD_DIM] = got[h * ROOM : (h + 1) * ROOM]

    attended = jnp.dot(
        place_t[...], mixed[...].astype(jnp.bfloat16), preferred_element_type=jnp.float32
    ).astype(jnp.bfloat16)
    out[...] = attended
    for copy in out_copies:
        copy.wait()
    send[...] = block(attended, wo.at[0])
    keep[...] = block(attended, wo.at[1])
    mine_copy.wait()


def project_kernel(spots, rows, w_out, out, wo, sem, *, first):
    copies = [
        pltpu.make_async_copy(columns(w_out, spots[first + i], wo.shape[2]), wo.at[i], sem.at[i])
        for i in range(3)
    ]
    for copy in copies:
        copy.start()
    for i in range(3):
        copies[i].wait()
        out[i] = block(rows[...], wo.at[i])


def halves_kernel(keep, other, first, second):
    total = keep[...].astype(jnp.float32) + other[...].astype(jnp.float32)
    total = total.astype(jnp.bfloat16)
    half = first.shape[0]
    first[...] = total[:half]
    second[...] = total[half:]


def pack_kernel(s0, s1, s3, s2, out, sem):
    copies = [
        pltpu.make_async_copy(ref, out.at[i], sem.at[i]) for i, ref in enumerate((s0, s1, s3, s2))
    ]
    for copy in copies:
        copy.start()
    for copy in copies:
        copy.wait()


def fetch(pairs, sem):
    copies = [pltpu.make_async_copy(ref, buf, sem.at[i]) for i, (ref, buf) in enumerate(pairs)]
    for copy in copies:
        copy.start()
    return copies


def relay_kernel(keep, other, ahead, behind, to_next, to_last, kb, ob, ab, bb, sem):
    half = ahead.shape[0]
    pairs = []
    for i, (got, buf) in enumerate(((ahead, ab), (behind, bb))):
        pairs += [(keep.at[i], kb.at[i]), (other.at[i], ob.at[i]), (got, buf)]
    copies = fetch(pairs, sem)
    for i, (ref, got, low) in enumerate(((to_next, ab, 0), (to_last, bb, half))):
        for copy in copies[3 * i : 3 * i + 3]:
            copy.wait()
        high = half - low
        total = kb[i].astype(jnp.float32) + ob[i].astype(jnp.float32)
        ref[low : low + half] = (
            total[low : low + half] + got[...].astype(jnp.float32)
        ).astype(jnp.bfloat16)
        ref[high : high + half] = total[high : high + half].astype(jnp.bfloat16)


def split3(values):
    high = values.astype(jnp.bfloat16).astype(jnp.float32)
    rest = values - high
    middle = rest.astype(jnp.bfloat16).astype(jnp.float32)
    return high, middle, rest - middle


def prepare_kernel(
    spots, mine, keep, other, s0, sl, sr, g1, g2, base, weights, mb, kb, ob, wt, sem
):
    piece = s0.shape[2]
    copies = fetch([(mine, mb), (keep.at[2], kb), (other.at[2], ob)], sem)
    pieces = []
    for ref, source, first, number in (
        (s0, 0, 0, 4), (sl, 1, 0, 4), (sr, 2, 0, 4), (g1, 3, 0, 2), (g2, 3, 2, 2),
    ):
        for j in range(number):
            start = pl.multiple_of(spots[11 + source * 4 + first + j], piece)
            pieces.append(
                pltpu.make_async_copy(
                    ref.at[j], wt.at[:, pl.ds(start, piece)], sem.at[3 + len(pieces)]
                )
            )
            pieces[-1].start()
    for copy in copies:
        copy.wait()
    base[...] = (
        mb[...].astype(jnp.float32) + kb[...].astype(jnp.float32) + ob[...].astype(jnp.float32)
    )
    for copy in pieces:
        copy.wait()
    width = wt.shape[2]
    for source in range(8):
        at = (source % 2 * 4 + source // 2) * width
        weights[:, at : at + width] = wt[source]


def talker_kernel(
    spots, base, from_last, from_next, gain, weights, send, kept, squares, bb, lb, nb, wb, sem
):
    copies = fetch([(base, bb), (from_last, lb), (from_next, nb), (weights, wb)], sem)
    for copy in copies[:3]:
        copy.wait()
    total = bb[...] + lb[...].astype(jnp.float32) + nb[...].astype(jnp.float32)
    hidden = total.astype(jnp.bfloat16).astype(jnp.float32)
    square = jnp.zeros((hidden.shape[0], 128), jnp.float32)
    for j in range(0, hidden.shape[1], 128):
        square = square + hidden[:, j : j + 128] * hidden[:, j : j + 128]
    row = jnp.sum(jnp.transpose(square), axis=0, keepdims=True)
    squares[...] = jnp.broadcast_to(row, squares.shape)
    scaled = (hidden * gain[...].astype(jnp.float32)).astype(jnp.bfloat16)
    rows, width = kept.shape
    copies[3].wait()
    send[:rows] = jnp.dot(
        scaled, wb[:, pl.ds(pl.multiple_of(spots[28], width), width)],
        preferred_element_type=jnp.float32,
    ).astype(jnp.bfloat16)
    kept[...] = jnp.dot(
        scaled, wb[:, pl.ds(pl.multiple_of(spots[27], width), width)],
        preferred_element_type=jnp.float32,
    )
    parts = jnp.concatenate(list(split3(row)) + [jnp.zeros((13, rows), jnp.float32)], axis=0)
    parts = jnp.concatenate([parts, jnp.zeros((16, width - rows), jnp.float32)], axis=1)
    send[rows:] = parts.astype(jnp.bfloat16)


def across_kernel(spots, kept, squares, got, own, squares_out, s1, s3, s2):
    rows = kept.shape[0]
    width = own.shape[1]
    tail = got[rows:, :rows].astype(jnp.float32)
    row = squares[0:1] + (tail[0:1] + tail[1:2] + tail[2:3])
    squares_out[...] = jnp.broadcast_to(row, squares_out.shape)
    pieces = []
    for part in split3(row):
        pieces += [part[:, j : j + 128] for j in range(0, rows, 128)]
    tail = jnp.concatenate(
        pieces + [jnp.zeros((16 - len(pieces), 128), jnp.float32)], axis=0
    ).astype(jnp.bfloat16)
    for i, ref in enumerate((own, s1, s3, s2)):
        at = pl.ds(pl.multiple_of(spots[29 + i], width), width)
        total = kept[:, at] + got[:rows, at].astype(jnp.float32)
        ref[:rows] = total.astype(ref.dtype)
        if i > 0:
            ref[rows:] = tail


def route_kernel(own, squares, g1, g3, g2, routing, out, *, features):
    rows = own.shape[0]
    total = own[...]
    row = squares[0:1]
    for ref in (g1, g3, g2):
        total = total + ref[:rows].astype(jnp.float32)
        tail = ref[rows:].astype(jnp.float32)
        row = row + jnp.concatenate(
            [tail[j : j + 1] + tail[2 + j : 3 + j] + tail[4 + j : 5 + j] for j in range(2)], axis=1
        )
    scale = lax.rsqrt(row / features + EPSILON)
    scale = jnp.transpose(jnp.broadcast_to(scale, (128, rows)))
    values = (total * scale).astype(jnp.bfloat16)
    out[...] = jnp.dot(routing[...], values, preferred_element_type=jnp.float32).astype(
        jnp.bfloat16
    )


def on_device(
    thinker_rows,
    norm_gain,
    w_query,
    w_key,
    w_value,
    w_out,
    cache_keys,
    cache_values,
    session_ids,
    cache_lens,
    owners,
    talker_gain,
    w_talker,
):
    local, features = thinker_rows.shape
    bf16, f32 = jnp.bfloat16, jnp.float32
    tokens = local * 8
    share = features // 8
    width = w_talker.shape[1]
    heads = w_query.shape[1]
    piece = share // 16
    x, z = lax.axis_index("x"), lax.axis_index("z")
    y, core = lax.axis_index("y"), lax.axis_index("core")
    member = y * 2 + core

    half = local // 2
    left, right = shift(thinker_rows, "y", 1), shift(thinker_rows, "y", -1)
    twin = shift(thinker_rows, "core", 1)
    strip = lax.dynamic_index_in_dim(
        w_talker.reshape(8, 16, piece, width), x * 4 + z, 1, keepdims=False
    )
    strip = lax.all_to_all(strip, ("y", "core"), split_axis=0, concat_axis=0, tiled=True)
    left, right, strip = lax.optimization_barrier((left, right, strip))
    low, high = left[:half], right[half:]
    far_low, far_high = shift(low, "y", 1), shift(high, "y", -1)
    twin_left, twin_right = shift(left, "core", 1), shift(right, "core", 1)
    strips = [strip] + [shift(strip, "z", d) for d in (1, 3, 2)]
    twin_low, twin_high = shift(far_low, "core", 1), shift(far_high, "core", 1)

    near = [y, (y + 3) % 4, (y + 1) % 4, (y + 2) % 4]
    ids, lens, owner_ids, _ = lax.optimization_barrier((session_ids, cache_lens, owners, left))
    slot, destination = tables(ids[0], owner_ids[:, 0])
    places = jnp.arange(SESS * ROOM, dtype=jnp.int32)
    place_t = (slot[:, None] == places[None, :]).astype(bf16)
    place = (slot[None, :] == places[:, None]).astype(bf16)
    routing = (
        destination[None, :] == jnp.arange(16 * CAPS * MOST, dtype=jnp.int32)[:, None]
    ).astype(bf16)
    spots = []
    for chip in near:
        spots += [(chip * 2 + core) * local, (chip * 2 + 1 - core) * local]
    spots += [member * share]
    order = [(y + 2) % 4, (y + 1) % 4, (y + 3) % 4, y]
    sends = [(chip * 2 + 1 - core) * share for chip in order]
    keeps = [(chip * 2 + core) * share for chip in order]
    nearx = [x, (x + 3) % 4, (x + 1) % 4, (x + 2) % 4]
    nearz = [z, (z + 3) % 4, (z + 1) % 4, (z + 2) % 4]
    spots += [sends[0], keeps[0]]
    spots += [(cx * 4 + cz) * piece for cx in nearx for cz in nearz]
    spots += [core * 4 * width, (1 - core) * 4 * width]
    spots += [((y + d) % 4) * width for d in (0, 1, 3, 2)]
    spots = jnp.stack(spots + sends[1:] + keeps[1:]).astype(jnp.int32)
    gain = lax.dynamic_slice(talker_gain, (member * share,), (share,))[None, :]

    block_type = ((tokens, share), bf16)
    rows, mine, send_far, keep_far = call(
        attention_kernel,
        [((tokens, heads), bf16), block_type + (ANY,), block_type, block_type],
        [SMEM, SMEM] + [ANY] * 10 + [VMEM] + [ANY] * 6 + [VMEM] * 2,
        [
            pltpu.VMEM((tokens, features), bf16),
            pltpu.VMEM((features, heads + 256), bf16),
            pltpu.VMEM((2, heads, share), bf16),
            pltpu.VMEM((tokens, heads + 256), f32),
            pltpu.VMEM((SESS * ROOM, heads + 256), f32),
            pltpu.VMEM((SESS, KEYS, HEAD_DIM), bf16),
            pltpu.VMEM((SESS, KEYS, HEAD_DIM), bf16),
            pltpu.VMEM((SESS * ROOM, heads), f32),
            DMA((10,)),
            DMA((3, 8)),
            DMA((5,)),
        ],
        limit=36,
        flops=5 * 10**9,
        nbytes=24 * 10**6,
    )(
        spots, lens, thinker_rows, twin, left, twin_left, right, twin_right, far_low,
        far_high, twin_low, twin_high, norm_gain[None, :], w_query, w_key, w_value, cache_keys,
        cache_values, w_out, place, place_t,
    )
    other_far = shift(send_far, "core", 1)

    def project(first):
        return call(
            functools.partial(project_kernel, first=first),
            [((3, tokens, share), bf16)],
            [SMEM, VMEM, ANY],
            [pltpu.VMEM((3, heads, share), bf16), DMA((3,))],
            flops=8 * 10**8,
            nbytes=5 * 10**6,
        )(spots, rows, w_out)[0]

    send = project(33)
    other = shift(send, "core", 1)
    first, second = call(
        halves_kernel, [((tokens // 2, share), bf16)] * 2, [VMEM] * 2,
        flops=10**6, nbytes=2 * 10**6,
    )(keep_far, other_far)
    ahead, behind = shift(first, "y", 1), shift(second, "y", -1)
    keep = project(36)
    (strip,) = call(
        pack_kernel, [((4, 8, piece, width), bf16, ANY)], [ANY] * 4, [DMA((4,))],
        flops=10**5, nbytes=10**6,
    )(*strips)
    strip_left, strip_right = shift(strip, "x", 1), shift(strip, "x", -1)
    to_next, to_last = call(
        relay_kernel,
        [block_type] * 2,
        [ANY] * 4,
        [pltpu.VMEM((2, tokens, share), bf16)] * 2
        + [pltpu.VMEM((tokens // 2, share), bf16)] * 2
        + [DMA((6,))],
        flops=10**6,
        nbytes=4 * 10**6,
    )(keep, other, ahead, behind)
    from_last, from_next = shift(to_next, "y", 1), shift(to_last, "y", -1)
    strip_low = shift(strip_left[:2], "x", 1)
    strip_high = shift(strip_right[2:], "x", -1)
    base, weights = call(
        prepare_kernel,
        [((tokens, share), f32), ((share, 8 * width), bf16)],
        [SMEM] + [ANY] * 8,
        [pltpu.VMEM((tokens, share), bf16)] * 3
        + [pltpu.VMEM((8, share, width), bf16), DMA((19,))],
        flops=10**6,
        nbytes=4 * 10**6,
    )(spots, mine, keep, other, strip, strip_left, strip_right, strip_low, strip_high)
    sent, kept, squares = call(
        talker_kernel,
        [((tokens + 16, 4 * width), bf16), ((tokens, 4 * width), f32), ((8, tokens), f32)],
        [SMEM] + [ANY] * 3 + [VMEM, ANY],
        [pltpu.VMEM((tokens, share), f32)]
        + [pltpu.VMEM((tokens, share), bf16)] * 2
        + [pltpu.VMEM((share, 8 * width), bf16), DMA((4,))],
        flops=6 * 10**8,
        nbytes=4 * 10**6,
    )(spots, base, from_last, from_next, gain, weights)
    got = shift(sent, "core", 1)
    tall = ((tokens + 16, width), bf16)
    own, squares, s1, s3, s2 = call(
        across_kernel, [((tokens, width), f32), ((8, tokens), f32), tall, tall, tall],
        [SMEM] + [VMEM] * 3, flops=10**6, nbytes=10**6,
    )(spots, kept, squares, got)
    g2 = shift(s2, "y", 2)
    g1, g3 = shift(s1, "y", 1), shift(s3, "y", 3)
    (outgoing,) = call(
        functools.partial(route_kernel, features=features),
        [((16 * CAPS * MOST, width), bf16)], [VMEM] * 6, flops=4 * 10**7, nbytes=10**6,
    )(own, squares, g1, g3, g2, routing)
    arrived = lax.all_to_all(
        outgoing.reshape(16, CAPS * MOST, width), ("x", "z"), split_axis=0, concat_axis=0,
        tiled=True,
    )
    return arrived.reshape(16 * CAPS * MOST, width)


def solution(mesh):
    grp, tp = ("x", "z"), ("y", "core")
    return jax.shard_map(
        on_device,
        mesh=Mesh(mesh.devices.reshape(4, 4, 4, 2), grp + tp),
        in_specs=(
            P(grp + tp, None),
            P(),
            P(None, tp),
            P(None, tp),
            P(None, tp),
            P(tp, None),
            P(grp, None, tp),
            P(grp, None, tp),
            P(grp, None),
            P(grp, None),
            P(grp, None),
            P(),
            P(None, tp),
        ),
        out_specs=P(grp, tp),
        check_vma=False,
    )
```

time: 154 us -> 131 us (0.85)
  local copies, waits for them, and re-layouts: 31.3 us -> 18.9 us
  other arithmetic: 6.53 us -> 0.66 us
  waiting for transfers between devices: 38.5 us -> 33.4 us
  blocking collectives: 11 us -> 13.1 us
  Pallas kernels: 30.2 us -> 28.1 us
    ppermute x30 -> x26, waiting for transfers between devices: 38.5 us -> 24.8 us  [shift(): lax.ppermute(values, axis, [(i, (i + step) % size) for i in range(size)])]
    all_to_all x0 -> x1, waiting for transfers between devices: none -> 8.59 us  [on_device(): lax.all_to_all(strip, ('y', 'core'), split_axis=0, concat_axis=0, tiled=T...]
    unnamed x43 -> x41, local copies, waits for them, and re-layouts: 20.1 us -> 12.7 us
    dynamic_update_slice x4 -> x0, local copies, waits for them, and re-layouts: 5.44 us -> none  [talker_strip(): across = lax.dynamic_update_index_in_dim(across, part, (y - d) % 4, 0)]
    all_to_all x0 -> x1, starting transfers between devices: none -> 3.38 us  [on_device(): lax.all_to_all(strip, ('y', 'core'), split_axis=0, concat_axis=0, tiled=T...]
    pallas_call x8 -> x10, Pallas kernels: 30.2 us -> 28.1 us  [the longest x1 14 us: on_device(): call(attention_kernel, [((tokens, heads), bf16), block_type + (ANY,), blo...]
    ppermute x30 -> x26, starting transfers between devices: 34.8 us -> 32.6 us  [shift(): lax.ppermute(values, axis, [(i, (i + step) % size) for i in range(size)])]
    all_to_all x1, blocking collectives: 11 us -> 13.1 us  [on_device(): lax.all_to_all(outgoing.reshape(16, CAPS * MOST, width), ('x', 'z'), spli...]
  transfers between devices with their start and end apart: 30 -> 27, of which waited for: 13 -> 14; matrix products, arithmetic and copies ran while one was open for 12% -> 5% of each run, Pallas kernels for 3% -> 6%
where the time goes in v4:
time: 131 us; the launch traced here: 130 us
  starting transfers between devices  36 us (27%)
  waiting for transfers between devices  33.4 us (25%)
  Pallas kernels  28.1 us (21%)
  local copies, waits for them, and re-layouts  18.9 us (14%)
  blocking collectives  13.1 us (10%)
    ppermute x26, starting transfers between devices, shift(): lax.ppermute(values, axis, [(i, (i + step) % size) for i in range(size)])  32.6 us
    ppermute x26, waiting for transfers between devices, shift(): lax.ppermute(values, axis, [(i, (i + step) % size) for i in range(size)])  24.8 us
    pallas_call x1, Pallas kernels, on_device(): call(attention_kernel, [((tokens, heads), bf16), block_type + (ANY,), blo...  14 us
    all_to_all x1, blocking collectives, on_device(): lax.all_to_all(outgoing.reshape(16, CAPS * MOST, width), ('x', 'z'), spli...  13.1 us
    unnamed x41, local copies, waits for them, and re-layouts  12.7 us
    all_to_all x1, waiting for transfers between devices, on_device(): lax.all_to_all(strip, ('y', 'core'), split_axis=0, concat_axis=0, tiled=T...  8.59 us
    pallas_call x2, Pallas kernels, project(): call(functools.partial(project_kernel, first=first), [((3, tokens, share)...  5.06 us
    all_to_all x1, starting transfers between devices, on_device(): lax.all_to_all(strip, ('y', 'core'), split_axis=0, concat_axis=0, tiled=T...  3.38 us
  transfers between devices with their start and end apart: 27, of which 14 were waited for; matrix products, arithmetic and copies ran while one was open for 5% of the time, Pallas kernels for 6%

profile of v4, /device:TPU:0, one launch (start us, length us, event | category | flops | bytes accessed | tf_op | source)
XLA Modules:
  0.0 130.4 jit_solution(3288873547443069182)
XLA Ops:
  0.0 1.8 %collective-permute-start = (bf16[32,8192]{1,0:T(8,128)(2,1)}, bf16[32,8192]{1,0:T(8,128)(2,1)}, u32[]{:S(2)}, u32[]{:S(2)}) collective-permute-start(bf16[32,8192]{1,0:T(8,128)(2,1)} %x0.1), channel_id=1, source_target_pairs={{0,2},{2,4},{4,6},{6,0},{1,3},{3,5},{5,7},{7,1},{8,10},{10,12},{12... | collective-permute-start | bytes 1572872 | tf_op jit(solution)/shard_map/ppermute | solution.py:42
  1.8 1.5 %collective-permute-start.1 = (bf16[32,8192]{1,0:T(8,128)(2,1)}, bf16[32,8192]{1,0:T(8,128)(2,1)}, u32[]{:S(2)}, u32[]{:S(2)}) collective-permute-start(bf16[32,8192]{1,0:T(8,128)(2,1)} %x0.1), channel_id=1, source_target_pairs={{0,6},{2,0},{4,2},{6,4},{1,7},{3,1},{5,3},{7,5},{8,14},{10,8},{12,... | collective-permute-start | bytes 1572872 | tf_op jit(solution)/shard_map/ppermute | solution.py:42
  4.0 3.4 %all-to-all-start = ((bf16[8,64,128]{2,1,0:T(8,128)(2,1)}), bf16[8,64,128]{2,1,0:T(8,128)(2,1)S(1)}, u32[]{:S(2)}, u32[]{:S(2)}) async-start(bf16[8,64,128]{2,1,0:T(8,128)(2,1)} %dynamic-slice_bitcast_fusion), calls=%async_computation | async-start | bytes 262144 | tf_op jit(solution)/shard_map/all_to_all | solution.py:395
  7.9 1.3 %broadcast_in_dim.4.gain = bf16[1,8192]{1,0:T(2,128)(2,1)} reshape(bf16[8192]{0:T(1024)(128)(2,1)} %param.14) | data formatting | bytes 32768 | tf_op jit(solution)/shard_map/broadcast_in_dim | solution.py:451
  9.4 8.6 %all-to-all-done.s0 = bf16[8,64,128]{2,1,0:T(8,128)(2,1)S(1)} async-done(((bf16[8,64,128]{2,1,0:T(8,128)(2,1)}), bf16[8,64,128]{2,1,0:T(8,128)(2,1)S(1)}, u32[]{:S(2)}, u32[]{:S(2)}) %all-to-all-start) | async-done | bytes 131104 | tf_op jit(solution)/shard_map/all_to_all | solution.py:395
  17.9 1.0 slice.12
  19.0 1.0 slice.13
  20.9 1.2 collective-permute-start.5
  22.1 2.1 %collective-permute-start.6 = (bf16[16,8192]{1,0:T(8,128)(2,1)S(1)}, bf16[16,8192]{1,0:T(8,128)(2,1)S(1)}, u32[]{:S(2)}, u32[]{:S(2)}) collective-permute-start(bf16[16,8192]{1,0:T(8,128)(2,1)S(1)} %slice.13), channel_id=1, source_target_pairs={{0,6},{2,0},{4,2},{6,4},{1,7},{3,1},{5,3},{7,5},{8,14},{10,8},{12,... | collective-permute-start | bytes 786440 | tf_op jit(solution)/shard_map/ppermute | solution.py:42
  24.4 6.0 %collective-permute-done.5.f1 = bf16[16,8192]{1,0:T(8,128)(2,1)S(1)} collective-permute-done((bf16[16,8192]{1,0:T(8,128)(2,1)S(1)}, bf16[16,8192]{1,0:T(8,128)(2,1)S(1)}, u32[]{:S(2)}, u32[]{:S(2)}) %collective-permute-start.5) | collective-permute-done | bytes 262176 | tf_op jit(solution)/shard_map/ppermute | solution.py:42
  31.0 0.9 collective-permute-done.7.e1
  32.3 1.6 %copy-done.5 = bf16[8192,128]{1,0:T(8,128)(2,1)S(1)} copy-done((bf16[8192,128]{1,0:T(8,128)(2,1)S(1)}, bf16[8192,128]{1,0:T(8,128)(2,1)}, u32[]{:S(2)}) %copy-start.5) | copy-done | bytes 2097176
  33.9 1.6 %copy-done.6 = bf16[8192,128]{1,0:T(8,128)(2,1)S(1)} copy-done((bf16[8192,128]{1,0:T(8,128)(2,1)S(1)}, bf16[8192,128]{1,0:T(8,128)(2,1)}, u32[]{:S(2)}) %copy-start.6) | copy-done | bytes 2097176
  35.5 1.3 %copy-done.8 = bf16[16,320,128]{2,1,0:T(8,128)(2,1)S(1)} copy-done((bf16[16,320,128]{2,1,0:T(8,128)(2,1)S(1)}, bf16[16,320,128]{2,1,0:T(8,128)(2,1)}, u32[]{:S(2)}) %copy-start.8) | copy-done | bytes 1310744
  36.8 1.0 copy-done.11
  37.9 0.8 copy-done.14
  38.6 14.0 %shard_map.127 = (bf16[256,512]{1,0:T(8,128)(2,1)S(1)}, bf16[256,1024]{1,0:T(8,128)(2,1)S(1)}, bf16[256,1024]{1,0:T(8,128)(2,1)S(1)}, bf16[256,1024]{1,0:T(8,128)(2,1)S(1)}) custom-call(s32[39]{0:T(128)S(1)} %stack.156.spots, s32[1,16]{1,0:T(1,128)S(1)} %copy-done.15, bf16[32,8192]{1,0:T(8,128)(2,1)S(1)} %copy-done.11, ...), custom_call_target="tpu_custom_call" | custom-call | flops 5000000000 | bytes 24000000 | tf_op jit(solution)/shard_map/pallas_call | solution.py:429
  52.6 2.5 %shard_map.129 = bf16[3,256,1024]{2,1,0:T(8,128)(2,1)S(1)} custom-call(s32[39]{0:T(128)S(1)} %stack.156.spots, bf16[256,512]{1,0:T(8,128)(2,1)S(1)} %get-tuple-element.34.rows, bf16[512,8192]{1,0:T(8,128)(2,1)S(1)} %bitcast.52), custom_call_target="tpu_custom_call" | custom-call | flops 800000000 | bytes 5000000 | tf_op jit(solution)/shard_map/pallas_call | solution.py:457
  55.8 1.9 %collective-permute-start.10 = (bf16[8,64,128]{2,1,0:T(8,128)(2,1)S(1)}, bf16[8,64,128]{2,1,0:T(8,128)(2,1)S(1)}, u32[]{:S(2)}, u32[]{:S(2)}) collective-permute-start(bf16[8,64,128]{2,1,0:T(8,128)(2,1)S(1)} %all-to-all-done.s0), channel_id=1, source_target_pairs={{0,8},{8,16},{16,24},{24,0},{1,9},{9,17},{17,25},{25,1},{2,10},{10... | collective-permute-start | bytes 393224 | tf_op jit(solution)/shard_map/ppermute | solution.py:42
  57.7 2.1 %collective-permute-start.11 = (bf16[8,64,128]{2,1,0:T(8,128)(2,1)S(1)}, bf16[8,64,128]{2,1,0:T(8,128)(2,1)S(1)}, u32[]{:S(2)}, u32[]{:S(2)}) collective-permute-start(bf16[8,64,128]{2,1,0:T(8,128)(2,1)S(1)} %all-to-all-done.s0), channel_id=1, source_target_pairs={{0,24},{8,0},{16,8},{24,16},{1,25},{9,1},{17,9},{25,17},{2,26},{10... | collective-permute-start | bytes 393224 | tf_op jit(solution)/shard_map/ppermute | solution.py:42
  59.8 1.9 %collective-permute-start.12 = (bf16[8,64,128]{2,1,0:T(8,128)(2,1)S(1)}, bf16[8,64,128]{2,1,0:T(8,128)(2,1)S(1)}, u32[]{:S(2)}, u32[]{:S(2)}) collective-permute-start(bf16[8,64,128]{2,1,0:T(8,128)(2,1)S(1)} %all-to-all-done.s0), channel_id=1, source_target_pairs={{0,16},{8,24},{16,0},{24,8},{1,17},{9,25},{17,1},{25,9},{2,18},{10... | collective-permute-start | bytes 393224 | tf_op jit(solution)/shard_map/ppermute | solution.py:42
  61.7 1.9 %collective-permute-done.10.s1 = bf16[8,64,128]{2,1,0:T(8,128)(2,1)S(1)} collective-permute-done((bf16[8,64,128]{2,1,0:T(8,128)(2,1)S(1)}, bf16[8,64,128]{2,1,0:T(8,128)(2,1)S(1)}, u32[]{:S(2)}, u32[]{:S(2)}) %collective-permute-start.10) | collective-permute-done | bytes 131104 | tf_op jit(solution)/shard_map/ppermute | solution.py:42
  63.6 2.1 %collective-permute-done.11.s3 = bf16[8,64,128]{2,1,0:T(8,128)(2,1)S(1)} collective-permute-done((bf16[8,64,128]{2,1,0:T(8,128)(2,1)S(1)}, bf16[8,64,128]{2,1,0:T(8,128)(2,1)S(1)}, u32[]{:S(2)}, u32[]{:S(2)}) %collective-permute-start.11) | collective-permute-done | bytes 131104 | tf_op jit(solution)/shard_map/ppermute | solution.py:42
  65.7 1.9 %collective-permute-done.12.s2 = bf16[8,64,128]{2,1,0:T(8,128)(2,1)S(1)} collective-permute-done((bf16[8,64,128]{2,1,0:T(8,128)(2,1)S(1)}, bf16[8,64,128]{2,1,0:T(8,128)(2,1)S(1)}, u32[]{:S(2)}, u32[]{:S(2)}) %collective-permute-start.12) | collective-permute-done | bytes 131104 | tf_op jit(solution)/shard_map/ppermute | solution.py:42
  68.3 1.6 %collective-permute-start.13 = (bf16[4,8,64,128]{3,2,1,0:T(8,128)(2,1)S(1)}, bf16[4,8,64,128]{3,2,1,0:T(8,128)(2,1)S(1)}, u32[]{:S(2)}, u32[]{:S(2)}) collective-permute-start(bf16[4,8,64,128]{3,2,1,0:T(8,128)(2,1)S(1)} %shard_map.130.s0), channel_id=1, source_target_pairs={{0,32},{32,64},{64,96},{96,0},{1,33},{33,65},{65,97},{97,1},{2,34}... | collective-permute-start | bytes 1572872 | tf_op jit(solution)/shard_map/ppermute | solution.py:42
  70.1 3.2 %collective-permute-start.19 = (bf16[128,1024]{1,0:T(8,128)(2,1)S(1)}, bf16[128,1024]{1,0:T(8,128)(2,1)S(1)}, u32[]{:S(2)}, u32[]{:S(2)}) collective-permute-start(bf16[128,1024]{1,0:T(8,128)(2,1)S(1)} %get-tuple-element.40), channel_id=1, source_target_pairs={{0,6},{2,0},{4,2},{6,4},{1,7},{3,1},{5,3},{7,5},{8,14},{10,8},{12,... | collective-permute-start | bytes 786440 | tf_op jit(solution)/shard_map/ppermute | solution.py:42
  73.3 1.7 %collective-permute-start.14 = (bf16[4,8,64,128]{3,2,1,0:T(8,128)(2,1)S(1)}, bf16[4,8,64,128]{3,2,1,0:T(8,128)(2,1)S(1)}, u32[]{:S(2)}, u32[]{:S(2)}) collective-permute-start(bf16[4,8,64,128]{3,2,1,0:T(8,128)(2,1)S(1)} %shard_map.130.s0), channel_id=1, source_target_pairs={{0,96},{32,0},{64,32},{96,64},{1,97},{33,1},{65,33},{97,65},{2,98}... | collective-permute-start | bytes 1572872 | tf_op jit(solution)/shard_map/ppermute | solution.py:42
  75.0 2.5 %shard_map.128.keep = bf16[3,256,1024]{2,1,0:T(8,128)(2,1)S(1)} custom-call(s32[39]{0:T(128)S(1)} %stack.156.spots, bf16[256,512]{1,0:T(8,128)(2,1)S(1)} %get-tuple-element.34.rows, bf16[512,8192]{1,0:T(8,128)(2,1)S(1)} %bitcast.52), custom_call_target="tpu_custom_call" | custom-call | flops 800000000 | bytes 5000000 | tf_op jit(solution)/shard_map/pallas_call | solution.py:457
  77.6 0.9 collective-permute-done.18.ahead
  78.5 1.6 %shard_map.133 = (bf16[256,1024]{1,0:T(8,128)(2,1)}, bf16[256,1024]{1,0:T(8,128)(2,1)}) custom-call(bf16[3,256,1024]{2,1,0:T(8,128)(2,1)S(1)} %shard_map.128.keep, bf16[3,256,1024]{2,1,0:T(8,128)(2,1)S(1)} %collective-permute-done.9.other, bf16[128,1024]{1,0:T(8,128)(2,1)S(1)} %collective-permute-done.18.ahead, ...), custom_call_target="tpu_custom_call" | custom-call | flops 1000000 | bytes 4000000 | tf_op jit(solution)/shard_map/pallas_call | solution.py:479
  80.0 1.1 collective-permute-start.20
  81.1 2.2 %collective-permute-start.21 = (bf16[256,1024]{1,0:T(8,128)(2,1)}, bf16[256,1024]{1,0:T(8,128)(2,1)}, u32[]{:S(2)}, u32[]{:S(2)}) collective-permute-start(bf16[256,1024]{1,0:T(8,128)(2,1)} %get-tuple-element.42), channel_id=1, source_target_pairs={{0,6},{2,0},{4,2},{6,4},{1,7},{3,1},{5,3},{7,5},{8,14},{10,8},{12,... | collective-permute-start | bytes 1572872 | tf_op jit(solution)/shard_map/ppermute | solution.py:42
  84.1 1.5 %collective-permute-start.15 = (bf16[2,8,64,128]{3,2,1,0:T(8,128)(2,1)}, bf16[2,8,64,128]{3,2,1,0:T(8,128)(2,1)S(1)}, u32[]{:S(2)}, u32[]{:S(2)}) collective-permute-start(bf16[2,8,64,128]{3,2,1,0:T(8,128)(2,1)} %slice.16), channel_id=1, source_target_pairs={{0,32},{32,64},{64,96},{96,0},{1,33},{33,65},{65,97},{97,1},{2,34}... | collective-permute-start | bytes 786440 | tf_op jit(solution)/shard_map/ppermute | solution.py:42
  86.3 0.8 copy-done.9
  87.1 2.9 %collective-permute-start.16 = (bf16[2,8,64,128]{3,2,1,0:T(8,128)(2,1)}, bf16[2,8,64,128]{3,2,1,0:T(8,128)(2,1)}, u32[]{:S(2)}, u32[]{:S(2)}) collective-permute-start(bf16[2,8,64,128]{3,2,1,0:T(8,128)(2,1)} %slice.17), channel_id=1, source_target_pairs={{0,96},{32,0},{64,32},{96,64},{1,97},{33,1},{65,33},{97,65},{2,98}... | collective-permute-start | bytes 786440 | tf_op jit(solution)/shard_map/ppermute | solution.py:42
  90.7 1.2 collective-permute-done.15.g1
  91.9 2.4 %collective-permute-done.16.g2 = bf16[2,8,64,128]{3,2,1,0:T(8,128)(2,1)} collective-permute-done((bf16[2,8,64,128]{3,2,1,0:T(8,128)(2,1)}, bf16[2,8,64,128]{3,2,1,0:T(8,128)(2,1)}, u32[]{:S(2)}, u32[]{:S(2)}) %collective-permute-start.16) | collective-permute-done | bytes 262176 | tf_op jit(solution)/shard_map/ppermute | solution.py:42
  94.2 1.4 %copy-done.2 = bf16[3,256,1024]{2,1,0:T(8,128)(2,1)S(1)} copy-done((bf16[3,256,1024]{2,1,0:T(8,128)(2,1)S(1)}, bf16[3,256,1024]{2,1,0:T(8,128)(2,1)}, u32[]{:S(2)}) %copy-start.2) | copy-done | bytes 1572888
  95.7 1.4 %copy-done.4 = bf16[3,256,1024]{2,1,0:T(8,128)(2,1)S(1)} copy-done((bf16[3,256,1024]{2,1,0:T(8,128)(2,1)S(1)}, bf16[3,256,1024]{2,1,0:T(8,128)(2,1)}, u32[]{:S(2)}) %copy-start.4) | copy-done | bytes 1572888
  97.1 1.0 copy-done.10
  98.1 1.0 copy-done.13
  99.1 2.8 %shard_map.131 = (f32[256,1024]{1,0:T(8,128)S(1)}, bf16[1024,1024]{1,0:T(8,128)(2,1)S(1)}) custom-call(s32[39]{0:T(128)S(1)} %stack.156.spots, bf16[256,1024]{1,0:T(8,128)(2,1)S(1)} %copy-done.13, bf16[3,256,1024]{2,1,0:T(8,128)(2,1)S(1)} %copy-done.2, bf16[3,256,1024]{2,1,0:T(8,128)(2,1)S(1)} %copy-done.4, bf16[4,8,64,128]{3,2,1,0:T(8,128)(2,1)S(1)} %shard_map.130.s0, ...), custom_call_target="tpu_custom_call" | custom-call | flops 1000000 | bytes 4000000 | tf_op jit(solution)/shard_map/pallas_call | solution.py:492
  101.9 2.9 %shard_map.134 = (bf16[272,512]{1,0:T(8,128)(2,1)S(1)}, f32[256,512]{1,0:T(8,128)S(1)}, f32[8,256]{1,0:T(8,128)S(1)}) custom-call(s32[39]{0:T(128)S(1)} %stack.156.spots, f32[256,1024]{1,0:T(8,128)S(1)} %get-tuple-element.36.base, bf16[256,1024]{1,0:T(8,128)(2,1)} %collective-permute-done.20.from_last, bf16[256,1024]{1,0:T(8,128)(2,1)} %collective-permute-done.21.from_next, ...), custom_call_target="tpu_custom_call" | custom-call | flops 600000000 | bytes 4000000 | tf_op jit(solution)/shard_map/pallas_call | solution.py:501
  105.0 1.5 %collective-permute-done.22.got = bf16[272,512]{1,0:T(8,128)(2,1)S(1)} collective-permute-done((bf16[272,512]{1,0:T(8,128)(2,1)S(1)}, bf16[272,512]{1,0:T(8,128)(2,1)S(1)}, u32[]{:S(2)}, u32[]{:S(2)}) %collective-permute-start.22) | collective-permute-done | bytes 278560 | tf_op jit(solution)/shard_map/ppermute | solution.py:42
  107.3 3.2 %collective-permute-start.24 = (bf16[272,128]{1,0:T(8,128)(2,1)S(1)}, bf16[272,128]{1,0:T(8,128)(2,1)S(1)}, u32[]{:S(2)}, u32[]{:S(2)}) collective-permute-start(bf16[272,128]{1,0:T(8,128)(2,1)S(1)} %get-tuple-element.50), channel_id=1, source_target_pairs={{0,6},{2,0},{4,2},{6,4},{1,7},{3,1},{5,3},{7,5},{8,14},{10,8},{12,... | collective-permute-start | bytes 208904 | tf_op jit(solution)/shard_map/ppermute | solution.py:42
  110.7 2.0 %collective-permute-done.23.g1 = bf16[272,128]{1,0:T(8,128)(2,1)S(1)} collective-permute-done((bf16[272,128]{1,0:T(8,128)(2,1)S(1)}, bf16[272,128]{1,0:T(8,128)(2,1)S(1)}, u32[]{:S(2)}, u32[]{:S(2)}) %collective-permute-start.23) | collective-permute-done | bytes 69664 | tf_op jit(solution)/shard_map/ppermute | solution.py:42
  113.5 2.8 %collective-permute-done.25.g2 = bf16[272,128]{1,0:T(8,128)(2,1)S(1)} collective-permute-done((bf16[272,128]{1,0:T(8,128)(2,1)S(1)}, bf16[272,128]{1,0:T(8,128)(2,1)S(1)}, u32[]{:S(2)}, u32[]{:S(2)}) %collective-permute-start.25) | collective-permute-done | bytes 69664 | tf_op jit(solution)/shard_map/ppermute | solution.py:42
  116.7 13.1 %all_to_all.10 = bf16[16,40,128]{2,1,0:T(8,128)(2,1)S(1)} all-to-all(bf16[16,40,128]{2,1,0:T(8,128)(2,1)S(1)} %bitcast.53), channel_id=1, replica_groups=mesh['x'=4,'z'=4,'y'=4,'core'=2] {'x','z'}, dimensions={0} | all-to-all | bytes 327680 | tf_op jit(solution)/shard_map/all_to_all | solution.py:523
  (77 shorter events, 9.9 us)
Async XLA Ops:
  0.0 3.3 %copy-start = (bf16[8192,128]{1,0:T(8,128)(2,1)S(1)}, bf16[8192,128]{1,0:T(8,128)(2,1)}, u32[]{:S(2)}) copy-start(bf16[8192,128]{1,0:T(8,128)(2,1)} %param.25) | copy-start | bytes 6291460
  0.0 20.8 %copy-start.16 = (s32[1,256]{1,0:T(1,128)S(1)}, s32[1,256]{1,0:T(1,128)}, u32[]{:S(2)}) copy-start(s32[1,256]{1,0:T(1,128)} %param.21) | copy-start | bytes 3076
  0.0 32.3 %copy-start.15 = (s32[1,16]{1,0:T(1,128)S(1)}, s32[1,16]{1,0:T(1,128)}, u32[]{:S(2)}) copy-start(s32[1,16]{1,0:T(1,128)} %live) | copy-start | bytes 196
  0.0 20.6 %copy-start.17 = (s32[16,1]{0,1:T(1,128)S(1)}, s32[16,1]{0,1:T(1,128)}, u32[]{:S(2)}) copy-start(s32[16,1]{0,1:T(1,128)} %param.23) | copy-start | bytes 196
  0.0 32.3 %copy-start.7 = (bf16[16,320,128]{2,1,0:T(8,128)(2,1)S(1)}, bf16[16,320,128]{2,1,0:T(8,128)(2,1)}, u32[]{:S(2)}) copy-start(bf16[16,320,128]{2,1,0:T(8,128)(2,1)} %ck.1) | copy-start | bytes 3932164
  0.0 17.9 %collective-permute-start = (bf16[32,8192]{1,0:T(8,128)(2,1)}, bf16[32,8192]{1,0:T(8,128)(2,1)}, u32[]{:S(2)}, u32[]{:S(2)}) collective-permute-start(bf16[32,8192]{1,0:T(8,128)(2,1)} %x0.1), channel_id=1, source_target_pairs={{0,2},{2,4},{4,6},{6,0},{1,3},{3,5},{5,7},{7,1},{8,10},{10,12},{12... | collective-permute-start | bytes 1572872 | tf_op jit(solution)/shard_map/ppermute | solution.py:42
  1.8 16.2 %collective-permute-start.1 = (bf16[32,8192]{1,0:T(8,128)(2,1)}, bf16[32,8192]{1,0:T(8,128)(2,1)}, u32[]{:S(2)}, u32[]{:S(2)}) collective-permute-start(bf16[32,8192]{1,0:T(8,128)(2,1)} %x0.1), channel_id=1, source_target_pairs={{0,6},{2,0},{4,2},{6,4},{1,7},{3,1},{5,3},{7,5},{8,14},{10,8},{12,... | collective-permute-start | bytes 1572872 | tf_op jit(solution)/shard_map/ppermute | solution.py:42
  4.0 13.9 %all-to-all-start = ((bf16[8,64,128]{2,1,0:T(8,128)(2,1)}), bf16[8,64,128]{2,1,0:T(8,128)(2,1)S(1)}, u32[]{:S(2)}, u32[]{:S(2)}) async-start(bf16[8,64,128]{2,1,0:T(8,128)(2,1)} %dynamic-slice_bitcast_fusion), calls=%async_computation | async-start | bytes 262144 | tf_op jit(solution)/shard_map/all_to_all | solution.py:395
  7.4 23.6 %collective-permute-start.2 = (bf16[32,8192]{1,0:T(8,128)(2,1)}, bf16[32,8192]{1,0:T(8,128)(2,1)}, u32[]{:S(2)}, u32[]{:S(2)}) collective-permute-start(bf16[32,8192]{1,0:T(8,128)(2,1)} %x0.1), channel_id=1, source_target_pairs={{0,1},{1,0},{2,3},{3,2},{4,5},{5,4},{6,7},{7,6},{8,9},{9,8},{10,11... | collective-permute-start | bytes 1572872 | tf_op jit(solution)/shard_map/ppermute | solution.py:42
  18.9 13.4 %collective-permute-start.3 = (bf16[32,8192]{1,0:T(8,128)(2,1)}, bf16[32,8192]{1,0:T(8,128)(2,1)S(1)}, u32[]{:S(2)}, u32[]{:S(2)}) collective-permute-start(bf16[32,8192]{1,0:T(8,128)(2,1)} %collective-permute-done.xl), channel_id=1, source_target_pairs={{0,1},{1,0},{2,3},{3,2},{4,5},{5,4},{6,7},{7,6},{8,9},{9,8},{10,11... | collective-permute-start | bytes 1572872 | tf_op jit(solution)/shard_map/ppermute | solution.py:42
  20.0 12.3 %collective-permute-start.4 = (bf16[32,8192]{1,0:T(8,128)(2,1)}, bf16[32,8192]{1,0:T(8,128)(2,1)S(1)}, u32[]{:S(2)}, u32[]{:S(2)}) collective-permute-start(bf16[32,8192]{1,0:T(8,128)(2,1)} %collective-permute-done.1.xr), channel_id=1, source_target_pairs={{0,1},{1,0},{2,3},{3,2},{4,5},{5,4},{6,7},{7,6},{8,9},{9,8},{10,11... | collective-permute-start | bytes 1572872 | tf_op jit(solution)/shard_map/ppermute | solution.py:42
  20.9 9.5 %collective-permute-start.5 = (bf16[16,8192]{1,0:T(8,128)(2,1)S(1)}, bf16[16,8192]{1,0:T(8,128)(2,1)S(1)}, u32[]{:S(2)}, u32[]{:S(2)}) collective-permute-start(bf16[16,8192]{1,0:T(8,128)(2,1)S(1)} %slice.12), channel_id=1, source_target_pairs={{0,2},{2,4},{4,6},{6,0},{1,3},{3,5},{5,7},{7,1},{8,10},{10,12},{12... | collective-permute-start | bytes 786440 | tf_op jit(solution)/shard_map/ppermute | solution.py:42
  22.1 8.3 %collective-permute-start.6 = (bf16[16,8192]{1,0:T(8,128)(2,1)S(1)}, bf16[16,8192]{1,0:T(8,128)(2,1)S(1)}, u32[]{:S(2)}, u32[]{:S(2)}) collective-permute-start(bf16[16,8192]{1,0:T(8,128)(2,1)S(1)} %slice.13), channel_id=1, source_target_pairs={{0,6},{2,0},{4,2},{6,4},{1,7},{3,1},{5,3},{7,5},{8,14},{10,8},{12,... | collective-permute-start | bytes 786440 | tf_op jit(solution)/shard_map/ppermute | solution.py:42
  24.3 28.3 %slice-start = ((s8[8388608]{0:T(1024)(128)(4,1)}), s8[4194304]{0:T(1024)(128)(4,1)S(1)}, s32[]{:S(2)}) async-start(s8[8388608]{0:T(1024)(128)(4,1)} %bitcast.51), calls=%async_computation.2 | async-start | bytes 8388608
  30.4 1.5 %collective-permute-start.7 = (bf16[16,8192]{1,0:T(8,128)(2,1)S(1)}, bf16[16,8192]{1,0:T(8,128)(2,1)S(1)}, u32[]{:S(2)}, u32[]{:S(2)}) collective-permute-start(bf16[16,8192]{1,0:T(8,128)(2,1)S(1)} %collective-permute-done.5.f1), channel_id=1, source_target_pairs={{0,1},{1,0},{2,3},{3,2},{4,5},{5,4},{6,7},{7,6},{8,9},{9,8},{10,11... | collective-permute-start | bytes 786440 | tf_op jit(solution)/shard_map/ppermute | solution.py:42
  30.4 1.9 %collective-permute-start.8 = (bf16[16,8192]{1,0:T(8,128)(2,1)S(1)}, bf16[16,8192]{1,0:T(8,128)(2,1)S(1)}, u32[]{:S(2)}, u32[]{:S(2)}) collective-permute-start(bf16[16,8192]{1,0:T(8,128)(2,1)S(1)} %collective-permute-done.6.f2), channel_id=1, source_target_pairs={{0,1},{1,0},{2,3},{3,2},{4,5},{5,4},{6,7},{7,6},{8,9},{9,8},{10,11... | collective-permute-start | bytes 786440 | tf_op jit(solution)/shard_map/ppermute | solution.py:42
  31.0 21.6 %slice-start.1 = ((s8[8388608]{0:T(1024)(128)(4,1)}), s8[4194304]{0:T(1024)(128)(4,1)S(1)}, s32[]{:S(2)}) async-start(s8[8388608]{0:T(1024)(128)(4,1)} %bitcast.51), calls=%async_computation.3 | async-start | bytes 8388608
  32.3 1.6 %copy-start.5 = (bf16[8192,128]{1,0:T(8,128)(2,1)S(1)}, bf16[8192,128]{1,0:T(8,128)(2,1)}, u32[]{:S(2)}) copy-start(bf16[8192,128]{1,0:T(8,128)(2,1)} %wk.1) | copy-start | bytes 6291460
  33.9 1.6 %copy-start.6 = (bf16[8192,128]{1,0:T(8,128)(2,1)S(1)}, bf16[8192,128]{1,0:T(8,128)(2,1)}, u32[]{:S(2)}) copy-start(bf16[8192,128]{1,0:T(8,128)(2,1)} %wv.1) | copy-start | bytes 6291460
  35.5 1.3 %copy-start.8 = (bf16[16,320,128]{2,1,0:T(8,128)(2,1)S(1)}, bf16[16,320,128]{2,1,0:T(8,128)(2,1)}, u32[]{:S(2)}) copy-start(bf16[16,320,128]{2,1,0:T(8,128)(2,1)} %cv.1) | copy-start | bytes 3932164
  36.8 1.0 copy-start.11
  37.9 0.8 copy-start.14
  52.6 2.6 %copy-start.12 = (bf16[256,1024]{1,0:T(8,128)(2,1)}, bf16[256,1024]{1,0:T(8,128)(2,1)S(1)}, u32[]{:S(2)}) copy-start(bf16[256,1024]{1,0:T(8,128)(2,1)S(1)} %get-tuple-element.33.mine) | copy-start | bytes 1572868
  55.2 23.3 %collective-permute-start.9 = (bf16[3,256,1024]{2,1,0:T(8,128)(2,1)S(1)}, bf16[3,256,1024]{2,1,0:T(8,128)(2,1)S(1)}, u32[]{:S(2)}, u32[]{:S(2)}) collective-permute-start(bf16[3,256,1024]{2,1,0:T(8,128)(2,1)S(1)} %shard_map.129), channel_id=1, source_target_pairs={{0,1},{1,0},{2,3},{3,2},{4,5},{5,4},{6,7},{7,6},{8,9},{9,8},{10,11... | collective-permute-start | bytes 4718600 | tf_op jit(solution)/shard_map/ppermute | solution.py:42
  55.4 14.5 %collective-permute-start.17 = (bf16[256,1024]{1,0:T(8,128)(2,1)S(1)}, bf16[256,1024]{1,0:T(8,128)(2,1)S(1)}, u32[]{:S(2)}, u32[]{:S(2)}) collective-permute-start(bf16[256,1024]{1,0:T(8,128)(2,1)S(1)} %get-tuple-element.38), channel_id=1, source_target_pairs={{0,1},{1,0},{2,3},{3,2},{4,5},{5,4},{6,7},{7,6},{8,9},{9,8},{10,11... | collective-permute-start | bytes 1572872 | tf_op jit(solution)/shard_map/ppermute | solution.py:42
  55.8 7.8 %collective-permute-start.10 = (bf16[8,64,128]{2,1,0:T(8,128)(2,1)S(1)}, bf16[8,64,128]{2,1,0:T(8,128)(2,1)S(1)}, u32[]{:S(2)}, u32[]{:S(2)}) collective-permute-start(bf16[8,64,128]{2,1,0:T(8,128)(2,1)S(1)} %all-to-all-done.s0), channel_id=1, source_target_pairs={{0,8},{8,16},{16,24},{24,0},{1,9},{9,17},{17,25},{25,1},{2,10},{10... | collective-permute-start | bytes 393224 | tf_op jit(solution)/shard_map/ppermute | solution.py:42
  57.7 8.0 %collective-permute-start.11 = (bf16[8,64,128]{2,1,0:T(8,128)(2,1)S(1)}, bf16[8,64,128]{2,1,0:T(8,128)(2,1)S(1)}, u32[]{:S(2)}, u32[]{:S(2)}) collective-permute-start(bf16[8,64,128]{2,1,0:T(8,128)(2,1)S(1)} %all-to-all-done.s0), channel_id=1, source_target_pairs={{0,24},{8,0},{16,8},{24,16},{1,25},{9,1},{17,9},{25,17},{2,26},{10... | collective-permute-start | bytes 393224 | tf_op jit(solution)/shard_map/ppermute | solution.py:42
  59.8 7.8 %collective-permute-start.12 = (bf16[8,64,128]{2,1,0:T(8,128)(2,1)S(1)}, bf16[8,64,128]{2,1,0:T(8,128)(2,1)S(1)}, u32[]{:S(2)}, u32[]{:S(2)}) collective-permute-start(bf16[8,64,128]{2,1,0:T(8,128)(2,1)S(1)} %all-to-all-done.s0), channel_id=1, source_target_pairs={{0,16},{8,24},{16,0},{24,8},{1,17},{9,25},{17,1},{25,9},{2,18},{10... | collective-permute-start | bytes 393224 | tf_op jit(solution)/shard_map/ppermute | solution.py:42
  68.3 15.1 %collective-permute-start.13 = (bf16[4,8,64,128]{3,2,1,0:T(8,128)(2,1)S(1)}, bf16[4,8,64,128]{3,2,1,0:T(8,128)(2,1)S(1)}, u32[]{:S(2)}, u32[]{:S(2)}) collective-permute-start(bf16[4,8,64,128]{3,2,1,0:T(8,128)(2,1)S(1)} %shard_map.130.s0), channel_id=1, source_target_pairs={{0,32},{32,64},{64,96},{96,0},{1,33},{33,65},{65,97},{97,1},{2,34}... | collective-permute-start | bytes 1572872 | tf_op jit(solution)/shard_map/ppermute | solution.py:42
  70.0 8.5 %collective-permute-start.18 = (bf16[128,1024]{1,0:T(8,128)(2,1)S(1)}, bf16[128,1024]{1,0:T(8,128)(2,1)S(1)}, u32[]{:S(2)}, u32[]{:S(2)}) collective-permute-start(bf16[128,1024]{1,0:T(8,128)(2,1)S(1)} %get-tuple-element.39), channel_id=1, source_target_pairs={{0,2},{2,4},{4,6},{6,0},{1,3},{3,5},{5,7},{7,1},{8,10},{10,12},{12... | collective-permute-start | bytes 786440 | tf_op jit(solution)/shard_map/ppermute | solution.py:42
  70.1 8.4 %collective-permute-start.19 = (bf16[128,1024]{1,0:T(8,128)(2,1)S(1)}, bf16[128,1024]{1,0:T(8,128)(2,1)S(1)}, u32[]{:S(2)}, u32[]{:S(2)}) collective-permute-start(bf16[128,1024]{1,0:T(8,128)(2,1)S(1)} %get-tuple-element.40), channel_id=1, source_target_pairs={{0,6},{2,0},{4,2},{6,4},{1,7},{3,1},{5,3},{7,5},{8,14},{10,8},{12,... | collective-permute-start | bytes 786440 | tf_op jit(solution)/shard_map/ppermute | solution.py:42
  73.3 12.3 %collective-permute-start.14 = (bf16[4,8,64,128]{3,2,1,0:T(8,128)(2,1)S(1)}, bf16[4,8,64,128]{3,2,1,0:T(8,128)(2,1)S(1)}, u32[]{:S(2)}, u32[]{:S(2)}) collective-permute-start(bf16[4,8,64,128]{3,2,1,0:T(8,128)(2,1)S(1)} %shard_map.130.s0), channel_id=1, source_target_pairs={{0,96},{32,0},{64,32},{96,64},{1,97},{33,1},{65,33},{97,65},{2,98}... | collective-permute-start | bytes 1572872 | tf_op jit(solution)/shard_map/ppermute | solution.py:42
  77.6 6.5 %copy-start.1 = (bf16[3,256,1024]{2,1,0:T(8,128)(2,1)}, bf16[3,256,1024]{2,1,0:T(8,128)(2,1)S(1)}, u32[]{:S(2)}) copy-start(bf16[3,256,1024]{2,1,0:T(8,128)(2,1)S(1)} %shard_map.128.keep) | copy-start | bytes 4718596
  78.5 5.6 %copy-start.3 = (bf16[3,256,1024]{2,1,0:T(8,128)(2,1)}, bf16[3,256,1024]{2,1,0:T(8,128)(2,1)S(1)}, u32[]{:S(2)}) copy-start(bf16[3,256,1024]{2,1,0:T(8,128)(2,1)S(1)} %collective-permute-done.9.other) | copy-start | bytes 4718596
  80.0 21.9 %collective-permute-start.20 = (bf16[256,1024]{1,0:T(8,128)(2,1)}, bf16[256,1024]{1,0:T(8,128)(2,1)}, u32[]{:S(2)}, u32[]{:S(2)}) collective-permute-start(bf16[256,1024]{1,0:T(8,128)(2,1)} %get-tuple-element.41), channel_id=1, source_target_pairs={{0,2},{2,4},{4,6},{6,0},{1,3},{3,5},{5,7},{7,1},{8,10},{10,12},{12... | collective-permute-start | bytes 1572872 | tf_op jit(solution)/shard_map/ppermute | solution.py:42
  81.1 20.8 %collective-permute-start.21 = (bf16[256,1024]{1,0:T(8,128)(2,1)}, bf16[256,1024]{1,0:T(8,128)(2,1)}, u32[]{:S(2)}, u32[]{:S(2)}) collective-permute-start(bf16[256,1024]{1,0:T(8,128)(2,1)} %get-tuple-element.42), channel_id=1, source_target_pairs={{0,6},{2,0},{4,2},{6,4},{1,7},{3,1},{5,3},{7,5},{8,14},{10,8},{12,... | collective-permute-start | bytes 1572872 | tf_op jit(solution)/shard_map/ppermute | solution.py:42
  84.1 7.8 %collective-permute-start.15 = (bf16[2,8,64,128]{3,2,1,0:T(8,128)(2,1)}, bf16[2,8,64,128]{3,2,1,0:T(8,128)(2,1)S(1)}, u32[]{:S(2)}, u32[]{:S(2)}) collective-permute-start(bf16[2,8,64,128]{3,2,1,0:T(8,128)(2,1)} %slice.16), channel_id=1, source_target_pairs={{0,32},{32,64},{64,96},{96,0},{1,33},{33,65},{65,97},{97,1},{2,34}... | collective-permute-start | bytes 786440 | tf_op jit(solution)/shard_map/ppermute | solution.py:42
  86.3 0.8 copy-start.9
  87.1 7.1 %collective-permute-start.16 = (bf16[2,8,64,128]{3,2,1,0:T(8,128)(2,1)}, bf16[2,8,64,128]{3,2,1,0:T(8,128)(2,1)}, u32[]{:S(2)}, u32[]{:S(2)}) collective-permute-start(bf16[2,8,64,128]{3,2,1,0:T(8,128)(2,1)} %slice.17), channel_id=1, source_target_pairs={{0,96},{32,0},{64,32},{96,64},{1,97},{33,1},{65,33},{97,65},{2,98}... | collective-permute-start | bytes 786440 | tf_op jit(solution)/shard_map/ppermute | solution.py:42
  94.2 1.4 %copy-start.2 = (bf16[3,256,1024]{2,1,0:T(8,128)(2,1)S(1)}, bf16[3,256,1024]{2,1,0:T(8,128)(2,1)}, u32[]{:S(2)}) copy-start(bf16[3,256,1024]{2,1,0:T(8,128)(2,1)} %copy-done.1) | copy-start | bytes 4718596
  95.7 1.4 %copy-start.4 = (bf16[3,256,1024]{2,1,0:T(8,128)(2,1)S(1)}, bf16[3,256,1024]{2,1,0:T(8,128)(2,1)}, u32[]{:S(2)}) copy-start(bf16[3,256,1024]{2,1,0:T(8,128)(2,1)} %copy-done.3) | copy-start | bytes 4718596
  97.1 1.0 copy-start.10
  98.1 1.0 copy-start.13
  104.9 1.6 %collective-permute-start.22 = (bf16[272,512]{1,0:T(8,128)(2,1)S(1)}, bf16[272,512]{1,0:T(8,128)(2,1)S(1)}, u32[]{:S(2)}, u32[]{:S(2)}) collective-permute-start(bf16[272,512]{1,0:T(8,128)(2,1)S(1)} %get-tuple-element.46), channel_id=1, source_target_pairs={{0,1},{1,0},{2,3},{3,2},{4,5},{5,4},{6,7},{7,6},{8,9},{9,8},{10,11... | collective-permute-start | bytes 835592 | tf_op jit(solution)/shard_map/ppermute | solution.py:42
  107.2 5.6 %collective-permute-start.23 = (bf16[272,128]{1,0:T(8,128)(2,1)S(1)}, bf16[272,128]{1,0:T(8,128)(2,1)S(1)}, u32[]{:S(2)}, u32[]{:S(2)}) collective-permute-start(bf16[272,128]{1,0:T(8,128)(2,1)S(1)} %get-tuple-element.49), channel_id=1, source_target_pairs={{0,2},{2,4},{4,6},{6,0},{1,3},{3,5},{5,7},{7,1},{8,10},{10,12},{12... | collective-permute-start | bytes 208904 | tf_op jit(solution)/shard_map/ppermute | solution.py:42
  107.3 6.2 %collective-permute-start.24 = (bf16[272,128]{1,0:T(8,128)(2,1)S(1)}, bf16[272,128]{1,0:T(8,128)(2,1)S(1)}, u32[]{:S(2)}, u32[]{:S(2)}) collective-permute-start(bf16[272,128]{1,0:T(8,128)(2,1)S(1)} %get-tuple-element.50), channel_id=1, source_target_pairs={{0,6},{2,0},{4,2},{6,4},{1,7},{3,1},{5,3},{7,5},{8,14},{10,8},{12,... | collective-permute-start | bytes 208904 | tf_op jit(solution)/shard_map/ppermute | solution.py:42
  110.5 5.8 %collective-permute-start.25 = (bf16[272,128]{1,0:T(8,128)(2,1)S(1)}, bf16[272,128]{1,0:T(8,128)(2,1)S(1)}, u32[]{:S(2)}, u32[]{:S(2)}) collective-permute-start(bf16[272,128]{1,0:T(8,128)(2,1)S(1)} %get-tuple-element.51), channel_id=1, source_target_pairs={{0,4},{2,6},{4,0},{6,2},{1,5},{3,7},{5,1},{7,3},{8,12},{10,14},{12... | collective-permute-start | bytes 208904 | tf_op jit(solution)/shard_map/ppermute | solution.py:42
